TPU v7x, 512 devices: a whole 4x4x16 slice. The times are simulated.
512 devices in a mesh: tm: 32 (over z, core), bat: 16 (over y, x).
Axes of the slice: x: 4, y: 4, z: 16, core: 2. Of those that a mesh axis runs over, the one named last changes fastest.
Arguments:
- power0: float32 [512, 6144], P('tm', 'bat'), may hold values from -0.5 to 0.5
- charge0: float32 [512, 6144], P('tm', 'bat'), may hold values from 0 to 1
- dyn_dual0: float32 [512, 6144], P('tm', 'bat'), may hold values from -3 to 3
- feeder_dual0: float32 [512, 3072], P(('tm', 'bat')), may hold values from 0 to 0.5
- price: float32 [512, 6144], P('tm', 'bat'), may hold values from -12 to 12
- inflow: float32 [512, 6144], P('tm', 'bat'), may hold values from -1.5 to 1.5
- power_limit: float32 [6144], P('bat'), may hold values from 0.5 to 6
- capacity: float32 [6144], P('bat'), may hold values from 0.5 to 8
- feeder_limit: float32 [3072], replicated, may hold values from 0 to 1
- block_values: float32 [72, 128, 128], replicated, may hold values from -0.3125 to 0.3125
- block_cols: int32 [72], replicated, may hold values from 0 to 47, as said below
- block_offsets: int32 [25], replicated, may hold values from 0 to 72, as said below
Outputs:
- power: float32 [512, 6144], P('tm', 'bat')
- charge: float32 [512, 6144], P('tm', 'bat')
- dyn_dual: float32 [512, 6144], P('tm', 'bat')
- feeder_dual: float32 [512, 3072], P(('tm', 'bat'))
Inputs may be any that keep to these rules, and one draw needn't show every extreme that they name: `block_cols`: every battery block 0 to 47 appears at least once. block_offsets[0] = 0, strictly rising, block_offsets[24] = 72.
All inputs are finite; a program needn't handle non-finite values.
Results may differ from a plain program's by a relative error of at most 0.0001.
Values sent between devices are 32-bit elements; how exact they have to be, the bound alone decides.
No kernel may reach another device: no remote copies, remote signals or barrier semaphores. Data moves between devices by JAX's collectives and lax.ppermute only.
A program may use at most 64 MiB of HBM per device.

v0:
```python
import jax
import jax.numpy as jnp
from jax import lax
from jax.sharding import PartitionSpec as P

ITERS = 4


HIGH = lax.Precision.HIGHEST
ETA_STEP = 0.4
EPS_NORM = 1e-06


def shifted(block, axis, distance):
    devices = range(lax.axis_size(axis))
    route = [(i - distance, i) for i in devices if i - distance in devices]
    return lax.ppermute(block, axis, route)


def row_table(block_offsets, count):
    index_all = jnp.arange(count, dtype=jnp.int32)
    row_of = jnp.sum((index_all[:, None] >= block_offsets[None, 1:-1]).astype(jnp.int32), axis=1)
    feed_count = block_offsets.shape[0] - 1
    return (row_of[:, None] == jnp.arange(feed_count, dtype=jnp.int32)[None, :]).astype(jnp.float32)


def feeder_apply(field, block_values, rows_tab, cols_tab):
    count_rows = field.shape[0]
    blk = block_values.shape[1]
    blocks = field.reshape(count_rows, -1, blk)
    picked = jnp.einsum("rnk,jn->rjk", blocks, cols_tab, precision=HIGH)
    partial_rows = jnp.einsum("rjk,jmk->rjm", picked, block_values, precision=HIGH)
    summed = jnp.einsum("rjm,jf->rfm", partial_rows, rows_tab, precision=HIGH)
    return summed.reshape(count_rows, -1)


def feeder_adjoint(duals, block_values, rows_tab, cols_tab):
    count_rows = duals.shape[0]
    blk = block_values.shape[1]
    blocks = duals.reshape(count_rows, -1, blk)
    chosen = jnp.einsum("rfm,jf->rjm", blocks, rows_tab, precision=HIGH)
    pushed = jnp.einsum("rjm,jmk->rjk", chosen, block_values, precision=HIGH)
    spread = jnp.einsum("rjk,jn->rnk", pushed, cols_tab, precision=HIGH)
    return spread.reshape(count_rows, -1)


def shards(
    power0,
    charge0,
    dyn_dual0,
    feeder_dual0,
    price,
    inflow,
    power_limit,
    capacity,
    feeder_limit,
    block_values,
    block_cols,
    block_offsets,
):
    blk = block_values.shape[1]
    rows_tab = row_table(block_offsets, block_values.shape[0])
    local_batteries = power0.shape[1]
    local_blocks = local_batteries // blk
    first_block = lax.axis_index("bat") * local_blocks
    inside = (block_cols >= first_block) & (block_cols < first_block + local_blocks)
    local_cols = jnp.clip(block_cols - first_block, 0, local_blocks - 1)
    local_tab = (
        (local_cols[:, None] == jnp.arange(local_blocks, dtype=jnp.int32)[None, :])
        & inside[:, None]
    ).astype(jnp.float32)

    def couple_backward(duals):
        return feeder_adjoint(
            lax.all_gather(duals, "bat", axis=0, tiled=True), block_values, rows_tab, local_tab
        )

    power, charge, dyn_dual, feeder_dual = (power0, charge0, dyn_dual0, feeder_dual0)
    weight = jnp.asarray(1.0, dtype=jnp.float32)
    pushed = couple_backward(feeder_dual)
    limit_row = power_limit[None, :]
    for iteration in range(ITERS):
        step_primal = ETA_STEP / weight
        step_dual = ETA_STEP * weight
        following = shifted(dyn_dual[:1], "tm", -1)
        dual_next = jnp.concatenate([dyn_dual[1:], following], axis=0)
        power_new = jnp.clip(
            power - step_primal * (price - dyn_dual + pushed), -limit_row, limit_row
        )
        charge_new = jnp.clip(charge - step_primal * (dyn_dual - dual_next), 0.0, capacity[None, :])
        power_bar = 2.0 * power_new - power
        charge_bar = 2.0 * charge_new - charge
        last_iteration = iteration + 1 == ITERS
        if not last_iteration:
            move_power = power_new - power
            move_charge = charge_new - charge
            primal_local = jnp.sum(move_power * move_power + move_charge * move_charge)
            primal_sq = lax.psum(primal_local, ("tm", "bat"))
        coupled = lax.psum_scatter(
            feeder_apply(power_bar, block_values, rows_tab, local_tab),
            "bat",
            scatter_dimension=0,
            tiled=True,
        )
        preceding = shifted(charge_bar[-1:], "tm", 1)
        charge_prev = jnp.concatenate([preceding, charge_bar[:-1]], axis=0)
        dyn_new = dyn_dual + step_dual * (charge_bar - charge_prev - power_bar - inflow)
        feeder_new = jnp.maximum(0.0, feeder_dual + step_dual * (coupled - feeder_limit[None, :]))
        if not last_iteration:
            move_dyn = dyn_new - dyn_dual
            move_feed = feeder_new - feeder_dual
            dual_local = jnp.sum(move_dyn * move_dyn) + jnp.sum(move_feed * move_feed)
            dual_sq = lax.psum(dual_local, ("tm", "bat"))
            weight = jnp.sqrt(weight * jnp.sqrt((dual_sq + EPS_NORM) / (primal_sq + EPS_NORM)))
            pushed = couple_backward(feeder_new)
        power, charge, dyn_dual, feeder_dual = (power_new, charge_new, dyn_new, feeder_new)
    return (power, charge, dyn_dual, feeder_dual)


def solution(mesh):
    return jax.shard_map(
        shards,
        mesh=mesh,
        in_specs=(
            P("tm", "bat"),
            P("tm", "bat"),
            P("tm", "bat"),
            P(("tm", "bat"), None),
            P("tm", "bat"),
            P("tm", "bat"),
            P("bat"),
            P("bat"),
            P(),
            P(),
            P(),
            P(),
        ),
        out_specs=(P("tm", "bat"), P("tm", "bat"), P("tm", "bat"), P(("tm", "bat"), None)),
        check_vma=False,
    )
```

profile of v0, /device:TPU:1, one launch (start us, length us, event | category | flops | bytes accessed | tf_op | source)
XLA Modules:
  0.0 976.6 jit_solution(11067665464385182962)
XLA Ops:
  8.0 8.8 collective-permute-start
  18.9 16.3 %all-gather = f32[16,1,3072]{2,1,0:T(1,128)S(1)} all-gather(f32[1,1,3072]{2,1,0:T(1,128)} %bitcast.181), channel_id=1, replica_groups=mesh['tm'=32,'bat'=16] {'bat'}, dimensions={0}, use_global_device_ids=true | all-gather | bytes 208896 | tf_op jit(solution)/shard_map/all_gather | solution.py:75
  35.7 5.8 convolution_bitcast_fusion.15
  42.7 5.9 collective-permute-start.1
  50.5 9.2 convolution_bitcast_fusion.14
  60.9 1.3 dynamic-slice
  62.3 2.0 collective-permute-start.2
  64.2 113.2 %all-reduce.12.cloned.1.call-done = f32[16,3072]{1,0:T(8,128)} async-done(((f32[16,3072]{1,0:T(8,128)}), f32[16,3072]{1,0:T(8,128)}) %all-reduce.12.cloned.1.call-update) | async-done | bytes 196624
  177.4 2.2 multiply_reduce_fusion.5
  179.6 17.3 %all-gather.1 = f32[16,1,3072]{2,1,0:T(1,128)S(1)} all-gather(f32[1,1,3072]{2,1,0:T(1,128)S(1)} %bitcast.179), channel_id=1, replica_groups=mesh['tm'=32,'bat'=16] {'bat'}, dimensions={0}, use_global_device_ids=true | all-gather | bytes 208896 | tf_op jit(solution)/shard_map/all_gather | solution.py:75
  197.3 5.8 convolution_bitcast_fusion.13
  204.9 109.0 %all-reduce.6 = (f32[]{:T(128)}, f32[]{:T(128)}) all-reduce(f32[]{:T(128)S(6)} %add.99, f32[]{:T(128)} %get-tuple-element.31), channel_id=1, replica_groups=mesh['tm'=32,'bat'=16] {'tm','bat'}, use_global_device_ids=true, to_apply=%region_4.5 | all-reduce | flops 2 | bytes 16 | tf_op jit(solution)/shard_map/psum | solution.py:113
  316.0 2.5 collective-permute-start.3
  320.2 9.2 convolution_bitcast_fusion.12
  330.6 2.1 collective-permute-start.4
  332.7 108.3 %all-reduce.14.cloned.1.call-done = f32[16,3072]{1,0:T(8,128)} async-done(((f32[16,3072]{1,0:T(8,128)}), f32[16,3072]{1,0:T(8,128)}) %all-reduce.14.cloned.1.call-update) | async-done | bytes 196624
  441.0 2.2 multiply_reduce_fusion.4
  443.2 17.3 %all-gather.2 = f32[16,1,3072]{2,1,0:T(1,128)S(1)} all-gather(f32[1,1,3072]{2,1,0:T(1,128)S(1)} %bitcast.178), channel_id=1, replica_groups=mesh['tm'=32,'bat'=16] {'bat'}, dimensions={0}, use_global_device_ids=true | all-gather | bytes 208896 | tf_op jit(solution)/shard_map/all_gather | solution.py:75
  460.9 5.8 convolution_bitcast_fusion.11
  468.5 109.0 %all-reduce.5 = (f32[]{:T(128)}, f32[]{:T(128)}) all-reduce(f32[]{:T(128)S(6)} %add.106, f32[]{:T(128)} %get-tuple-element.23), channel_id=1, replica_groups=mesh['tm'=32,'bat'=16] {'tm','bat'}, use_global_device_ids=true, to_apply=%region_10.11 | all-reduce | flops 2 | bytes 16 | tf_op jit(solution)/shard_map/psum | solution.py:113
  579.6 2.3 collective-permute-start.5
  583.7 9.2 convolution_bitcast_fusion.10
  594.2 2.1 collective-permute-start.6
  596.3 108.3 %all-reduce.16.cloned.1.call-done = f32[16,3072]{1,0:T(8,128)} async-done(((f32[16,3072]{1,0:T(8,128)}), f32[16,3072]{1,0:T(8,128)}) %all-reduce.16.cloned.1.call-update) | async-done | bytes 196624
  704.6 2.2 multiply_reduce_fusion.3
  706.8 17.5 %all-gather.3 = f32[16,1,3072]{2,1,0:T(1,128)S(1)} all-gather(f32[1,1,3072]{2,1,0:T(1,128)S(1)} %bitcast.180), channel_id=1, replica_groups=mesh['tm'=32,'bat'=16] {'bat'}, dimensions={0}, use_global_device_ids=true | all-gather | bytes 208896 | tf_op jit(solution)/shard_map/all_gather | solution.py:75
  724.7 5.8 convolution_bitcast_fusion.9
  731.8 109.0 %all-reduce.4 = (f32[]{:T(128)}, f32[]{:T(128)}) all-reduce(f32[]{:T(128)S(6)} %add.113, f32[]{:T(128)} %get-tuple-element.15), channel_id=1, replica_groups=mesh['tm'=32,'bat'=16] {'tm','bat'}, use_global_device_ids=true, to_apply=%region_16.17 | all-reduce | flops 2 | bytes 16 | tf_op jit(solution)/shard_map/psum | solution.py:113
  842.9 2.3 collective-permute-start.7
  847.1 9.2 convolution_bitcast_fusion.8
  857.5 110.5 %all-reduce.18.cloned.1.call-done = f32[16,3072]{1,0:T(8,128)} async-done(((f32[16,3072]{1,0:T(8,128)}), f32[16,3072]{1,0:T(8,128)}) %all-reduce.18.cloned.1.call-update) | async-done | bytes 196624
  968.0 2.1 fusion.92
  (87 shorter events, 20.6 us)
Async XLA Ops:
  7.2 34.8 %copy-start.2 = (f32[16,384]{1,0:T(8,128)S(1)}, f32[16,384]{1,0:T(8,128)}, u32[]{:S(2)}) copy-start(f32[16,384]{1,0:T(8,128)} %param.14) | copy-start | bytes 73732
  7.2 34.8 %copy-start.6 = (f32[384]{0:T(512)S(1)}, f32[384]{0:T(512)}, u32[]{:S(2)}) copy-start(f32[384]{0:T(512)} %param.18) | copy-start | bytes 4612
  7.2 34.8 %copy-start.4 = (f32[16,384]{1,0:T(8,128)S(1)}, f32[16,384]{1,0:T(8,128)}, u32[]{:S(2)}) copy-start(f32[16,384]{1,0:T(8,128)} %param.12) | copy-start | bytes 73732
  7.2 34.8 %copy-start.5 = (f32[16,384]{1,0:T(8,128)S(1)}, f32[16,384]{1,0:T(8,128)}, u32[]{:S(2)}) copy-start(f32[16,384]{1,0:T(8,128)} %param.13) | copy-start | bytes 73732
  7.2 34.8 %copy-start.1 = (f32[16,384]{1,0:T(8,128)S(1)}, f32[16,384]{1,0:T(8,128)}, u32[]{:S(2)}) copy-start(f32[16,384]{1,0:T(8,128)} %param.16) | copy-start | bytes 73732
  7.2 34.8 %copy-start.8 = (f32[384]{0:T(512)S(1)}, f32[384]{0:T(512)}, u32[]{:S(2)}) copy-start(f32[384]{0:T(512)} %param.19) | copy-start | bytes 4612
  7.2 42.2 %copy-start = (f32[16,384]{1,0:T(8,128)S(1)}, f32[16,384]{1,0:T(8,128)}, u32[]{:S(2)}) copy-start(f32[16,384]{1,0:T(8,128)} %param.17) | copy-start | bytes 73732
  7.2 170.2 %all-reduce.12.cloned.1.call-start = ((), (), s32[]{:S(2)}) async-start(), calls=%async_computation | async-start | bytes 393216
  8.0 34.0 %collective-permute-start = (f32[1,384]{1,0:T(1,128)S(1)}, f32[1,384]{1,0:T(1,128)S(1)}, u32[]{:S(2)}, u32[]{:S(2)}) collective-permute-start(f32[1,384]{1,0:T(1,128)S(1)} %slice.53), channel_id=1, source_target_pairs={{16,0},{32,16},{48,32},{64,48},{80,64},{96,80},{112,96},{128,112},... | collective-permute-start | bytes 4616 | tf_op jit(solution)/shard_map/ppermute | solution.py:17
  41.5 135.9 %copy-start.3 = (f32[3072]{0:T(1024)S(1)}, f32[3072]{0:T(1024)}, u32[]{:S(2)}) copy-start(f32[3072]{0:T(1024)} %param.20) | copy-start | bytes 36868
  41.5 135.9 %copy-start.7 = (f32[1,3072]{1,0:T(1,128)S(1)}, f32[1,3072]{1,0:T(1,128)}, u32[]{:S(2)}) copy-start(f32[1,3072]{1,0:T(1,128)} %param.15) | copy-start | bytes 36868
  42.7 6.7 collective-permute-start.1
  60.9 380.2 %all-reduce.14.cloned.1.call-start = ((), (), s32[]{:S(2)}) async-start(), calls=%async_computation.1 | async-start | bytes 393216
  62.3 253.1 %collective-permute-start.2 = (f32[1,384]{1,0:T(1,128)S(1)}, f32[1,384]{1,0:T(1,128)S(1)}, u32[]{:S(2)}, u32[]{:S(2)}) collective-permute-start(f32[1,384]{1,0:T(1,128)S(1)} %slice.71), channel_id=1, source_target_pairs={{16,0},{32,16},{48,32},{64,48},{80,64},{96,80},{112,96},{128,112},... | collective-permute-start | bytes 4616 | tf_op jit(solution)/shard_map/ppermute | solution.py:17
  316.0 3.1 collective-permute-start.3
  330.6 374.1 %all-reduce.16.cloned.1.call-start = ((), (), s32[]{:S(2)}) async-start(), calls=%async_computation.2 | async-start | bytes 393216
  330.6 248.3 %collective-permute-start.4 = (f32[1,384]{1,0:T(1,128)S(1)}, f32[1,384]{1,0:T(1,128)S(1)}, u32[]{:S(2)}, u32[]{:S(2)}) collective-permute-start(f32[1,384]{1,0:T(1,128)S(1)} %slice.75), channel_id=1, source_target_pairs={{16,0},{32,16},{48,32},{64,48},{80,64},{96,80},{112,96},{128,112},... | collective-permute-start | bytes 4616 | tf_op jit(solution)/shard_map/ppermute | solution.py:17
  579.6 3.1 collective-permute-start.5
  594.1 373.8 %all-reduce.18.cloned.1.call-start = ((), (), s32[]{:S(2)}) async-start(), calls=%async_computation.3 | async-start | bytes 393216
  594.2 248.1 %collective-permute-start.6 = (f32[1,384]{1,0:T(1,128)S(1)}, f32[1,384]{1,0:T(1,128)S(1)}, u32[]{:S(2)}, u32[]{:S(2)}) collective-permute-start(f32[1,384]{1,0:T(1,128)S(1)} %slice.79), channel_id=1, source_target_pairs={{16,0},{32,16},{48,32},{64,48},{80,64},{96,80},{112,96},{128,112},... | collective-permute-start | bytes 4616 | tf_op jit(solution)/shard_map/ppermute | solution.py:17
  842.9 3.0 collective-permute-start.7
Sparse Core Ops, SparseCore 0:
  61.0 116.4 all-reduce.11
  330.7 110.3 all-reduce.13
  594.3 110.3 all-reduce.15
  857.6 110.3 all-reduce.17
where the time goes:
time: 978 us; the launch traced here: 977 us
  waiting for transfers between devices  443 us (45%)
  blocking collectives  395 us (40%)
  matrix products  67.2 us (7%)
  starting transfers between devices  28.2 us (3%)
  between operations  22.5 us (2%)
  other arithmetic  15.1 us (2%)
    unnamed x8, waiting for transfers between devices  440 us
    psum x3, blocking collectives, shards(): dual_sq = lax.psum(dual_local, ('tm', 'bat'))  327 us
    all_gather x4, blocking collectives, couple_backward(): lax.all_gather(duals, 'bat', axis=0, tiled=True)  68.3 us
    dot_general x4, matrix products, feeder_apply(): jnp.einsum('rjk,jmk->rjm', picked, block_values, precision=HIGH)  36.7 us
    ppermute x8, starting transfers between devices, shifted(): return lax.ppermute(block, axis, route)  28 us
    dot_general x4, matrix products, feeder_adjoint(): pushed = jnp.einsum('rjm,jmk->rjk', chosen, block_values, precision=HIGH)  23.3 us
  transfers between devices with their start and end apart: 12, of which 8 were waited for; matrix products, arithmetic and copies ran while one was open for 4% of the time, Pallas kernels for 0%

commit v1 on v0

v1 whole, which is shorter than its diff:
```python
import functools

import jax
import jax.numpy as jnp
from jax import lax
from jax.experimental import pallas as pl
from jax.experimental.pallas import tpu as pltpu
from jax.sharding import PartitionSpec as P

ITERS = 4
ETA_STEP = 0.4
EPS_NORM = 1e-06
LANES = 128
HALF = LANES // 2
F32 = jnp.float32

VMEM = pl.BlockSpec(memory_space=pltpu.VMEM)
SMEM = pl.BlockSpec(memory_space=pltpu.SMEM)

POWER, CHARGE, DYN, PRICE, INFLOW, DYN_NEXT, DYN_PREV, CHARGE_PREV, LIMIT, CAPACITY = range(10)


def rows_up(count):
    return -(-count // 8) * 8


def lane_iota(shape):
    return lax.broadcasted_iota(jnp.int32, shape, len(shape) - 1)


def clip(value, low, high):
    return jnp.minimum(jnp.maximum(value, low), high)


def total(value):
    return jnp.sum(jnp.sum(value, axis=0, keepdims=True), axis=1, keepdims=True)


def take_row(ref, array, pieces, groups, slot_rows):
    parts = [ref[pl.ds(array * pieces + i, groups, stride=slot_rows), :] for i in range(pieces)]
    return jnp.concatenate(parts, axis=0)


def put_row(ref, array, value, pieces, groups, slot_rows):
    for i in range(pieces):
        ref[pl.ds(array * pieces + i, groups, stride=slot_rows), :] = value[i * groups : (i + 1) * groups]


def row_of_block(block, pieces, groups):
    return (block % pieces) * groups + block // pieces


def feeder_adjoint(values, cols, offsets, duals_t, spread, sums, pieces, groups):
    blk = values.shape[1]
    for f in range(spread.shape[0]):
        spread[f] = jnp.broadcast_to(duals_t[:, f : f + 1], spread.shape[1:])
    sums[...] = jnp.zeros_like(sums)

    def step(j, f):
        f = jnp.where(j == offsets[f + 1], f + 1, f)
        product = values[j] * spread[f]
        c = row_of_block(cols[j], pieces, groups)
        sums[c] = sums[c] + jnp.sum(product.reshape(blk // 8, 8, LANES), axis=0)
        return f

    lax.fori_loop(0, values.shape[0], step, 0, unroll=4)
    return jnp.sum(sums[...], axis=1)


def feeder_apply(values, cols, offsets, field, sums, pieces, groups):
    blk = values.shape[1]

    def step(j, carry):
        f, acc = carry
        fresh = j == offsets[f + 1]
        f = jnp.where(fresh, f + 1, f)
        keep = jnp.where(fresh, 0.0, 1.0).astype(F32)
        c = row_of_block(cols[j], pieces, groups)
        acc = acc * keep + values[j] * field[pl.ds(c, 1), :]
        sums[f] = acc
        return f, acc

    lax.fori_loop(0, values.shape[0], step, (0, jnp.zeros((blk, LANES), F32)), unroll=4)
    lane = lane_iota((blk, LANES))
    out = jnp.zeros((blk, LANES), F32)
    for f in range(sums.shape[0]):
        out = jnp.where(lane == f, jnp.sum(sums[f], axis=1, keepdims=True), out)
    return out


def pack_sums(primal, dual):
    lane = lane_iota(primal.shape)
    return jnp.where(
        lane < HALF, primal + pltpu.roll(primal, HALF, 1), dual + pltpu.roll(dual, HALF, 1)
    )


def next_weight(weight, parts):
    both = jnp.sum(parts, axis=0, keepdims=True)
    lane = lane_iota(both.shape)
    primal_sq = total(jnp.where(lane < HALF, both, 0.0))
    dual_sq = total(jnp.where(lane < HALF, 0.0, both))
    ratio = jnp.sqrt((dual_sq + EPS_NORM) / (primal_sq + EPS_NORM))
    return jnp.broadcast_to(jnp.sqrt(weight[:, :1] * ratio), (1, LANES))


def row_sum(value):
    return jnp.sum(value, axis=0, keepdims=True)


def first_duals_kernel(dims, duals, limits, values, cols, offsets, pushed, duals_t, limits_t, spread, sums):
    blk = values.shape[1]
    feeds = duals.shape[0]
    for source, target in ((duals, duals_t), (limits, limits_t)):
        padded = jnp.concatenate([source[...], jnp.zeros((blk - feeds, LANES), F32)], axis=0)
        target[...] = jnp.transpose(padded)
    pushed[...] = feeder_adjoint(values, cols, offsets, duals_t[...], spread, sums, *dims[:2])


def slots_kernel(dims, power, charge, dyn, price, inflow, limit, capacity, after, before, slots):
    pieces, groups, slot_rows = dims
    arrays = {POWER: power, CHARGE: charge, DYN: dyn, PRICE: price, INFLOW: inflow}
    for i in range(pieces):
        cut = slice(i * LANES, (i + 1) * LANES)
        for array, ref in arrays.items():
            slots[pl.ds(array * pieces + i, groups, stride=slot_rows), :] = ref[:, cut]
        for array, ref in ((LIMIT, limit), (CAPACITY, capacity)):
            slots[pl.ds(array * pieces + i, groups, stride=slot_rows), :] = jnp.broadcast_to(
                ref[:, cut], (groups, LANES)
            )
        last = (groups - 1) * slot_rows
        slots[pl.ds(DYN_NEXT * pieces + i, groups - 1, stride=slot_rows), :] = dyn[1:, cut]
        slots[last + DYN_NEXT * pieces + i, :] = after[0, cut]
        for array, ref, line in ((DYN_PREV, dyn, 0), (CHARGE_PREV, charge, 1)):
            slots[pl.ds(slot_rows + array * pieces + i, groups - 1, stride=slot_rows), :] = ref[:-1, cut]
            slots[array * pieces + i, :] = before[line, cut]


def row_step(weight, first, power, charge, dyn, dyn_next, dyn_prev, charge_prev, pushed, price, inflow, limit, capacity):
    step_primal = ETA_STEP / weight[:, :1]
    step_dual = ETA_STEP * weight[:, :1]
    power_new = clip(power - step_primal * (price - dyn + pushed), -limit, limit)
    charge_new = clip(charge - step_primal * (dyn - dyn_next), 0.0, capacity)
    prev_new = clip(charge_prev - step_primal * (dyn_prev - dyn), 0.0, capacity)
    power_bar = 2.0 * power_new - power
    charge_bar = 2.0 * charge_new - charge
    prev_bar = jnp.where(first, 0.0, 2.0 * prev_new - charge_prev)
    dyn_new = dyn + step_dual * (charge_bar - prev_bar - power_bar - inflow)
    primal = row_sum((power_new - power) ** 2 + (charge_new - charge) ** 2)
    dual = row_sum((dyn_new - dyn) ** 2)
    return power_new, charge_new, dyn_new, prev_new, power_bar, primal, dual


def first_step():
    return (lax.axis_index("tm") == 0) & (lax.axis_index("bat") == 0)


def first_row_kernel(dims, slots, pushed, weight, power_out, charge_out, dyn_out, prev_out, bar_out, primal_out, dual_out):
    take = lambda array: take_row(slots, array, *dims)
    weight[...] = jnp.ones_like(weight)
    results = row_step(
        weight[...], first_step(), take(POWER), take(CHARGE), take(DYN), take(DYN_NEXT), take(DYN_PREV),
        take(CHARGE_PREV), pushed[...], take(PRICE), take(INFLOW), take(LIMIT), take(CAPACITY),
    )
    for ref, value in zip((power_out, charge_out, dyn_out, prev_out, bar_out, primal_out, dual_out), results):
        ref[...] = value


def row_kernel(dims, slots, parts, weight_in, power, charge, dyn, dyn_next, dyn_prev, charge_prev, pushed,
               weight, power_out, charge_out, dyn_out, prev_out, bar_out, primal_out, dual_out):
    take = lambda array: take_row(slots, array, *dims)
    weight[...] = next_weight(weight_in[...], parts[...])
    results = row_step(
        weight[...], first_step(), power[...], charge[...], dyn[...], dyn_next[...], dyn_prev[...],
        charge_prev[...], pushed[...], take(PRICE), take(INFLOW), take(LIMIT), take(CAPACITY),
    )
    for ref, value in zip((power_out, charge_out, dyn_out, prev_out, bar_out, primal_out, dual_out), results):
        ref[...] = value


def feeder_step(weight, coupled, duals_t, limits_t):
    step_dual = ETA_STEP * weight[:, :1]
    return jnp.maximum(0.0, duals_t + step_dual * (coupled - limits_t))


def feeder_kernel(dims, weight, bar, primal, dual, duals_t, limits_t, values, cols, offsets,
                  pushed, duals_out, parts, spread, sums):
    pieces, groups = dims[:2]
    coupled = feeder_apply(values, cols, offsets, bar, spread, pieces, groups)
    new = feeder_step(weight[...], coupled, duals_t[...], limits_t[...])
    duals_out[...] = new
    parts[...] = pack_sums(primal[...], dual[...] + row_sum((new - duals_t[...]) ** 2))
    pushed[...] = feeder_adjoint(values, cols, offsets, new, spread, sums, pieces, groups)


def back_kernel(dims, back_rows, weight, power, charge, dyn, bar, primal, dual, duals_t, limits_t, values, cols,
                offsets, pushed, duals_out, slots, spread, sums):
    pieces, groups = dims[:2]
    coupled = feeder_apply(values, cols, offsets, bar, spread, pieces, groups)
    new = feeder_step(weight[...], coupled, duals_t[...], limits_t[...])
    duals_out[...] = new
    parts = pack_sums(primal[...], dual[...] + row_sum((new - duals_t[...]) ** 2))
    slots[pl.ds(4 * pieces, groups, stride=back_rows), :] = jnp.broadcast_to(parts, (groups, LANES))
    adjoint = feeder_adjoint(values, cols, offsets, new, spread, sums, pieces, groups)
    pushed[...] = adjoint
    for array, value in enumerate((power[...], charge[...], dyn[...], adjoint)):
        put_row(slots, array, value, pieces, groups, back_rows)


def last_kernel(dims, back_rows, slots, parts, weight_in, power, dyn, pushed, duals_t, limits_t, values, cols,
                offsets, back, price, inflow, limit, capacity, after, before,
                power_out, charge_out, dyn_out, duals_out, bar, sums):
    pieces, groups, slot_rows = dims
    take = lambda array: take_row(slots, array, *dims)
    weight = next_weight(weight_in[...], parts[...])
    step_primal = ETA_STEP / weight[:, :1]
    step_dual = ETA_STEP * weight[:, :1]
    row_limit = take(LIMIT)
    row_new = clip(power[...] - step_primal * (take(PRICE) - dyn[...] + pushed[...]), -row_limit, row_limit)
    bar[...] = 2.0 * row_new - power[...]
    first = lax.axis_index("tm") == 0
    row = lax.broadcasted_iota(jnp.int32, (groups, LANES), 0)
    for i in range(pieces):
        cut = slice(i * LANES, (i + 1) * LANES)
        old = [back[pl.ds(array * pieces + i, groups, stride=back_rows), :] for array in range(4)]
        o_power, o_charge, o_dyn, o_pushed = old
        o_limit, o_capacity = limit[:, cut], capacity[:, cut]
        power_new = clip(o_power - step_primal * (price[:, cut] - o_dyn + o_pushed), -o_limit, o_limit)
        dyn_next = jnp.where(row == groups - 1, after[i : i + 1, :], pltpu.roll(o_dyn, groups - 1, 0))
        charge_new = clip(o_charge - step_primal * (o_dyn - dyn_next), 0.0, o_capacity)
        power_bar = 2.0 * power_new - o_power
        charge_bar = 2.0 * charge_new - o_charge
        edge_charge, edge_dyn = before[i : i + 1, :], before[pieces + i : pieces + i + 1, :]
        edge_new = clip(edge_charge - step_primal * (edge_dyn - o_dyn[:1]), 0.0, o_capacity)
        edge_bar = jnp.where(first, 0.0, 2.0 * edge_new - edge_charge)
        prev_bar = jnp.where(row == 0, edge_bar, pltpu.roll(charge_bar, 1, 0))
        dyn_new = o_dyn + step_dual * (charge_bar - prev_bar - power_bar - inflow[:, cut])
        power_out[:, cut] = power_new
        charge_out[:, cut] = charge_new
        dyn_out[:, cut] = dyn_new
    coupled = feeder_apply(values, cols, offsets, bar, sums, pieces, groups)
    new = feeder_step(weight, coupled, duals_t[...], limits_t[...])
    duals_out[...] = jnp.transpose(new)[: duals_out.shape[0]]


def shapes(*dims):
    return [jax.ShapeDtypeStruct(dim, F32) for dim in dims]


def call(kernel, name, in_specs, out_dims, scratch=(), flops=0, moved=0):
    return pl.pallas_call(
        kernel,
        name=name,
        in_specs=in_specs,
        out_specs=[VMEM] * len(out_dims),
        out_shape=shapes(*out_dims),
        scratch_shapes=[pltpu.VMEM(dim, F32) for dim in scratch],
        compiler_params=pltpu.CompilerParams(vmem_limit_bytes=24 * 1024 * 1024),
        cost_estimate=pl.CostEstimate(flops=flops, bytes_accessed=moved, transcendentals=0),
    )


def moved_to(value, axis, distance):
    count = lax.axis_size(axis)
    return lax.ppermute(value, axis, [(i, i + distance) for i in range(count) if 0 <= i + distance < count])


def exchange(value, axis):
    return lax.all_to_all(value, axis, 0, 0, tiled=True)


def shards(power0, charge0, dyn_dual0, feeder_dual0, price, inflow, power_limit, capacity, feeder_limit,
           block_values, block_cols, block_offsets):
    groups, local = power0.shape
    pieces = local // LANES
    blocks, blk = block_values.shape[:2]
    feeds = block_offsets.shape[0] - 1
    steps = lax.axis_size("tm")
    slot_rows = rows_up(10 * pieces)
    back_rows = rows_up(4 * pieces + 1)
    dims = (pieces, groups, slot_rows)
    row = (pieces * groups, LANES)
    line = (1, LANES)
    square = (blk, LANES)
    spread, sums = (feeds, blk, LANES), (pieces * groups, 8, LANES)
    matrix = (block_values, block_cols, block_offsets)
    matrix_specs = [VMEM, SMEM, SMEM]
    work = 2 * blocks * blk * LANES
    limit_line, capacity_line = power_limit.reshape(1, local), capacity.reshape(1, local)

    after = moved_to(dyn_dual0[:1], "tm", -1)
    before = moved_to(jnp.concatenate([dyn_dual0[-1:], charge0[-1:]], axis=0), "tm", 1)
    pushed, duals_t, limits_t = call(
        functools.partial(first_duals_kernel, dims), "first_duals",
        [VMEM, VMEM] + matrix_specs, [row, square, square], [spread, sums], work, 4 * blocks * blk * LANES,
    )(feeder_dual0.reshape(feeds, blk), feeder_limit.reshape(feeds, blk), *matrix)
    slots = call(
        functools.partial(slots_kernel, dims), "slots", [VMEM] * 9, [(groups * slot_rows, LANES)],
    )(power0, charge0, dyn_dual0, price, inflow, limit_line, capacity_line, after, before)[0]
    slots = exchange(slots.reshape(groups, slot_rows, LANES), "bat").reshape(groups * slot_rows, LANES)

    row_outs = [line] + [row] * 5 + [line] * 2
    weight, power, charge, dyn, charge_prev, bar, primal, dual = call(
        functools.partial(first_row_kernel, dims), "first_row", [VMEM] * 2, row_outs
    )(slots, pushed)

    for iteration in range(1, ITERS):
        if iteration + 1 < ITERS:
            dyn_next = moved_to(dyn, ("tm", "bat"), -1)
            dyn_prev = moved_to(dyn, ("tm", "bat"), 1)
            pushed, duals_t, parts = call(
                functools.partial(feeder_kernel, dims), "feeder",
                [VMEM] * 6 + matrix_specs, [row, square, line], [spread, sums], 2 * work, 4 * blocks * blk * LANES,
            )(weight, bar, primal, dual, duals_t, limits_t, *matrix)
            parts = exchange(jnp.broadcast_to(parts[None], (groups, 1, LANES)), "bat")
            parts = jnp.sum(parts, axis=0, keepdims=True)
            parts = exchange(jnp.broadcast_to(parts, (steps, 1, LANES)), "tm").reshape(steps, LANES)
            weight, power, charge, dyn, charge_prev, bar, primal, dual = call(
                functools.partial(row_kernel, dims), "row", [VMEM] * 10, row_outs
            )(slots, parts, weight, power, charge, dyn, dyn_next, dyn_prev, charge_prev, pushed)
        else:
            pushed, duals_t, back = call(
                functools.partial(back_kernel, dims, back_rows), "feeder_back",
                [VMEM] * 9 + matrix_specs, [row, square, (groups * back_rows, LANES)], [spread, sums], 2 * work,
                4 * blocks * blk * LANES,
            )(weight, power, charge, dyn, bar, primal, dual, duals_t, limits_t, *matrix)
            back = exchange(back.reshape(groups, back_rows, LANES), "bat")
            after = moved_to(back[0, 2 * pieces : 3 * pieces], "tm", -1)
            before = moved_to(back[-1, pieces : 3 * pieces], "tm", 1)
            parts = jnp.sum(back[:, 4 * pieces : 4 * pieces + 1], axis=0, keepdims=True)
            parts = exchange(jnp.broadcast_to(parts, (steps, 1, LANES)), "tm").reshape(steps, LANES)

    power, charge, dyn_dual, feeder_dual = call(
        functools.partial(last_kernel, dims, back_rows), "last",
        [VMEM] * 8 + matrix_specs + [VMEM] * 7,
        [(groups, local)] * 3 + [(feeds, blk)], [row, spread], work, 4 * blocks * blk * LANES,
    )(slots, parts, weight, power, dyn, pushed, duals_t, limits_t, *matrix,
      back.reshape(groups * back_rows, LANES), price, inflow, limit_line, capacity_line, after, before)
    return power, charge, dyn_dual, feeder_dual.reshape(1, feeds * blk)


def solution(mesh):
    split = P("tm", "bat")
    steps = P(("tm", "bat"), None)
    return jax.shard_map(
        shards,
        mesh=mesh,
        in_specs=(split, split, split, steps, split, split, P("bat"), P("bat"), P(), P(), P(), P()),
        out_specs=(split, split, split, steps),
        check_vma=False,
    )
```

time: 978 us -> 176 us (0.18)
  waiting for transfers between devices: 443 us -> 15.8 us
  blocking collectives: 395 us -> 39.2 us
  matrix products: 67.2 us -> 0 us
  starting transfers between devices: 28.2 us -> 78.5 us
  between operations: 22.5 us -> 0.89 us
  Pallas kernels: 0 us -> 17.1 us
  local copies, waits for them, and re-layouts: 5.79 us -> 22.8 us
  other arithmetic: 15.1 us -> 0.08 us
    unnamed x8 -> x0, waiting for transfers between devices: 440 us -> none
    psum x3 -> x0, blocking collectives: 327 us -> none  [shards(): dual_sq = lax.psum(dual_local, ('tm', 'bat'))]
    all_gather x4 -> x0, blocking collectives: 68.3 us -> none  [couple_backward(): lax.all_gather(duals, 'bat', axis=0, tiled=True)]
    dot_general x24 -> x0, matrix products: 67.2 us -> none  [the longest x4 36.7 us: feeder_apply(): jnp.einsum('rjk,jmk->rjm', picked, block_values, precision=HIGH)]
    all_to_all x0 -> x4, starting transfers between devices: none -> 45.8 us  [exchange(): return lax.all_to_all(value, axis, 0, 0, tiled=True)]
    all_to_all x0 -> x3, blocking collectives: none -> 39.2 us  [exchange(): return lax.all_to_all(value, axis, 0, 0, tiled=True)]
    pallas_call x0 -> x9, Pallas kernels: none -> 17.1 us  [the longest x2 6.68 us: shards(): call(functools.partial(feeder_kernel, dims), 'feeder', [VMEM] * 6 + matri...]
    unnamed x23 -> x36, local copies, waits for them, and re-layouts: 4.25 us -> 18.1 us
  transfers between devices with their start and end apart: 12 -> 12, of which waited for: 8 -> 7; matrix products, arithmetic and copies ran while one was open for 4% -> 1% of each run, Pallas kernels for 0% -> 1%
where the time goes in v1:
time: 176 us; the launch traced here: 174 us
  starting transfers between devices  78.5 us (45%)
  blocking collectives  39.2 us (22%)
  local copies, waits for them, and re-layouts  22.8 us (13%)
  Pallas kernels  17.1 us (10%)
  waiting for transfers between devices  15.8 us (9%)
    all_to_all x4, starting transfers between devices, exchange(): return lax.all_to_all(value, axis, 0, 0, tiled=True)  45.8 us
    all_to_all x3, blocking collectives, exchange(): return lax.all_to_all(value, axis, 0, 0, tiled=True)  39.2 us
    ppermute x8, starting transfers between devices, moved_to(): lax.ppermute(value, axis, [(i, i + distance) for i in range(count) if 0 <...  32.7 us
    unnamed x36, local copies, waits for them, and re-layouts  18.1 us
    all_to_all x4, waiting for transfers between devices, exchange(): return lax.all_to_all(value, axis, 0, 0, tiled=True)  10.9 us
    pallas_call x2, Pallas kernels, shards(): call(functools.partial(feeder_kernel, dims), 'feeder', [VMEM] * 6 + matri...  6.68 us
    ppermute x8, waiting for transfers between devices, moved_to(): lax.ppermute(value, axis, [(i, i + distance) for i in range(count) if 0 <...  4.89 us
  transfers between devices with their start and end apart: 12, of which 7 were waited for; matrix products, arithmetic and copies ran while one was open for 1% of the time, Pallas kernels for 1%

profile of v1, /device:TPU:1, one launch (start us, length us, event | category | flops | bytes accessed | tf_op | source)
XLA Modules:
  0.0 174.5 jit_solution(5537867213678757334)
XLA Ops:
  2.1 4.9 %collective-permute-start.1 = (f32[2,384]{1,0:T(2,128)S(1)}, f32[2,384]{1,0:T(2,128)S(1)}, u32[]{:S(2)}, u32[]{:S(2)}) collective-permute-start(f32[2,384]{1,0:T(2,128)S(1)} %pad_maximum_fusion), channel_id=1, source_target_pairs={{0,16},{16,32},{32,48},{48,64},{64,80},{80,96},{96,112},{112,128},... | collective-permute-start | bytes 9224 | tf_op jit(solution)/shard_map/ppermute | solution.py:265
  7.1 5.1 %collective-permute-start = (f32[1,384]{1,0:T(1,128)S(1)}, f32[1,384]{1,0:T(1,128)S(1)}, u32[]{:S(2)}, u32[]{:S(2)}) collective-permute-start(f32[1,384]{1,0:T(1,128)S(1)} %get-tuple-element.83), channel_id=1, source_target_pairs={{16,0},{32,16},{48,32},{64,48},{80,64},{96,80},{112,96},{128,112},... | collective-permute-start | bytes 4616 | tf_op jit(solution)/shard_map/ppermute | solution.py:265
  18.1 5.1 %all-to-all-start = ((f32[16,32,128]{2,1,0:T(8,128)}), f32[16,32,128]{2,1,0:T(8,128)S(1)}, u32[]{:S(2)}, u32[]{:S(2)}) async-start(f32[16,32,128]{2,1,0:T(8,128)} %bitcast), calls=%async_computation | async-start | bytes 524288 | tf_op jit(solution)/shard_map/all_to_all | solution.py:269
  23.3 2.3 %copy-done = f32[72,128,128]{2,1,0:T(8,128)S(1)} copy-done((f32[72,128,128]{2,1,0:T(8,128)S(1)}, f32[72,128,128]{2,1,0:T(8,128)}, u32[]{:S(2)}) %copy-start) | copy-done | bytes 4718616
  28.4 2.1 %first_duals.1 = (f32[48,128]{1,0:T(8,128)S(1)}, f32[128,128]{1,0:T(8,128)S(1)}, f32[128,128]{1,0:T(8,128)S(1)}) custom-call(f32[24,128]{1,0:T(8,128)S(1)} %bitcast.27, f32[24,128]{1,0:T(8,128)S(1)} %bitcast.28, f32[72,128,128]{2,1,0:T(8,128)S(1)} %copy-done, s32[72]{0:T(128)S(1)} %copy-done.12, s32[25]{0:T(128)S(1)} %copy-done.14), custom_call_target="tpu_custom_call" | custom-call | flops 2359296 | bytes 4718592 | tf_op jit(solution)/shard_map/first_duals/pallas_call | solution.py:293
  31.3 2.3 %copy-done.1 = f32[72,128,128]{2,1,0:T(8,128)S(1)} copy-done((f32[72,128,128]{2,1,0:T(8,128)S(1)}, f32[72,128,128]{2,1,0:T(8,128)}, u32[]{:S(2)}) %copy-start.1) | copy-done | bytes 4718616
  33.7 3.3 %feeder.2 = (f32[48,128]{1,0:T(8,128)S(1)}, f32[128,128]{1,0:T(8,128)S(1)}, f32[1,128]{1,0:T(1,128)S(1)}) custom-call(f32[1,128]{1,0:T(1,128)S(1)} %get-tuple-element.44.weight.weight_in, f32[48,128]{1,0:T(8,128)S(1)} %get-tuple-element.45.bar, f32[1,128]{1,0:T(1,128)S(1)} %get-tuple-element.46.primal, f32[1,128]{1,0:T(1,128)S(1)} %get-tuple-element.47.dual, ...), custom_call_target="tpu_custom_call" | custom-call | flops 4718592 | bytes 4718592 | tf_op jit(solution)/shard_map/feeder/pallas_call | solution.py:311
  37.0 12.2 %all_to_all.35 = f32[16,1,128]{2,1,0:T(1,128)S(1)} all-to-all(f32[16,1,128]{2,1,0:T(1,128)S(1)} %broadcast_in_dim.15), channel_id=1, replica_groups=mesh['tm'=32,'bat'=16] {'bat'}, dimensions={0} | all-to-all | bytes 16384 | tf_op jit(solution)/shard_map/all_to_all | solution.py:269
  49.9 17.1 %all-to-all-start.2 = ((f32[32,1,128]{2,1,0:T(1,128)}), f32[32,1,128]{2,1,0:T(1,128)S(1)}, u32[]{:S(2)}, u32[]{:S(2)}) async-start(f32[32,1,128]{2,1,0:T(1,128)} %broadcast_in_dim.16), calls=%async_computation.2 | async-start | bytes 32768 | tf_op jit(solution)/shard_map/all_to_all | solution.py:269
  67.0 2.2 %collective-permute-start.3 = (f32[48,128]{1,0:T(8,128)S(1)}, f32[48,128]{1,0:T(8,128)S(1)}, u32[]{:S(2)}, u32[]{:S(2)}) collective-permute-start(f32[48,128]{1,0:T(8,128)S(1)} %get-tuple-element.53.dyn), channel_id=1, source_target_pairs={{0,1},{1,2},{2,3},{3,4},{4,5},{5,6},{6,7},{7,8},{8,9},{9,10},{10,1... | collective-permute-start | bytes 73736 | tf_op jit(solution)/shard_map/ppermute | solution.py:265
  69.2 6.7 %collective-permute-start.2 = (f32[48,128]{1,0:T(8,128)S(1)}, f32[48,128]{1,0:T(8,128)S(1)}, u32[]{:S(2)}, u32[]{:S(2)}) collective-permute-start(f32[48,128]{1,0:T(8,128)S(1)} %get-tuple-element.53.dyn), channel_id=1, source_target_pairs={{1,0},{2,1},{3,2},{4,3},{5,4},{6,5},{7,6},{8,7},{9,8},{10,9},{11,1... | collective-permute-start | bytes 73736 | tf_op jit(solution)/shard_map/ppermute | solution.py:265
  75.9 0.9 collective-permute-done.2.dyn_next
  76.8 1.9 %all-to-all-done.2 = f32[32,1,128]{2,1,0:T(1,128)S(1)} async-done(((f32[32,1,128]{2,1,0:T(1,128)}), f32[32,1,128]{2,1,0:T(1,128)S(1)}, u32[]{:S(2)}, u32[]{:S(2)}) %all-to-all-start.2) | async-done | bytes 16416 | tf_op jit(solution)/shard_map/all_to_all | solution.py:269
  79.0 2.3 %copy-done.2 = f32[72,128,128]{2,1,0:T(8,128)S(1)} copy-done((f32[72,128,128]{2,1,0:T(8,128)S(1)}, f32[72,128,128]{2,1,0:T(8,128)}, u32[]{:S(2)}) %copy-start.2) | copy-done | bytes 4718616
  81.3 3.3 %feeder.3 = (f32[48,128]{1,0:T(8,128)S(1)}, f32[128,128]{1,0:T(8,128)S(1)}, f32[1,128]{1,0:T(1,128)S(1)}) custom-call(f32[1,128]{1,0:T(1,128)S(1)} %get-tuple-element.56.weight.weight_in, f32[48,128]{1,0:T(8,128)S(1)} %get-tuple-element.57.bar, f32[1,128]{1,0:T(1,128)S(1)} %get-tuple-element.58.primal, f32[1,128]{1,0:T(1,128)S(1)} %get-tuple-element.59.dual, ...), custom_call_target="tpu_custom_call" | custom-call | flops 4718592 | bytes 4718592 | tf_op jit(solution)/shard_map/feeder/pallas_call | solution.py:311
  84.7 13.3 %all_to_all.36 = f32[16,1,128]{2,1,0:T(1,128)S(1)} all-to-all(f32[16,1,128]{2,1,0:T(1,128)S(1)} %broadcast_in_dim.18), channel_id=1, replica_groups=mesh['tm'=32,'bat'=16] {'bat'}, dimensions={0} | all-to-all | bytes 16384 | tf_op jit(solution)/shard_map/all_to_all | solution.py:269
  98.6 12.0 %all-to-all-start.4 = ((f32[32,1,128]{2,1,0:T(1,128)}), f32[32,1,128]{2,1,0:T(1,128)S(1)}, u32[]{:S(2)}, u32[]{:S(2)}) async-start(f32[32,1,128]{2,1,0:T(1,128)} %broadcast_in_dim.19), calls=%async_computation.4 | async-start | bytes 32768 | tf_op jit(solution)/shard_map/all_to_all | solution.py:269
  110.7 2.2 %collective-permute-start.5 = (f32[48,128]{1,0:T(8,128)S(1)}, f32[48,128]{1,0:T(8,128)S(1)}, u32[]{:S(2)}, u32[]{:S(2)}) collective-permute-start(f32[48,128]{1,0:T(8,128)S(1)} %get-tuple-element.64.dyn), channel_id=1, source_target_pairs={{0,1},{1,2},{2,3},{3,4},{4,5},{5,6},{6,7},{7,8},{8,9},{9,10},{10,1... | collective-permute-start | bytes 73736 | tf_op jit(solution)/shard_map/ppermute | solution.py:265
  112.9 6.7 %collective-permute-start.4 = (f32[48,128]{1,0:T(8,128)S(1)}, f32[48,128]{1,0:T(8,128)S(1)}, u32[]{:S(2)}, u32[]{:S(2)}) collective-permute-start(f32[48,128]{1,0:T(8,128)S(1)} %get-tuple-element.64.dyn), channel_id=1, source_target_pairs={{1,0},{2,1},{3,2},{4,3},{5,4},{6,5},{7,6},{8,7},{9,8},{10,9},{11,1... | collective-permute-start | bytes 73736 | tf_op jit(solution)/shard_map/ppermute | solution.py:265
  119.6 0.9 collective-permute-done.4.dyn_next
  120.5 1.9 %all-to-all-done.4 = f32[32,1,128]{2,1,0:T(1,128)S(1)} async-done(((f32[32,1,128]{2,1,0:T(1,128)}), f32[32,1,128]{2,1,0:T(1,128)S(1)}, u32[]{:S(2)}, u32[]{:S(2)}) %all-to-all-start.4) | async-done | bytes 16416 | tf_op jit(solution)/shard_map/all_to_all | solution.py:269
  122.4 0.9 row.3
  123.3 2.3 %copy-done.3 = f32[72,128,128]{2,1,0:T(8,128)S(1)} copy-done((f32[72,128,128]{2,1,0:T(8,128)S(1)}, f32[72,128,128]{2,1,0:T(8,128)}, u32[]{:S(2)}) %copy-start.3) | copy-done | bytes 4718616
  125.6 3.4 %feeder_back.1 = (f32[48,128]{1,0:T(8,128)S(1)}, f32[128,128]{1,0:T(8,128)S(1)}, f32[256,128]{1,0:T(8,128)S(1)}) custom-call(f32[1,128]{1,0:T(1,128)S(1)} %get-tuple-element.67.weight.weight_in, f32[48,128]{1,0:T(8,128)S(1)} %get-tuple-element.68.power, f32[48,128]{1,0:T(8,128)S(1)} %get-tuple-element.69.charge, f32[48,128]{1,0:T(8,128)S(1)} %get-tuple-element.70.dyn, ...), custom_call_target="tpu_custom_call" | custom-call | flops 4718592 | bytes 4718592 | tf_op jit(solution)/shard_map/feeder_back/pallas_call | solution.py:322
  129.0 13.7 %all_to_all.37 = f32[16,16,128]{2,1,0:T(8,128)S(1)} all-to-all(f32[16,16,128]{2,1,0:T(8,128)S(1)} %bitcast.23), channel_id=1, replica_groups=mesh['tm'=32,'bat'=16] {'bat'}, dimensions={0} | all-to-all | bytes 262144 | tf_op jit(solution)/shard_map/all_to_all | solution.py:269
  142.7 2.7 %collective-permute-start.7 = (f32[6,128]{1,0:T(8,128)S(1)}, f32[6,128]{1,0:T(8,128)S(1)}, u32[]{:S(2)}, u32[]{:S(2)}) collective-permute-start(f32[6,128]{1,0:T(8,128)S(1)} %slice_bitcast_fusion), channel_id=1, source_target_pairs={{0,16},{16,32},{32,48},{48,64},{64,80},{80,96},{96,112},{112,128},... | collective-permute-start | bytes 9224 | tf_op jit(solution)/shard_map/ppermute | solution.py:265
  146.1 11.6 %all-to-all-start.6 = ((f32[32,1,128]{2,1,0:T(1,128)}), f32[32,1,128]{2,1,0:T(1,128)S(1)}, u32[]{:S(2)}, u32[]{:S(2)}) async-start(f32[32,1,128]{2,1,0:T(1,128)} %broadcast_in_dim.40), calls=%async_computation.6 | async-start | bytes 32768 | tf_op jit(solution)/shard_map/all_to_all | solution.py:269
  157.7 2.1 %collective-permute-start.6 = (f32[3,128]{1,0:T(4,128)S(1)}, f32[3,128]{1,0:T(4,128)S(1)}, u32[]{:S(2)}, u32[]{:S(2)}) collective-permute-start(f32[3,128]{1,0:T(4,128)S(1)} %slice_bitcast_fusion.1), channel_id=1, source_target_pairs={{16,0},{32,16},{48,32},{64,48},{80,64},{96,80},{112,96},{128,112},... | collective-permute-start | bytes 4616 | tf_op jit(solution)/shard_map/ppermute | solution.py:265
  159.9 3.0 %collective-permute-done.6.after = f32[3,128]{1,0:T(4,128)S(1)} collective-permute-done((f32[3,128]{1,0:T(4,128)S(1)}, f32[3,128]{1,0:T(4,128)S(1)}, u32[]{:S(2)}, u32[]{:S(2)}) %collective-permute-start.6) | collective-permute-done | bytes 1568 | tf_op jit(solution)/shard_map/ppermute | solution.py:265
  162.9 6.5 %all-to-all-done.6 = f32[32,1,128]{2,1,0:T(1,128)S(1)} async-done(((f32[32,1,128]{2,1,0:T(1,128)}), f32[32,1,128]{2,1,0:T(1,128)S(1)}, u32[]{:S(2)}, u32[]{:S(2)}) %all-to-all-start.6) | async-done | bytes 16416 | tf_op jit(solution)/shard_map/all_to_all | solution.py:269
  169.4 2.3 %copy-done.4 = f32[72,128,128]{2,1,0:T(8,128)S(1)} copy-done((f32[72,128,128]{2,1,0:T(8,128)S(1)}, f32[72,128,128]{2,1,0:T(8,128)}, u32[]{:S(2)}) %copy-start.4) | copy-done | bytes 4718616
  171.8 2.7 %last.1 = (f32[16,384]{1,0:T(8,128)}, f32[16,384]{1,0:T(8,128)}, f32[16,384]{1,0:T(8,128)}, f32[24,128]{1,0:T(8,128)}) custom-call(f32[512,128]{1,0:T(8,128)S(1)} %bitcast.21, f32[32,128]{1,0:T(8,128)S(1)} %bitcast.26, f32[1,128]{1,0:T(1,128)S(1)} %get-tuple-element.67.weight.weight_in, f32[48,128]{1,0:T(8,128)S(1)} %get-tuple-element.68.power, ...), custom_call_target="tpu_custom_call" | custom-call | flops 2359296 | bytes 4718592 | tf_op jit(solution)/shard_map/last/pallas_call | solution.py:333
  (55 shorter events, 13.2 us)
Async XLA Ops:
  0.6 30.7 %copy-start.15 = (s32[25]{0:T(128)S(1)}, s32[25]{0:T(128)}, u32[]{:S(2)}) copy-start(s32[25]{0:T(128)} %offsets.9) | copy-start | bytes 304
  0.6 30.7 %copy-start.13 = (s32[72]{0:T(128)S(1)}, s32[72]{0:T(128)}, u32[]{:S(2)}) copy-start(s32[72]{0:T(128)} %cols.9) | copy-start | bytes 868
  2.1 11.5 %collective-permute-start.1 = (f32[2,384]{1,0:T(2,128)S(1)}, f32[2,384]{1,0:T(2,128)S(1)}, u32[]{:S(2)}, u32[]{:S(2)}) collective-permute-start(f32[2,384]{1,0:T(2,128)S(1)} %pad_maximum_fusion), channel_id=1, source_target_pairs={{0,16},{16,32},{32,48},{48,64},{64,80},{80,96},{96,112},{112,128},... | collective-permute-start | bytes 9224 | tf_op jit(solution)/shard_map/ppermute | solution.py:265
  7.1 6.5 %collective-permute-start = (f32[1,384]{1,0:T(1,128)S(1)}, f32[1,384]{1,0:T(1,128)S(1)}, u32[]{:S(2)}, u32[]{:S(2)}) collective-permute-start(f32[1,384]{1,0:T(1,128)S(1)} %get-tuple-element.83), channel_id=1, source_target_pairs={{16,0},{32,16},{48,32},{64,48},{80,64},{96,80},{112,96},{128,112},... | collective-permute-start | bytes 4616 | tf_op jit(solution)/shard_map/ppermute | solution.py:265
  13.6 0.7 copy-start.5
  14.3 0.7 copy-start.7
  15.1 0.7 copy-start.9
  15.8 0.7 copy-start.10
  16.5 0.7 copy-start.11
  18.1 13.0 %all-to-all-start = ((f32[16,32,128]{2,1,0:T(8,128)}), f32[16,32,128]{2,1,0:T(8,128)S(1)}, u32[]{:S(2)}, u32[]{:S(2)}) async-start(f32[16,32,128]{2,1,0:T(8,128)} %bitcast), calls=%async_computation | async-start | bytes 524288 | tf_op jit(solution)/shard_map/all_to_all | solution.py:269
  23.3 2.3 %copy-start = (f32[72,128,128]{2,1,0:T(8,128)S(1)}, f32[72,128,128]{2,1,0:T(8,128)}, u32[]{:S(2)}) copy-start(f32[72,128,128]{2,1,0:T(8,128)} %values.9) | copy-start | bytes 14155780
  25.6 0.7 copy-start.12
  26.3 0.7 copy-start.14
  26.9 0.7 copy-start.16
  27.6 0.7 copy-start.17
  31.3 2.3 %copy-start.1 = (f32[72,128,128]{2,1,0:T(8,128)S(1)}, f32[72,128,128]{2,1,0:T(8,128)}, u32[]{:S(2)}) copy-start(f32[72,128,128]{2,1,0:T(8,128)} %values.9) | copy-start | bytes 14155780
  49.9 28.8 %all-to-all-start.2 = ((f32[32,1,128]{2,1,0:T(1,128)}), f32[32,1,128]{2,1,0:T(1,128)S(1)}, u32[]{:S(2)}, u32[]{:S(2)}) async-start(f32[32,1,128]{2,1,0:T(1,128)} %broadcast_in_dim.16), calls=%async_computation.2 | async-start | bytes 32768 | tf_op jit(solution)/shard_map/all_to_all | solution.py:269
  67.0 8.9 %collective-permute-start.3 = (f32[48,128]{1,0:T(8,128)S(1)}, f32[48,128]{1,0:T(8,128)S(1)}, u32[]{:S(2)}, u32[]{:S(2)}) collective-permute-start(f32[48,128]{1,0:T(8,128)S(1)} %get-tuple-element.53.dyn), channel_id=1, source_target_pairs={{0,1},{1,2},{2,3},{3,4},{4,5},{5,6},{6,7},{7,8},{8,9},{9,10},{10,1... | collective-permute-start | bytes 73736 | tf_op jit(solution)/shard_map/ppermute | solution.py:265
  69.2 7.6 %collective-permute-start.2 = (f32[48,128]{1,0:T(8,128)S(1)}, f32[48,128]{1,0:T(8,128)S(1)}, u32[]{:S(2)}, u32[]{:S(2)}) collective-permute-start(f32[48,128]{1,0:T(8,128)S(1)} %get-tuple-element.53.dyn), channel_id=1, source_target_pairs={{1,0},{2,1},{3,2},{4,3},{5,4},{6,5},{7,6},{8,7},{9,8},{10,9},{11,1... | collective-permute-start | bytes 73736 | tf_op jit(solution)/shard_map/ppermute | solution.py:265
  79.0 2.3 %copy-start.2 = (f32[72,128,128]{2,1,0:T(8,128)S(1)}, f32[72,128,128]{2,1,0:T(8,128)}, u32[]{:S(2)}) copy-start(f32[72,128,128]{2,1,0:T(8,128)} %values.9) | copy-start | bytes 14155780
  81.3 88.1 %copy-start.6 = (f32[16,384]{1,0:T(8,128)S(1)}, f32[16,384]{1,0:T(8,128)}, u32[]{:S(2)}) copy-start(f32[16,384]{1,0:T(8,128)} %price.3) | copy-start | bytes 73732
  81.3 88.1 %copy-start.8 = (f32[16,384]{1,0:T(8,128)S(1)}, f32[16,384]{1,0:T(8,128)}, u32[]{:S(2)}) copy-start(f32[16,384]{1,0:T(8,128)} %inflow.3) | copy-start | bytes 73732
  98.6 23.8 %all-to-all-start.4 = ((f32[32,1,128]{2,1,0:T(1,128)}), f32[32,1,128]{2,1,0:T(1,128)S(1)}, u32[]{:S(2)}, u32[]{:S(2)}) async-start(f32[32,1,128]{2,1,0:T(1,128)} %broadcast_in_dim.19), calls=%async_computation.4 | async-start | bytes 32768 | tf_op jit(solution)/shard_map/all_to_all | solution.py:269
  110.7 8.9 %collective-permute-start.5 = (f32[48,128]{1,0:T(8,128)S(1)}, f32[48,128]{1,0:T(8,128)S(1)}, u32[]{:S(2)}, u32[]{:S(2)}) collective-permute-start(f32[48,128]{1,0:T(8,128)S(1)} %get-tuple-element.64.dyn), channel_id=1, source_target_pairs={{0,1},{1,2},{2,3},{3,4},{4,5},{5,6},{6,7},{7,8},{8,9},{9,10},{10,1... | collective-permute-start | bytes 73736 | tf_op jit(solution)/shard_map/ppermute | solution.py:265
  112.9 7.6 %collective-permute-start.4 = (f32[48,128]{1,0:T(8,128)S(1)}, f32[48,128]{1,0:T(8,128)S(1)}, u32[]{:S(2)}, u32[]{:S(2)}) collective-permute-start(f32[48,128]{1,0:T(8,128)S(1)} %get-tuple-element.64.dyn), channel_id=1, source_target_pairs={{1,0},{2,1},{3,2},{4,3},{5,4},{6,5},{7,6},{8,7},{9,8},{10,9},{11,1... | collective-permute-start | bytes 73736 | tf_op jit(solution)/shard_map/ppermute | solution.py:265
  123.3 2.3 %copy-start.3 = (f32[72,128,128]{2,1,0:T(8,128)S(1)}, f32[72,128,128]{2,1,0:T(8,128)}, u32[]{:S(2)}) copy-start(f32[72,128,128]{2,1,0:T(8,128)} %values.9) | copy-start | bytes 14155780
  142.7 20.2 %collective-permute-start.7 = (f32[6,128]{1,0:T(8,128)S(1)}, f32[6,128]{1,0:T(8,128)S(1)}, u32[]{:S(2)}, u32[]{:S(2)}) collective-permute-start(f32[6,128]{1,0:T(8,128)S(1)} %slice_bitcast_fusion), channel_id=1, source_target_pairs={{0,16},{16,32},{32,48},{48,64},{64,80},{80,96},{96,112},{112,128},... | collective-permute-start | bytes 9224 | tf_op jit(solution)/shard_map/ppermute | solution.py:265
  146.1 23.3 %all-to-all-start.6 = ((f32[32,1,128]{2,1,0:T(1,128)}), f32[32,1,128]{2,1,0:T(1,128)S(1)}, u32[]{:S(2)}, u32[]{:S(2)}) async-start(f32[32,1,128]{2,1,0:T(1,128)} %broadcast_in_dim.40), calls=%async_computation.6 | async-start | bytes 32768 | tf_op jit(solution)/shard_map/all_to_all | solution.py:269
  157.7 5.2 %collective-permute-start.6 = (f32[3,128]{1,0:T(4,128)S(1)}, f32[3,128]{1,0:T(4,128)S(1)}, u32[]{:S(2)}, u32[]{:S(2)}) collective-permute-start(f32[3,128]{1,0:T(4,128)S(1)} %slice_bitcast_fusion.1), channel_id=1, source_target_pairs={{16,0},{32,16},{48,32},{64,48},{80,64},{96,80},{112,96},{128,112},... | collective-permute-start | bytes 4616 | tf_op jit(solution)/shard_map/ppermute | solution.py:265
  169.4 2.3 %copy-start.4 = (f32[72,128,128]{2,1,0:T(8,128)S(1)}, f32[72,128,128]{2,1,0:T(8,128)}, u32[]{:S(2)}) copy-start(f32[72,128,128]{2,1,0:T(8,128)} %values.9) | copy-start | bytes 14155780

commit v2 on v1

v2 whole, which is shorter than its diff:
```python
import functools

import jax
import jax.numpy as jnp
from jax import lax
from jax.experimental import pallas as pl
from jax.experimental.pallas import tpu as pltpu
from jax.sharding import PartitionSpec as P

ITERS = 4
ETA_STEP = 0.4
EPS_NORM = 1e-06
LANES = 128
HALF = LANES // 2
F32 = jnp.float32

VMEM = pl.BlockSpec(memory_space=pltpu.VMEM)
SMEM = pl.BlockSpec(memory_space=pltpu.SMEM)

POWER, CHARGE, DYN, PRICE, INFLOW, LIMIT, CAPACITY, DYN_NEXT, DYN_PREV, CHARGE_PREV = range(10)


def rows_up(count):
    return -(-count // 8) * 8


def lane_iota(shape):
    return lax.broadcasted_iota(jnp.int32, shape, len(shape) - 1)


def clip(value, low, high):
    return jnp.minimum(jnp.maximum(value, low), high)


def total(value):
    return jnp.sum(jnp.sum(value, axis=0, keepdims=True), axis=1, keepdims=True)


def take_row(ref, array, pieces, groups, slot_rows):
    parts = [ref[pl.ds(array * pieces + i, groups, stride=slot_rows), :] for i in range(pieces)]
    return jnp.concatenate(parts, axis=0)


def put_row(ref, array, value, pieces, groups, slot_rows):
    for i in range(pieces):
        ref[pl.ds(array * pieces + i, groups, stride=slot_rows), :] = value[i * groups : (i + 1) * groups]


def row_of_block(block, pieces, groups):
    return (block % pieces) * groups + block // pieces


def feeder_adjoint(values, table, duals_t, spread, sums, pieces, groups):
    blocks, blk = values.shape[:2]
    for f in range(spread.shape[0]):
        spread[f] = jnp.broadcast_to(duals_t[:, f : f + 1], spread.shape[1:])
    sums[...] = jnp.zeros_like(sums)

    def step(j, f):
        f = jnp.where(j == table[blocks + f + 1], f + 1, f)
        product = values[j] * spread[f]
        c = row_of_block(table[j], pieces, groups)
        sums[c] = sums[c] + jnp.sum(product.reshape(blk // 8, 8, LANES), axis=0)
        return f

    lax.fori_loop(0, blocks, step, 0, unroll=4)
    return jnp.sum(sums[...], axis=1)


def feeder_apply(values, table, field, sums, pieces, groups):
    blocks, blk = values.shape[:2]

    def step(j, carry):
        f, acc = carry
        fresh = j == table[blocks + f + 1]
        f = jnp.where(fresh, f + 1, f)
        keep = jnp.where(fresh, 0.0, 1.0).astype(F32)
        c = row_of_block(table[j], pieces, groups)
        acc = acc * keep + values[j] * field[pl.ds(c, 1), :]
        sums[f] = acc
        return f, acc

    lax.fori_loop(0, blocks, step, (0, jnp.zeros((blk, LANES), F32)), unroll=4)
    lane = lane_iota((blk, LANES))
    out = jnp.zeros((blk, LANES), F32)
    for f in range(sums.shape[0]):
        out = jnp.where(lane == f, jnp.sum(sums[f], axis=1, keepdims=True), out)
    return out


def pack_sums(primal, dual):
    lane = lane_iota(primal.shape)
    return jnp.where(
        lane < HALF, primal + pltpu.roll(primal, HALF, 1), dual + pltpu.roll(dual, HALF, 1)
    )


def next_weight(weight, parts):
    both = jnp.sum(parts, axis=0, keepdims=True)
    lane = lane_iota(both.shape)
    primal_sq = total(jnp.where(lane < HALF, both, 0.0))
    dual_sq = total(jnp.where(lane < HALF, 0.0, both))
    ratio = jnp.sqrt((dual_sq + EPS_NORM) / (primal_sq + EPS_NORM))
    return jnp.broadcast_to(jnp.sqrt(weight[:, :1] * ratio), (1, LANES))


def row_sum(value):
    return jnp.sum(value, axis=0, keepdims=True)


def first_duals_kernel(dims, duals, values, table, pushed, duals_t, limits_t, spread, sums):
    blk = values.shape[1]
    feeds = duals.shape[1]
    for i, target in enumerate((duals_t, limits_t)):
        padded = jnp.concatenate([duals[i], jnp.zeros((blk - feeds, LANES), F32)], axis=0)
        target[...] = jnp.transpose(padded)
    pushed[...] = feeder_adjoint(values, table, duals_t[...], spread, sums, *dims[:2])


def slots_kernel(dims, inputs, after, before, slots):
    pieces, groups, slot_rows = dims
    last = (groups - 1) * slot_rows
    for i in range(pieces):
        cut = slice(i * LANES, (i + 1) * LANES)
        for array in range(inputs.shape[0]):
            slots[pl.ds(array * pieces + i, groups, stride=slot_rows), :] = inputs[array, :, cut]
        slots[pl.ds(DYN_NEXT * pieces + i, groups - 1, stride=slot_rows), :] = inputs[DYN, 1:, cut]
        slots[last + DYN_NEXT * pieces + i, :] = after[0, cut]
        for array, source in ((DYN_PREV, DYN), (CHARGE_PREV, CHARGE)):
            slots[pl.ds(slot_rows + array * pieces + i, groups - 1, stride=slot_rows), :] = inputs[source, :-1, cut]
            slots[array * pieces + i, :] = before[source - CHARGE, cut]


def row_step(weight, first, power, charge, dyn, dyn_next, dyn_prev, charge_prev, pushed, price, inflow, limit, capacity):
    step_primal = ETA_STEP / weight[:, :1]
    step_dual = ETA_STEP * weight[:, :1]
    power_new = clip(power - step_primal * (price - dyn + pushed), -limit, limit)
    charge_new = clip(charge - step_primal * (dyn - dyn_next), 0.0, capacity)
    prev_new = clip(charge_prev - step_primal * (dyn_prev - dyn), 0.0, capacity)
    power_bar = 2.0 * power_new - power
    charge_bar = 2.0 * charge_new - charge
    prev_bar = jnp.where(first, 0.0, 2.0 * prev_new - charge_prev)
    dyn_new = dyn + step_dual * (charge_bar - prev_bar - power_bar - inflow)
    primal = row_sum((power_new - power) ** 2 + (charge_new - charge) ** 2)
    dual = row_sum((dyn_new - dyn) ** 2)
    return power_new, charge_new, dyn_new, prev_new, power_bar, primal, dual


def first_step():
    return (lax.axis_index("tm") == 0) & (lax.axis_index("bat") == 0)


def first_row_kernel(dims, slots, pushed, weight, power_out, charge_out, dyn_out, prev_out, bar_out, primal_out, dual_out):
    take = lambda array: take_row(slots, array, *dims)
    weight[...] = jnp.ones_like(weight)
    results = row_step(
        weight[...], first_step(), take(POWER), take(CHARGE), take(DYN), take(DYN_NEXT), take(DYN_PREV),
        take(CHARGE_PREV), pushed[...], take(PRICE), take(INFLOW), take(LIMIT), take(CAPACITY),
    )
    for ref, value in zip((power_out, charge_out, dyn_out, prev_out, bar_out, primal_out, dual_out), results):
        ref[...] = value


def row_kernel(dims, slots, parts, weight_in, power, charge, dyn, dyn_next, dyn_prev, charge_prev, pushed,
               weight, power_out, charge_out, dyn_out, prev_out, bar_out, primal_out, dual_out):
    take = lambda array: take_row(slots, array, *dims)
    weight[...] = next_weight(weight_in[...], parts[...])
    results = row_step(
        weight[...], first_step(), power[...], charge[...], dyn[...], dyn_next[...], dyn_prev[...],
        charge_prev[...], pushed[...], take(PRICE), take(INFLOW), take(LIMIT), take(CAPACITY),
    )
    for ref, value in zip((power_out, charge_out, dyn_out, prev_out, bar_out, primal_out, dual_out), results):
        ref[...] = value


def feeder_step(weight, coupled, duals_t, limits_t):
    step_dual = ETA_STEP * weight[:, :1]
    return jnp.maximum(0.0, duals_t + step_dual * (coupled - limits_t))


def feeder_kernel(dims, weight, bar, primal, dual, duals_t, limits_t, values, table,
                  pushed, duals_out, parts, spread, sums):
    pieces, groups = dims[:2]
    coupled = feeder_apply(values, table, bar, spread, pieces, groups)
    new = feeder_step(weight[...], coupled, duals_t[...], limits_t[...])
    duals_out[...] = new
    parts[...] = pack_sums(primal[...], dual[...] + row_sum((new - duals_t[...]) ** 2))
    pushed[...] = feeder_adjoint(values, table, new, spread, sums, pieces, groups)


def back_kernel(dims, back_rows, parts, *rest):
    pieces, groups = dims[:2]
    arrays, slots = rest[:-1], rest[-1]
    for array, ref in enumerate(arrays):
        put_row(slots, array, ref[...], pieces, groups, back_rows)
    slots[pl.ds(len(arrays) * pieces, groups, stride=back_rows), :] = jnp.broadcast_to(parts[...], (groups, LANES))


def relay_kernel(start, stride, received, parts):
    count = received.shape[0] // stride
    summed = jnp.sum(received[pl.ds(start, count, stride=stride), :], axis=0, keepdims=True)
    parts[...] = jnp.broadcast_to(summed, parts.shape)


def last_kernel(dims, back_rows, slots, parts, weight_in, power, dyn, pushed, duals_t, limits_t, values, table,
                back, inputs,
                power_out, charge_out, dyn_out, duals_out, bar, sums):
    pieces, groups, slot_rows = dims
    take = lambda array: take_row(slots, array, *dims)
    weight = next_weight(weight_in[...], parts[...])
    step_primal = ETA_STEP / weight[:, :1]
    row_limit = take(LIMIT)
    row_new = clip(power[...] - step_primal * (take(PRICE) - dyn[...] + pushed[...]), -row_limit, row_limit)
    bar[...] = 2.0 * row_new - power[...]
    first = (lax.axis_index("tm") == 0) & (lax.broadcasted_iota(jnp.int32, (groups, LANES), 0) == 0)
    for i in range(pieces):
        cut = slice(i * LANES, (i + 1) * LANES)
        state = [back[pl.ds(array * pieces + i, groups, stride=back_rows), :] for array in range(7)]
        results = row_step(
            weight, first, *state, *(inputs[array, :, cut] for array in (PRICE, INFLOW, LIMIT, CAPACITY))
        )
        for ref, value in zip((power_out, charge_out, dyn_out), results):
            ref[:, cut] = value
    coupled = feeder_apply(values, table, bar, sums, pieces, groups)
    new = feeder_step(weight, coupled, duals_t[...], limits_t[...])
    duals_out[...] = jnp.transpose(new)[: duals_out.shape[0]]


def shapes(*dims):
    return [jax.ShapeDtypeStruct(dim, F32) for dim in dims]


def call(kernel, name, in_specs, out_dims, scratch=(), flops=0, moved=0):
    return pl.pallas_call(
        kernel,
        name=name,
        in_specs=in_specs,
        out_specs=[VMEM] * len(out_dims),
        out_shape=shapes(*out_dims),
        scratch_shapes=[pltpu.VMEM(dim, F32) for dim in scratch],
        compiler_params=pltpu.CompilerParams(vmem_limit_bytes=16 * 1024 * 1024),
        cost_estimate=pl.CostEstimate(flops=flops, bytes_accessed=moved, transcendentals=0),
    )


def stacked(*arrays):
    shape = (len(arrays),) + arrays[0].shape
    index = lax.broadcasted_iota(jnp.int32, shape, 0)
    out = jnp.broadcast_to(arrays[-1], shape)
    for i, array in enumerate(arrays[:-1]):
        out = jnp.where(index == i, array, out)
    return out


def moved_to(value, axis, distance):
    count = lax.axis_size(axis)
    return lax.ppermute(value, axis, [(i, i + distance) for i in range(count) if 0 <= i + distance < count])


def exchange(value, axis):
    return lax.all_to_all(value, axis, 0, 0, tiled=True)


def shards(power0, charge0, dyn_dual0, feeder_dual0, price, inflow, power_limit, capacity, feeder_limit,
           block_values, block_cols, block_offsets):
    groups, local = power0.shape
    pieces = local // LANES
    blocks, blk = block_values.shape[:2]
    feeds = block_offsets.shape[0] - 1
    steps = lax.axis_size("tm")
    slot_rows = rows_up(10 * pieces)
    back_rows = rows_up(7 * pieces + 1)
    dims = (pieces, groups, slot_rows)
    row = (pieces * groups, LANES)
    line = (1, LANES)
    square = (blk, LANES)
    own = (groups, local)
    spread, sums = (feeds, blk, LANES), (pieces * groups, 8, LANES)
    matrix_specs = [VMEM, SMEM]
    work, moved = 2 * blocks * blk * LANES, 4 * blocks * blk * LANES
    inputs = stacked(power0, charge0, dyn_dual0, price, inflow, power_limit, capacity)
    duals = stacked(feeder_dual0.reshape(feeds, blk), feeder_limit.reshape(feeds, blk))
    matrix = (block_values, jnp.concatenate([block_cols, block_offsets]))

    after = moved_to(inputs[DYN, :1], "tm", -1)
    before = moved_to(inputs[CHARGE : DYN + 1, -1], "tm", 1)
    pushed, duals_t, limits_t = call(
        functools.partial(first_duals_kernel, dims), "first_duals",
        [VMEM] + matrix_specs, [row, square, square], [spread, sums], work, moved,
    )(duals, *matrix)
    pushed, after, before = lax.optimization_barrier((pushed, after, before))
    slots = call(
        functools.partial(slots_kernel, dims), "slots", [VMEM] * 3, [(groups * slot_rows, LANES)],
    )(inputs, after, before)[0]
    slots = exchange(slots.reshape(groups, slot_rows, LANES), "bat").reshape(groups * slot_rows, LANES)

    row_outs = [line] + [row] * 5 + [line] * 2
    weight, power, charge, dyn, charge_prev, bar, primal, dual = call(
        functools.partial(first_row_kernel, dims), "first_row", [VMEM] * 2, row_outs
    )(slots, pushed)

    for iteration in range(1, ITERS):
        dyn_next = moved_to(dyn, ("tm", "bat"), -1)
        dyn_prev = moved_to(dyn, ("tm", "bat"), 1)
        pushed, duals_t, parts = call(
            functools.partial(feeder_kernel, dims), "feeder",
            [VMEM] * 6 + matrix_specs, [row, square, line], [spread, sums], 2 * work, moved,
        )(weight, bar, primal, dual, duals_t, limits_t, *matrix)
        parts, dyn_next, dyn_prev = lax.optimization_barrier((parts, dyn_next, dyn_prev))
        if iteration + 1 < ITERS:
            received = exchange(jnp.broadcast_to(parts[None], (groups, 1, LANES)), "bat").reshape(groups, LANES)
            relay = functools.partial(relay_kernel, 0, 1)
        else:
            back = call(
                functools.partial(back_kernel, dims, back_rows), "back", [VMEM] * 8, [(groups * back_rows, LANES)]
            )(parts, power, charge, dyn, dyn_next, dyn_prev, charge_prev, pushed)[0]
            back = exchange(back.reshape(groups, back_rows, LANES), "bat").reshape(groups * back_rows, LANES)
            received = back
            relay = functools.partial(relay_kernel, 7 * pieces, back_rows)
        parts = call(relay, "relay", [VMEM], [(steps, LANES)])(received)[0]
        parts = exchange(parts.reshape(steps, 1, LANES), "tm").reshape(steps, LANES)
        if iteration + 1 < ITERS:
            weight, power, charge, dyn, charge_prev, bar, primal, dual = call(
                functools.partial(row_kernel, dims), "row", [VMEM] * 10, row_outs
            )(slots, parts, weight, power, charge, dyn, dyn_next, dyn_prev, charge_prev, pushed)

    power, charge, dyn_dual, feeder_dual = call(
        functools.partial(last_kernel, dims, back_rows), "last",
        [VMEM] * 8 + matrix_specs + [VMEM] * 2, [own] * 3 + [(feeds, blk)], [row, spread], work, moved,
    )(slots, parts, weight, power, dyn, pushed, duals_t, limits_t, *matrix,
      back, inputs)
    return power, charge, dyn_dual, feeder_dual.reshape(1, feeds * blk)


def solution(mesh):
    split = P("tm", "bat")
    steps = P(("tm", "bat"), None)
    return jax.shard_map(
        shards,
        mesh=mesh,
        in_specs=(split, split, split, steps, split, split, P("bat"), P("bat"), P(), P(), P(), P()),
        out_specs=(split, split, split, steps),
        check_vma=False,
    )
```

time: 176 us -> 170 us (0.966)
  blocking collectives: 39.2 us -> 110 us
  starting transfers between devices: 78.5 us -> 37.4 us
  local copies, waits for them, and re-layouts: 22.8 us -> 2.36 us
  waiting for transfers between devices: 15.8 us -> 0.02 us
  other arithmetic: 0.08 us -> 2.52 us
    all_to_all x3 -> x7, blocking collectives: 39.2 us -> 110 us  [exchange(): return lax.all_to_all(value, axis, 0, 0, tiled=True)]
    all_to_all x4 -> x0, starting transfers between devices: 45.8 us -> none  [exchange(): return lax.all_to_all(value, axis, 0, 0, tiled=True)]
    unnamed x36 -> x5, local copies, waits for them, and re-layouts: 18.1 us -> 2.34 us
    all_to_all x4 -> x0, waiting for transfers between devices: 10.9 us -> none  [exchange(): return lax.all_to_all(value, axis, 0, 0, tiled=True)]
    ppermute x8, waiting for transfers between devices: 4.89 us -> 0.02 us  [moved_to(): lax.ppermute(value, axis, [(i, i + distance) for i in range(count) if 0 <...]
    ppermute x8, starting transfers between devices: 32.7 us -> 37.4 us  [moved_to(): lax.ppermute(value, axis, [(i, i + distance) for i in range(count) if 0 <...]
    pallas_call x3 -> x6, Pallas kernels: 6.35 us -> 2.34 us  [the longest x1 2.11 us: shards(): call(functools.partial(first_duals_kernel, dims), 'first_duals', [VMEM] +...]
    pallas_call x2 -> x3, Pallas kernels: 6.68 us -> 10.5 us  [shards(): call(functools.partial(feeder_kernel, dims), 'feeder', [VMEM] * 6 + matri...]
  transfers between devices with their start and end apart: 12 -> 8, of which waited for: 7 -> 0; matrix products, arithmetic and copies ran while one was open for 1% -> 1% of each run, Pallas kernels for 1% -> 7%
where the time goes in v2:
time: 170 us; the launch traced here: 169 us
  blocking collectives  110 us (65%)
  starting transfers between devices  37.4 us (22%)
  Pallas kernels  16.4 us (10%)
  other arithmetic  2.52 us (1%)
  local copies, waits for them, and re-layouts  2.36 us (1%)
    all_to_all x7, blocking collectives, exchange(): return lax.all_to_all(value, axis, 0, 0, tiled=True)  110 us
    ppermute x8, starting transfers between devices, moved_to(): lax.ppermute(value, axis, [(i, i + distance) for i in range(count) if 0 <...  37.4 us
    pallas_call x3, Pallas kernels, shards(): call(functools.partial(feeder_kernel, dims), 'feeder', [VMEM] * 6 + matri...  10.5 us
  transfers between devices with their start and end apart: 8, of which 0 were waited for; matrix products, arithmetic and copies ran while one was open for 1% of the time, Pallas kernels for 7%

profile of v2, /device:TPU:1, one launch (start us, length us, event | category | flops | bytes accessed | tf_op | source)
XLA Modules:
  0.0 169.5 jit_solution(2307901184557350928)
XLA Ops:
  0.7 0.9 select_select_fusion.inputs
  1.6 8.8 %collective-permute-start = (f32[1,384]{1,0:T(1,128)S(1)}, f32[1,384]{1,0:T(1,128)S(1)}, u32[]{:S(2)}, u32[]{:S(2)}) collective-permute-start(f32[1,384]{1,0:T(1,128)S(1)} %slice_bitcast_fusion), channel_id=1, source_target_pairs={{16,0},{32,16},{48,32},{64,48},{80,64},{96,80},{112,96},{128,112},... | collective-permute-start | bytes 4616 | tf_op jit(solution)/shard_map/ppermute | solution.py:257
  10.5 1.9 %collective-permute-start.1 = (f32[2,384]{1,0:T(2,128)S(1)}, f32[2,384]{1,0:T(2,128)S(1)}, u32[]{:S(2)}, u32[]{:S(2)}) collective-permute-start(f32[2,384]{1,0:T(2,128)S(1)} %bitcast.48), channel_id=1, source_target_pairs={{0,16},{16,32},{32,48},{48,64},{64,80},{80,96},{96,112},{112,128},... | collective-permute-start | bytes 9224 | tf_op jit(solution)/shard_map/ppermute | solution.py:257
  12.4 0.8 broadcast_select_fusion.duals
  13.2 0.7 pad_add_fusion.table
  13.9 2.3 %copy-done = f32[72,128,128]{2,1,0:T(8,128)S(1)} copy-done((f32[72,128,128]{2,1,0:T(8,128)S(1)}, f32[72,128,128]{2,1,0:T(8,128)}, u32[]{:S(2)}) %copy-start) | copy-done | bytes 4718616
  16.3 2.1 %first_duals.1 = (f32[48,128]{1,0:T(8,128)S(1)}, f32[128,128]{1,0:T(8,128)S(1)}, f32[128,128]{1,0:T(8,128)S(1)}) custom-call(f32[2,24,128]{2,1,0:T(8,128)S(1)} %broadcast_select_fusion.duals, f32[72,128,128]{2,1,0:T(8,128)S(1)} %copy-done, s32[97]{0:T(128)S(1)} %pad_add_fusion.table), custom_call_target="tpu_custom_call" | custom-call | flops 2359296 | bytes 4718592 | tf_op jit(solution)/shard_map/first_duals/pallas_call | solution.py:287
  18.4 0.2 slots.1
  18.6 11.1 %all_to_all.35 = f32[16,32,128]{2,1,0:T(8,128)S(1)} all-to-all(f32[16,32,128]{2,1,0:T(8,128)S(1)} %bitcast.34), channel_id=1, replica_groups=mesh['tm'=32,'bat'=16] {'bat'}, dimensions={0} | all-to-all | bytes 524288 | tf_op jit(solution)/shard_map/all_to_all | solution.py:261
  29.7 0.2 first_row.1
  29.9 1.9 %collective-permute-start.3 = (f32[48,128]{1,0:T(8,128)S(1)}, f32[48,128]{1,0:T(8,128)S(1)}, u32[]{:S(2)}, u32[]{:S(2)}) collective-permute-start(f32[48,128]{1,0:T(8,128)S(1)} %get-tuple-element.67.dyn), channel_id=1, source_target_pairs={{0,1},{1,2},{2,3},{3,4},{4,5},{5,6},{6,7},{7,8},{8,9},{9,10},{10,1... | collective-permute-start | bytes 73736 | tf_op jit(solution)/shard_map/ppermute | solution.py:257
  31.8 7.0 %collective-permute-start.2 = (f32[48,128]{1,0:T(8,128)S(1)}, f32[48,128]{1,0:T(8,128)S(1)}, u32[]{:S(2)}, u32[]{:S(2)}) collective-permute-start(f32[48,128]{1,0:T(8,128)S(1)} %get-tuple-element.67.dyn), channel_id=1, source_target_pairs={{1,0},{2,1},{3,2},{4,3},{5,4},{6,5},{7,6},{8,7},{9,8},{10,9},{11,1... | collective-permute-start | bytes 73736 | tf_op jit(solution)/shard_map/ppermute | solution.py:257
  38.8 3.5 %feeder.3 = (f32[48,128]{1,0:T(8,128)S(1)}, f32[128,128]{1,0:T(8,128)S(1)}, f32[1,128]{1,0:T(1,128)S(1)}) custom-call(f32[1,128]{1,0:T(1,128)S(1)} %get-tuple-element.60.weight.weight_in, f32[48,128]{1,0:T(8,128)S(1)} %get-tuple-element.61.bar, f32[1,128]{1,0:T(1,128)S(1)} %get-tuple-element.62.primal, f32[1,128]{1,0:T(1,128)S(1)} %get-tuple-element.63.dual, ...), custom_call_target="tpu_custom_call" | custom-call | flops 4718592 | bytes 4718592 | tf_op jit(solution)/shard_map/feeder/pallas_call | solution.py:305
  42.3 0.0 collective-permute-done.3.dyn_prev
  42.3 0.0 collective-permute-done.2.dyn_next
  42.3 13.1 %all_to_all.36 = f32[16,1,128]{2,1,0:T(1,128)S(1)} all-to-all(f32[16,1,128]{2,1,0:T(1,128)S(1)} %broadcast_in_dim.56), channel_id=1, replica_groups=mesh['tm'=32,'bat'=16] {'bat'}, dimensions={0} | all-to-all | bytes 16384 | tf_op jit(solution)/shard_map/all_to_all | solution.py:261
  55.4 26.9 %all_to_all.37 = f32[32,1,128]{2,1,0:T(1,128)S(1)} all-to-all(f32[32,1,128]{2,1,0:T(1,128)S(1)} %bitcast.39), channel_id=1, replica_groups=mesh['tm'=32,'bat'=16] {'tm'}, dimensions={0} | all-to-all | bytes 32768 | tf_op jit(solution)/shard_map/all_to_all | solution.py:261
  82.3 0.3 row.2
  82.7 2.2 %collective-permute-start.5 = (f32[48,128]{1,0:T(8,128)S(1)}, f32[48,128]{1,0:T(8,128)S(1)}, u32[]{:S(2)}, u32[]{:S(2)}) collective-permute-start(f32[48,128]{1,0:T(8,128)S(1)} %get-tuple-element.81.dyn), channel_id=1, source_target_pairs={{0,1},{1,2},{2,3},{3,4},{4,5},{5,6},{6,7},{7,8},{8,9},{9,10},{10,1... | collective-permute-start | bytes 73736 | tf_op jit(solution)/shard_map/ppermute | solution.py:257
  84.9 6.7 %collective-permute-start.4 = (f32[48,128]{1,0:T(8,128)S(1)}, f32[48,128]{1,0:T(8,128)S(1)}, u32[]{:S(2)}, u32[]{:S(2)}) collective-permute-start(f32[48,128]{1,0:T(8,128)S(1)} %get-tuple-element.81.dyn), channel_id=1, source_target_pairs={{1,0},{2,1},{3,2},{4,3},{5,4},{6,5},{7,6},{8,7},{9,8},{10,9},{11,1... | collective-permute-start | bytes 73736 | tf_op jit(solution)/shard_map/ppermute | solution.py:257
  91.6 3.5 %feeder.4 = (f32[48,128]{1,0:T(8,128)S(1)}, f32[128,128]{1,0:T(8,128)S(1)}, f32[1,128]{1,0:T(1,128)S(1)}) custom-call(f32[1,128]{1,0:T(1,128)S(1)} %get-tuple-element.75.weight.weight_in, f32[48,128]{1,0:T(8,128)S(1)} %get-tuple-element.76.bar, f32[1,128]{1,0:T(1,128)S(1)} %get-tuple-element.77.primal, f32[1,128]{1,0:T(1,128)S(1)} %get-tuple-element.78.dual, ...), custom_call_target="tpu_custom_call" | custom-call | flops 4718592 | bytes 4718592 | tf_op jit(solution)/shard_map/feeder/pallas_call | solution.py:305
  95.1 0.0 collective-permute-done.4.dyn_next
  95.1 12.0 %all_to_all.38 = f32[16,1,128]{2,1,0:T(1,128)S(1)} all-to-all(f32[16,1,128]{2,1,0:T(1,128)S(1)} %broadcast_in_dim.58), channel_id=1, replica_groups=mesh['tm'=32,'bat'=16] {'bat'}, dimensions={0} | all-to-all | bytes 16384 | tf_op jit(solution)/shard_map/all_to_all | solution.py:261
  107.1 17.0 %all_to_all.39 = f32[32,1,128]{2,1,0:T(1,128)S(1)} all-to-all(f32[32,1,128]{2,1,0:T(1,128)S(1)} %bitcast.40), channel_id=1, replica_groups=mesh['tm'=32,'bat'=16] {'tm'}, dimensions={0} | all-to-all | bytes 32768 | tf_op jit(solution)/shard_map/all_to_all | solution.py:261
  124.1 0.3 row.3
  124.4 2.2 %collective-permute-start.7 = (f32[48,128]{1,0:T(8,128)S(1)}, f32[48,128]{1,0:T(8,128)S(1)}, u32[]{:S(2)}, u32[]{:S(2)}) collective-permute-start(f32[48,128]{1,0:T(8,128)S(1)} %get-tuple-element.95.rest_2_.dyn), channel_id=1, source_target_pairs={{0,1},{1,2},{2,3},{3,4},{4,5},{5,6},{6,7},{7,8},{8,9},{9,10},{10,1... | collective-permute-start | bytes 73736 | tf_op jit(solution)/shard_map/ppermute | solution.py:257
  126.6 6.7 %collective-permute-start.6 = (f32[48,128]{1,0:T(8,128)S(1)}, f32[48,128]{1,0:T(8,128)S(1)}, u32[]{:S(2)}, u32[]{:S(2)}) collective-permute-start(f32[48,128]{1,0:T(8,128)S(1)} %get-tuple-element.95.rest_2_.dyn), channel_id=1, source_target_pairs={{1,0},{2,1},{3,2},{4,3},{5,4},{6,5},{7,6},{8,7},{9,8},{10,9},{11,1... | collective-permute-start | bytes 73736 | tf_op jit(solution)/shard_map/ppermute | solution.py:257
  133.3 3.5 %feeder.5 = (f32[48,128]{1,0:T(8,128)S(1)}, f32[128,128]{1,0:T(8,128)S(1)}, f32[1,128]{1,0:T(1,128)S(1)}) custom-call(f32[1,128]{1,0:T(1,128)S(1)} %get-tuple-element.89.weight.weight_in, f32[48,128]{1,0:T(8,128)S(1)} %get-tuple-element.90.bar, f32[1,128]{1,0:T(1,128)S(1)} %get-tuple-element.91.primal, f32[1,128]{1,0:T(1,128)S(1)} %get-tuple-element.92.dual, ...), custom_call_target="tpu_custom_call" | custom-call | flops 4718592 | bytes 4718592 | tf_op jit(solution)/shard_map/feeder/pallas_call | solution.py:305
  136.8 0.0 collective-permute-done.6.rest_3_
  136.9 13.3 %all_to_all.40 = f32[16,24,128]{2,1,0:T(8,128)S(1)} all-to-all(f32[16,24,128]{2,1,0:T(8,128)S(1)} %bitcast.35), channel_id=1, replica_groups=mesh['tm'=32,'bat'=16] {'bat'}, dimensions={0} | all-to-all | bytes 393216 | tf_op jit(solution)/shard_map/all_to_all | solution.py:261
  150.2 16.5 %all_to_all.41 = f32[32,1,128]{2,1,0:T(1,128)S(1)} all-to-all(f32[32,1,128]{2,1,0:T(1,128)S(1)} %bitcast.41), channel_id=1, replica_groups=mesh['tm'=32,'bat'=16] {'tm'}, dimensions={0} | all-to-all | bytes 32768 | tf_op jit(solution)/shard_map/all_to_all | solution.py:261
  166.7 2.8 %last.1 = (f32[16,384]{1,0:T(8,128)}, f32[16,384]{1,0:T(8,128)}, f32[16,384]{1,0:T(8,128)}, f32[24,128]{1,0:T(8,128)}) custom-call(f32[512,128]{1,0:T(8,128)S(1)} %bitcast.31, f32[32,128]{1,0:T(8,128)S(1)} %bitcast.36, f32[1,128]{1,0:T(1,128)S(1)} %get-tuple-element.89.weight.weight_in, f32[48,128]{1,0:T(8,128)S(1)} %get-tuple-element.97.rest_0_.power, ...), custom_call_target="tpu_custom_call" | custom-call | flops 2359296 | bytes 4718592 | tf_op jit(solution)/shard_map/last/pallas_call | solution.py:327
  (20 shorter events, 0.1 us)
Async XLA Ops:
  1.6 16.8 %collective-permute-start = (f32[1,384]{1,0:T(1,128)S(1)}, f32[1,384]{1,0:T(1,128)S(1)}, u32[]{:S(2)}, u32[]{:S(2)}) collective-permute-start(f32[1,384]{1,0:T(1,128)S(1)} %slice_bitcast_fusion), channel_id=1, source_target_pairs={{16,0},{32,16},{48,32},{64,48},{80,64},{96,80},{112,96},{128,112},... | collective-permute-start | bytes 4616 | tf_op jit(solution)/shard_map/ppermute | solution.py:257
  10.5 8.0 %collective-permute-start.1 = (f32[2,384]{1,0:T(2,128)S(1)}, f32[2,384]{1,0:T(2,128)S(1)}, u32[]{:S(2)}, u32[]{:S(2)}) collective-permute-start(f32[2,384]{1,0:T(2,128)S(1)} %bitcast.48), channel_id=1, source_target_pairs={{0,16},{16,32},{32,48},{48,64},{64,80},{80,96},{96,112},{112,128},... | collective-permute-start | bytes 9224 | tf_op jit(solution)/shard_map/ppermute | solution.py:257
  13.9 2.3 %copy-start = (f32[72,128,128]{2,1,0:T(8,128)S(1)}, f32[72,128,128]{2,1,0:T(8,128)}, u32[]{:S(2)}) copy-start(f32[72,128,128]{2,1,0:T(8,128)} %values.9) | copy-start | bytes 14155780
  16.3 22.5 %copy-start.1 = (f32[72,128,128]{2,1,0:T(8,128)S(1)}, f32[72,128,128]{2,1,0:T(8,128)}, u32[]{:S(2)}) copy-start(f32[72,128,128]{2,1,0:T(8,128)} %values.9) | copy-start | bytes 14155780
  29.9 12.4 %collective-permute-start.3 = (f32[48,128]{1,0:T(8,128)S(1)}, f32[48,128]{1,0:T(8,128)S(1)}, u32[]{:S(2)}, u32[]{:S(2)}) collective-permute-start(f32[48,128]{1,0:T(8,128)S(1)} %get-tuple-element.67.dyn), channel_id=1, source_target_pairs={{0,1},{1,2},{2,3},{3,4},{4,5},{5,6},{6,7},{7,8},{8,9},{9,10},{10,1... | collective-permute-start | bytes 73736 | tf_op jit(solution)/shard_map/ppermute | solution.py:257
  31.8 10.5 %collective-permute-start.2 = (f32[48,128]{1,0:T(8,128)S(1)}, f32[48,128]{1,0:T(8,128)S(1)}, u32[]{:S(2)}, u32[]{:S(2)}) collective-permute-start(f32[48,128]{1,0:T(8,128)S(1)} %get-tuple-element.67.dyn), channel_id=1, source_target_pairs={{1,0},{2,1},{3,2},{4,3},{5,4},{6,5},{7,6},{8,7},{9,8},{10,9},{11,1... | collective-permute-start | bytes 73736 | tf_op jit(solution)/shard_map/ppermute | solution.py:257
  82.7 12.4 %collective-permute-start.5 = (f32[48,128]{1,0:T(8,128)S(1)}, f32[48,128]{1,0:T(8,128)S(1)}, u32[]{:S(2)}, u32[]{:S(2)}) collective-permute-start(f32[48,128]{1,0:T(8,128)S(1)} %get-tuple-element.81.dyn), channel_id=1, source_target_pairs={{0,1},{1,2},{2,3},{3,4},{4,5},{5,6},{6,7},{7,8},{8,9},{9,10},{10,1... | collective-permute-start | bytes 73736 | tf_op jit(solution)/shard_map/ppermute | solution.py:257
  84.9 10.2 %collective-permute-start.4 = (f32[48,128]{1,0:T(8,128)S(1)}, f32[48,128]{1,0:T(8,128)S(1)}, u32[]{:S(2)}, u32[]{:S(2)}) collective-permute-start(f32[48,128]{1,0:T(8,128)S(1)} %get-tuple-element.81.dyn), channel_id=1, source_target_pairs={{1,0},{2,1},{3,2},{4,3},{5,4},{6,5},{7,6},{8,7},{9,8},{10,9},{11,1... | collective-permute-start | bytes 73736 | tf_op jit(solution)/shard_map/ppermute | solution.py:257
  124.4 12.4 %collective-permute-start.7 = (f32[48,128]{1,0:T(8,128)S(1)}, f32[48,128]{1,0:T(8,128)S(1)}, u32[]{:S(2)}, u32[]{:S(2)}) collective-permute-start(f32[48,128]{1,0:T(8,128)S(1)} %get-tuple-element.95.rest_2_.dyn), channel_id=1, source_target_pairs={{0,1},{1,2},{2,3},{3,4},{4,5},{5,6},{6,7},{7,8},{8,9},{9,10},{10,1... | collective-permute-start | bytes 73736 | tf_op jit(solution)/shard_map/ppermute | solution.py:257
  126.6 10.2 %collective-permute-start.6 = (f32[48,128]{1,0:T(8,128)S(1)}, f32[48,128]{1,0:T(8,128)S(1)}, u32[]{:S(2)}, u32[]{:S(2)}) collective-permute-start(f32[48,128]{1,0:T(8,128)S(1)} %get-tuple-element.95.rest_2_.dyn), channel_id=1, source_target_pairs={{1,0},{2,1},{3,2},{4,3},{5,4},{6,5},{7,6},{8,7},{9,8},{10,9},{11,1... | collective-permute-start | bytes 73736 | tf_op jit(solution)/shard_map/ppermute | solution.py:257

commit v3 on v2

v3 whole, which is shorter than its diff:
```python
import functools

import jax
import jax.numpy as jnp
from jax import lax
from jax.experimental import pallas as pl
from jax.experimental.pallas import tpu as pltpu
from jax.sharding import PartitionSpec as P

ITERS = 4
ETA_STEP = 0.4
EPS_NORM = 1e-06
LANES = 128
HALF = LANES // 2
F32 = jnp.float32

VMEM = pl.BlockSpec(memory_space=pltpu.VMEM)
SMEM = pl.BlockSpec(memory_space=pltpu.SMEM)

POWER, CHARGE, DYN, PRICE, INFLOW, LIMIT, CAPACITY = range(7)
SLOT_DYN, SLOT_PUSHED, SLOT_POWER, SLOT_PRICE, SLOT_LIMIT = range(5)


def rows_up(count):
    return -(-count // 8) * 8


def lane_iota(shape):
    return lax.broadcasted_iota(jnp.int32, shape, len(shape) - 1)


def clip(value, low, high):
    return jnp.minimum(jnp.maximum(value, low), high)


def total(value):
    return jnp.sum(jnp.sum(value, axis=0, keepdims=True), axis=1, keepdims=True)


def take_row(ref, array, pieces, groups, slot_rows):
    parts = [ref[pl.ds(array * pieces + i, groups, stride=slot_rows), :] for i in range(pieces)]
    return jnp.concatenate(parts, axis=0)


def put_row(ref, array, value, pieces, groups, slot_rows):
    for i in range(pieces):
        ref[pl.ds(array * pieces + i, groups, stride=slot_rows), :] = value[i * groups : (i + 1) * groups]


def row_of_block(block, pieces, groups):
    return (block % pieces) * groups + block // pieces


def feeder_adjoint(values, table, duals_t, spread, sums, pieces, groups):
    blocks, blk = values.shape[:2]
    for f in range(spread.shape[0]):
        spread[f] = jnp.broadcast_to(duals_t[:, f : f + 1], spread.shape[1:])
    sums[...] = jnp.zeros_like(sums)

    def step(j, f):
        f = jnp.where(j == table[blocks + f + 1], f + 1, f)
        product = values[j] * spread[f]
        c = row_of_block(table[j], pieces, groups)
        sums[c] = sums[c] + jnp.sum(product.reshape(blk // 8, 8, LANES), axis=0)
        return f

    lax.fori_loop(0, blocks, step, 0, unroll=4)
    return jnp.sum(sums[...], axis=1)


def feeder_apply(values, table, field, sums, pieces, groups):
    blocks, blk = values.shape[:2]

    def step(j, carry):
        f, acc = carry
        fresh = j == table[blocks + f + 1]
        f = jnp.where(fresh, f + 1, f)
        keep = jnp.where(fresh, 0.0, 1.0).astype(F32)
        c = row_of_block(table[j], pieces, groups)
        acc = acc * keep + values[j] * field[pl.ds(c, 1), :]
        sums[f] = acc
        return f, acc

    lax.fori_loop(0, blocks, step, (0, jnp.zeros((blk, LANES), F32)), unroll=4)
    lane = lane_iota((blk, LANES))
    out = jnp.zeros((blk, LANES), F32)
    for f in range(sums.shape[0]):
        out = jnp.where(lane == f, jnp.sum(sums[f], axis=1, keepdims=True), out)
    return out


def pack_sums(primal, dual):
    lane = lane_iota(primal.shape)
    return jnp.where(
        lane < HALF, primal + pltpu.roll(primal, HALF, 1), dual + pltpu.roll(dual, HALF, 1)
    )


def next_weight(weight, parts):
    both = jnp.sum(parts, axis=0, keepdims=True)
    lane = lane_iota(both.shape)
    primal_sq = total(jnp.where(lane < HALF, both, 0.0))
    dual_sq = total(jnp.where(lane < HALF, 0.0, both))
    ratio = jnp.sqrt((dual_sq + EPS_NORM) / (primal_sq + EPS_NORM))
    return jnp.broadcast_to(jnp.sqrt(weight[:, :1] * ratio), (1, LANES))


def row_sum(value):
    return jnp.sum(value, axis=0, keepdims=True)


def first_kernel(dims, first_rows, duals, inputs, values, table, slots, duals_t, limits_t, pushed_out, spread, sums):
    pieces, groups = dims
    blk = values.shape[1]
    feeds = duals.shape[1]
    for i, target in enumerate((duals_t, limits_t)):
        padded = jnp.concatenate([duals[i], jnp.zeros((blk - feeds, LANES), F32)], axis=0)
        target[...] = jnp.transpose(padded)
    sent = ((SLOT_DYN, DYN), (SLOT_POWER, POWER), (SLOT_PRICE, PRICE), (SLOT_LIMIT, LIMIT))
    for i in range(pieces):
        for slot, array in sent:
            slots[pl.ds(slot * pieces + i, groups, stride=first_rows), :] = inputs[array, :, i * LANES : (i + 1) * LANES]
    pushed = feeder_adjoint(values, table, duals_t[...], spread, sums, pieces, groups)
    pushed_out[...] = pushed
    put_row(slots, SLOT_PUSHED, pushed, pieces, groups, first_rows)


def local_step(dims, slot_rows, weight, received, inputs, state, edges, state_out, edge_out):
    pieces, groups = dims
    step_primal = ETA_STEP / weight[:, :1]
    step_dual = ETA_STEP * weight[:, :1]
    after, before_dyn, before_charge = edges
    begin = lax.axis_index("tm") == 0
    line = lax.broadcasted_iota(jnp.int32, (groups, LANES), 0)
    primal = jnp.zeros((1, LANES), F32)
    dual = jnp.zeros((1, LANES), F32)
    for i in range(pieces):
        cut = slice(i * LANES, (i + 1) * LANES)
        power, charge, dyn = (read(cut) for read in state)
        price, inflow, limit, capacity = (inputs[array, :, cut] for array in (PRICE, INFLOW, LIMIT, CAPACITY))
        pushed = received[pl.ds(SLOT_PUSHED * pieces + i, groups, stride=slot_rows), :]
        power_new = clip(power - step_primal * (price - dyn + pushed), -limit, limit)
        dyn_next = jnp.where(line == groups - 1, after(i), pltpu.roll(dyn, groups - 1, 0))
        charge_new = clip(charge - step_primal * (dyn - dyn_next), 0.0, capacity)
        power_bar = 2.0 * power_new - power
        charge_bar = 2.0 * charge_new - charge
        edge_charge = before_charge(i)
        edge_new = clip(edge_charge - step_primal * (before_dyn(i) - dyn[:1]), 0.0, capacity[:1])
        edge_bar = jnp.where(begin, 0.0, 2.0 * edge_new - edge_charge)
        prev_bar = jnp.where(line == 0, edge_bar, pltpu.roll(charge_bar, 1, 0))
        dyn_new = dyn + step_dual * (charge_bar - prev_bar - power_bar - inflow)
        for ref, value in zip(state_out, (power_new, charge_new, dyn_new)):
            ref[:, cut] = value
        if edge_out is not None:
            edge_out[:, cut] = edge_new
        primal = primal + row_sum((power_new - power) ** 2 + (charge_new - charge) ** 2)
        dual = dual + row_sum((dyn_new - dyn) ** 2)
    return primal, dual


def feeder_step(weight, coupled, duals_t, limits_t):
    step_dual = ETA_STEP * weight[:, :1]
    return jnp.maximum(0.0, duals_t + step_dual * (coupled - limits_t))


def row_power(dims, first_rows, weight, first, power, dyn, pushed, bar):
    pieces, groups = dims
    step_primal = ETA_STEP / weight[:, :1]
    price = take_row(first, SLOT_PRICE, pieces, groups, first_rows)
    limit = take_row(first, SLOT_LIMIT, pieces, groups, first_rows)
    new = clip(power - step_primal * (price - dyn + pushed), -limit, limit)
    bar[...] = 2.0 * new - power
    return new


def feeder_part(dims, slot_rows, weight, primal, dual, bar, dyn, duals_t, limits_t, values, table,
                duals_out, pushed_out, slots, spread, sums):
    pieces, groups = dims
    coupled = feeder_apply(values, table, bar, spread, pieces, groups)
    new = feeder_step(weight, coupled, duals_t[...], limits_t[...])
    duals_out[...] = new
    parts = pack_sums(primal, dual + row_sum((new - duals_t[...]) ** 2))
    slots[pl.ds(2 * pieces, groups, stride=slot_rows), :] = jnp.broadcast_to(parts, (groups, LANES))
    for i in range(pieces):
        slots[pl.ds(SLOT_DYN * pieces + i, groups, stride=slot_rows), :] = dyn[:, i * LANES : (i + 1) * LANES]
    pushed = feeder_adjoint(values, table, new, spread, sums, pieces, groups)
    pushed_out[...] = pushed
    put_row(slots, SLOT_PUSHED, pushed, pieces, groups, slot_rows)


def step_one_kernel(dims, first_rows, slot_rows, first, after, before, pushed_row, inputs, duals_t, limits_t, values,
                    table, weight, power_row, power_out, charge_out, dyn_out, edge_out, duals_out, pushed_out, slots,
                    bar, spread, sums):
    pieces, groups = dims
    weight[...] = jnp.ones_like(weight)
    state = [lambda cut, array=array: inputs[array, :, cut] for array in (POWER, CHARGE, DYN)]
    edges = [lambda i, ref=ref, k=k: ref[k : k + 1, i * LANES : (i + 1) * LANES]
             for ref, k in ((after, 0), (before, 1), (before, 0))]
    primal, dual = local_step(dims, first_rows, weight[...], first, inputs, state, edges,
                              (power_out, charge_out, dyn_out), edge_out)
    power_row[...] = row_power(dims, first_rows, weight[...], first,
                               take_row(first, SLOT_POWER, pieces, groups, first_rows),
                               take_row(first, SLOT_DYN, pieces, groups, first_rows), pushed_row[...], bar)
    feeder_part(dims, slot_rows, weight[...], primal, dual, bar, dyn_out, duals_t, limits_t, values, table,
                duals_out, pushed_out, slots, spread, sums)


def later_edges(parts, edge_in):
    steps = lax.axis_size("tm")
    here = lax.axis_index("tm")
    lines = parts.shape[0] // steps
    above, below = jnp.minimum(here + 1, steps - 1), jnp.maximum(here - 1, 0)
    after = lambda i: jnp.where(here == steps - 1, 0.0, parts[pl.ds(above * lines + 1 + i, 1), :])
    before_dyn = lambda i: parts[pl.ds(below * lines + 1 + i, 1), :]
    before_charge = lambda i: edge_in[:, i * LANES : (i + 1) * LANES]
    return after, before_dyn, before_charge


def later_weight(weight_in, parts):
    steps = lax.axis_size("tm")
    return next_weight(weight_in[...], parts[pl.ds(0, steps, stride=parts.shape[0] // steps), :])


def step_kernel(dims, first_rows, slot_rows, first, received, parts, weight_in, row_in, power, charge, dyn, edge_in,
                pushed_row, inputs, duals_t, limits_t, values, table, weight, power_row, power_out, charge_out,
                dyn_out, edge_out, duals_out, pushed_out, slots, bar, spread, sums):
    weight[...] = later_weight(weight_in, parts)
    state = [lambda cut, ref=ref: ref[:, cut] for ref in (power, charge, dyn)]
    primal, dual = local_step(dims, slot_rows, weight[...], received, inputs, state, later_edges(parts, edge_in),
                              (power_out, charge_out, dyn_out), edge_out)
    power_row[...] = row_power(dims, first_rows, weight[...], first, row_in[...],
                               take_row(received, SLOT_DYN, *dims, slot_rows), pushed_row[...], bar)
    feeder_part(dims, slot_rows, weight[...], primal, dual, bar, dyn_out, duals_t, limits_t, values, table,
                duals_out, pushed_out, slots, spread, sums)


def last_kernel(dims, first_rows, slot_rows, first, received, parts, weight_in, row_in, power, charge, dyn, edge_in,
                pushed_row, inputs, duals_t, limits_t, values, table, power_out, charge_out, dyn_out, duals_out,
                bar, spread):
    weight = later_weight(weight_in, parts)
    state = [lambda cut, ref=ref: ref[:, cut] for ref in (power, charge, dyn)]
    local_step(dims, slot_rows, weight, received, inputs, state, later_edges(parts, edge_in),
               (power_out, charge_out, dyn_out), None)
    row_power(dims, first_rows, weight, first, row_in[...], take_row(received, SLOT_DYN, *dims, slot_rows),
              pushed_row[...], bar)
    coupled = feeder_apply(values, table, bar, spread, *dims)
    new = feeder_step(weight, coupled, duals_t[...], limits_t[...])
    duals_out[...] = jnp.transpose(new)[: duals_out.shape[0]]


def relay_kernel(dims, slot_rows, received, dyn, parts):
    pieces, groups = dims
    steps = lax.axis_size("tm")
    here = lax.axis_index("tm")
    lines = parts.shape[0] // steps
    parts[...] = jnp.zeros_like(parts)
    summed = row_sum(received[pl.ds(2 * pieces, groups, stride=slot_rows), :])
    parts[pl.ds(0, steps, stride=lines), :] = jnp.broadcast_to(summed, (steps, LANES))

    @pl.when(here > 0)
    def _():
        for i in range(pieces):
            parts[pl.ds((here - 1) * lines + 1 + i, 1), :] = dyn[:1, i * LANES : (i + 1) * LANES]

    @pl.when(here < steps - 1)
    def _():
        for i in range(pieces):
            parts[pl.ds((here + 1) * lines + 1 + i, 1), :] = dyn[groups - 1 :, i * LANES : (i + 1) * LANES]


def shapes(*dims):
    return [jax.ShapeDtypeStruct(dim, F32) for dim in dims]


def call(kernel, name, in_specs, out_dims, scratch=(), flops=0, moved=0):
    return pl.pallas_call(
        kernel,
        name=name,
        in_specs=in_specs,
        out_specs=[VMEM] * len(out_dims),
        out_shape=shapes(*out_dims),
        scratch_shapes=[pltpu.VMEM(dim, F32) for dim in scratch],
        compiler_params=pltpu.CompilerParams(vmem_limit_bytes=16 * 1024 * 1024),
        cost_estimate=pl.CostEstimate(flops=flops, bytes_accessed=moved, transcendentals=0),
    )


def stacked(*arrays):
    shape = (len(arrays),) + arrays[0].shape
    index = lax.broadcasted_iota(jnp.int32, shape, 0)
    out = jnp.broadcast_to(arrays[-1], shape)
    for i, array in enumerate(arrays[:-1]):
        out = jnp.where(index == i, array, out)
    return out


def moved_to(value, axis, distance):
    count = lax.axis_size(axis)
    return lax.ppermute(value, axis, [(i, i + distance) for i in range(count) if 0 <= i + distance < count])


def exchange(value, axis):
    return lax.all_to_all(value, axis, 0, 0, tiled=True)


def shards(power0, charge0, dyn_dual0, feeder_dual0, price, inflow, power_limit, capacity, feeder_limit,
           block_values, block_cols, block_offsets):
    groups, local = power0.shape
    pieces = local // LANES
    blocks, blk = block_values.shape[:2]
    feeds = block_offsets.shape[0] - 1
    steps = lax.axis_size("tm")
    first_rows, slot_rows, lines = rows_up(5 * pieces), rows_up(2 * pieces + 1), 1 + pieces
    dims = (pieces, groups)
    row, line, square, own = (pieces * groups, LANES), (1, LANES), (blk, LANES), (groups, local)
    spread, sums = (feeds, blk, LANES), (pieces * groups, 8, LANES)
    matrix_specs = [VMEM, SMEM]
    work, moved = 2 * blocks * blk * LANES, 4 * blocks * blk * LANES

    inputs = stacked(power0, charge0, dyn_dual0, price, inflow, power_limit, capacity)
    duals = stacked(feeder_dual0.reshape(feeds, blk), feeder_limit.reshape(feeds, blk))
    matrix = (block_values, jnp.concatenate([block_cols, block_offsets]))

    after = moved_to(inputs[DYN, :1], "tm", -1)
    before = moved_to(inputs[CHARGE : DYN + 1, -1], "tm", 1)
    first, duals_t, limits_t, pushed = call(
        functools.partial(first_kernel, dims, first_rows), "first",
        [VMEM] * 2 + matrix_specs, [(groups * first_rows, LANES), square, square, row], [spread, sums], work, moved,
    )(duals, inputs, *matrix)
    first, after, before = lax.optimization_barrier((first, after, before))
    first = exchange(first.reshape(groups, first_rows, LANES), "bat").reshape(groups * first_rows, LANES)

    step_outs = [line, row] + [own] * 3 + [(1, local), square, row, (groups * slot_rows, LANES)]
    scratch = [row, spread, sums]
    for iteration in range(ITERS):
        last = iteration + 1 == ITERS
        outs = [own] * 3 + [(feeds, blk)] if last else step_outs
        sizes = (dims, first_rows, slot_rows)
        if iteration == 0:
            results = call(
                functools.partial(step_one_kernel, *sizes), "step_one", [VMEM] * 7 + matrix_specs, outs, scratch,
                2 * work, moved,
            )(first, after, before, pushed, inputs, duals_t, limits_t, *matrix)
        else:
            results = call(
                functools.partial(last_kernel if last else step_kernel, *sizes), "last" if last else "step",
                [VMEM] * 13 + matrix_specs, outs, scratch[:2] if last else scratch, 2 * work, moved,
            )(first, received, parts, weight, power_row, power, charge, dyn, edge, pushed, inputs, duals_t, limits_t,
              *matrix)
        if not last:
            weight, power_row, power, charge, dyn, edge, duals_t, pushed, slots = results
            received = exchange(slots.reshape(groups, slot_rows, LANES), "bat").reshape(groups * slot_rows, LANES)
            parts = call(
                functools.partial(relay_kernel, dims, slot_rows), "relay", [VMEM] * 2, [(steps * lines, LANES)]
            )(received, dyn)[0]
            parts = exchange(parts.reshape(steps, lines, LANES), "tm").reshape(steps * lines, LANES)
    power, charge, dyn_dual, feeder_dual = results
    return power, charge, dyn_dual, feeder_dual.reshape(1, feeds * blk)


def solution(mesh):
    split = P("tm", "bat")
    steps = P(("tm", "bat"), None)
    return jax.shard_map(
        shards,
        mesh=mesh,
        in_specs=(split, split, split, steps, split, split, P("bat"), P("bat"), P(), P(), P(), P()),
        out_specs=(split, split, split, steps),
        check_vma=False,
    )
```

time: 170 us -> 138 us (0.81)
  starting transfers between devices: 37.4 us -> 10.7 us
  blocking collectives: 110 us -> 106 us
    ppermute x8 -> x2, starting transfers between devices: 37.4 us -> 10.7 us  [moved_to(): lax.ppermute(value, axis, [(i, i + distance) for i in range(count) if 0 <...]
    all_to_all x7, blocking collectives: 110 us -> 106 us  [exchange(): return lax.all_to_all(value, axis, 0, 0, tiled=True)]
    pallas_call x13 -> x8, Pallas kernels: 16.4 us -> 16 us  [the longest x3 10.3 us: shards(): call(functools.partial(last_kernel if last else step_kernel, *sizes), 'la...]
  transfers between devices with their start and end apart: 8 -> 2, of which waited for: 0 -> 0; matrix products, arithmetic and copies ran while one was open for 1% -> 1% of each run, Pallas kernels for 7% -> 1%
where the time goes in v3:
time: 138 us
  blocking collectives  106 us (77%)
  Pallas kernels  16 us (12%)
  starting transfers between devices  10.7 us (8%)
  other arithmetic  2.52 us (2%)
  local copies, waits for them, and re-layouts  2.35 us (2%)
    all_to_all x7, blocking collectives, exchange(): return lax.all_to_all(value, axis, 0, 0, tiled=True)  106 us
    ppermute x2, starting transfers between devices, moved_to(): lax.ppermute(value, axis, [(i, i + distance) for i in range(count) if 0 <...  10.7 us
    pallas_call x3, Pallas kernels, shards(): call(functools.partial(last_kernel if last else step_kernel, *sizes), 'la...  10.3 us
    pallas_call x1, Pallas kernels, shards(): call(functools.partial(step_one_kernel, *sizes), 'step_one', [VMEM] * 7 +...  3.59 us
  transfers between devices with their start and end apart: 2, of which 0 were waited for; matrix products, arithmetic and copies ran while one was open for 1% of the time, Pallas kernels for 1%

profile of v3, /device:TPU:1, one launch (start us, length us, event | category | flops | bytes accessed | tf_op | source)
XLA Modules:
  0.0 137.9 jit_solution(14908569691704240113)
XLA Ops:
  0.7 0.9 select_select_fusion.inputs
  1.6 8.8 %collective-permute-start = (f32[1,384]{1,0:T(1,128)S(1)}, f32[1,384]{1,0:T(1,128)S(1)}, u32[]{:S(2)}, u32[]{:S(2)}) collective-permute-start(f32[1,384]{1,0:T(1,128)S(1)} %slice_bitcast_fusion), channel_id=1, source_target_pairs={{16,0},{32,16},{48,32},{64,48},{80,64},{96,80},{112,96},{128,112},... | collective-permute-start | bytes 4616 | tf_op jit(solution)/shard_map/ppermute | solution.py:299
  10.5 1.9 %collective-permute-start.1 = (f32[2,384]{1,0:T(2,128)S(1)}, f32[2,384]{1,0:T(2,128)S(1)}, u32[]{:S(2)}, u32[]{:S(2)}) collective-permute-start(f32[2,384]{1,0:T(2,128)S(1)} %bitcast.44), channel_id=1, source_target_pairs={{0,16},{16,32},{32,48},{48,64},{64,80},{80,96},{96,112},{112,128},... | collective-permute-start | bytes 9224 | tf_op jit(solution)/shard_map/ppermute | solution.py:299
  12.4 0.8 broadcast_select_fusion.duals
  13.2 0.7 pad_add_fusion.table
  13.9 0.0 copy-start
  13.9 2.3 %copy-done = f32[72,128,128]{2,1,0:T(8,128)S(1)} copy-done((f32[72,128,128]{2,1,0:T(8,128)S(1)}, f32[72,128,128]{2,1,0:T(8,128)}, u32[]{:S(2)}) %copy-start) | copy-done | bytes 4718616
  16.3 0.0 copy-start.1
  16.3 2.0 %first.1 = (f32[256,128]{1,0:T(8,128)S(1)}, f32[128,128]{1,0:T(8,128)S(1)}, f32[128,128]{1,0:T(8,128)S(1)}, f32[48,128]{1,0:T(8,128)S(1)}) custom-call(f32[2,24,128]{2,1,0:T(8,128)S(1)} %broadcast_select_fusion.duals, f32[7,16,384]{2,1,0:T(8,128)S(1)} %select_select_fusion.inputs, f32[72,128,128]{2,1,0:T(8,128)S(1)} %copy-done, s32[97]{0:T(128)S(1)} %pad_add_fusion.table), custom_call_target="tpu_custom_call" | custom-call | flops 2359296 | bytes 4718592 | tf_op jit(solution)/shard_map/first/pallas_call | solution.py:326
  18.3 0.0 collective-permute-done.after
  18.3 0.0 collective-permute-done.1.before
  18.4 9.5 %all_to_all.35 = f32[16,16,128]{2,1,0:T(8,128)S(1)} all-to-all(f32[16,16,128]{2,1,0:T(8,128)S(1)} %bitcast.38), channel_id=1, replica_groups=mesh['tm'=32,'bat'=16] {'bat'}, dimensions={0} | all-to-all | bytes 262144 | tf_op jit(solution)/shard_map/all_to_all | solution.py:303
  27.9 0.0 copy-done.1
  27.9 3.6 %step_one.1 = (f32[1,128]{1,0:T(1,128)S(1)}, f32[48,128]{1,0:T(8,128)S(1)}, f32[16,384]{1,0:T(8,128)S(1)}, f32[16,384]{1,0:T(8,128)S(1)}, f32[16,384]{1,0:T(8,12...) custom-call(f32[256,128]{1,0:T(8,128)S(1)} %bitcast.22, ...), custom_call_target="tpu_custom_call" | custom-call | flops 4718592 | bytes 4718592 | tf_op jit(solution)/shard_map/step_one/pallas_call | solution.py:340
  31.5 9.6 %all_to_all.36 = f32[16,8,128]{2,1,0:T(8,128)S(1)} all-to-all(f32[16,8,128]{2,1,0:T(8,128)S(1)} %bitcast.41), channel_id=1, replica_groups=mesh['tm'=32,'bat'=16] {'bat'}, dimensions={0} | all-to-all | bytes 131072 | tf_op jit(solution)/shard_map/all_to_all | solution.py:303
  41.1 30.2 %all_to_all.37 = f32[32,4,128]{2,1,0:T(4,128)S(1)} all-to-all(f32[32,4,128]{2,1,0:T(4,128)S(1)} %bitcast.32), channel_id=1, replica_groups=mesh['tm'=32,'bat'=16] {'tm'}, dimensions={0} | all-to-all | bytes 131072 | tf_op jit(solution)/shard_map/all_to_all | solution.py:303
  71.3 3.8 %step.2 = (f32[1,128]{1,0:T(1,128)S(1)}, f32[48,128]{1,0:T(8,128)S(1)}, f32[16,384]{1,0:T(8,128)S(1)}, f32[16,384]{1,0:T(8,128)S(1)}, f32[16,384]{1,0:T(8,128)S(...) custom-call(f32[256,128]{1,0:T(8,128)S(1)} %bitcast.23, ...), custom_call_target="tpu_custom_call" | custom-call | flops 4718592 | bytes 4718592 | tf_op jit(solution)/shard_map/step/pallas_call | solution.py:345
  75.1 9.4 %all_to_all.38 = f32[16,8,128]{2,1,0:T(8,128)S(1)} all-to-all(f32[16,8,128]{2,1,0:T(8,128)S(1)} %bitcast.39), channel_id=1, replica_groups=mesh['tm'=32,'bat'=16] {'bat'}, dimensions={0} | all-to-all | bytes 131072 | tf_op jit(solution)/shard_map/all_to_all | solution.py:303
  84.5 18.7 %all_to_all.39 = f32[32,4,128]{2,1,0:T(4,128)S(1)} all-to-all(f32[32,4,128]{2,1,0:T(4,128)S(1)} %bitcast.33), channel_id=1, replica_groups=mesh['tm'=32,'bat'=16] {'tm'}, dimensions={0} | all-to-all | bytes 131072 | tf_op jit(solution)/shard_map/all_to_all | solution.py:303
  103.2 3.8 %step.3 = (f32[1,128]{1,0:T(1,128)S(1)}, f32[48,128]{1,0:T(8,128)S(1)}, f32[16,384]{1,0:T(8,128)S(1)}, f32[16,384]{1,0:T(8,128)S(1)}, f32[16,384]{1,0:T(8,128)S(...) custom-call(f32[256,128]{1,0:T(8,128)S(1)} %bitcast.24, ...), custom_call_target="tpu_custom_call" | custom-call | flops 4718592 | bytes 4718592 | tf_op jit(solution)/shard_map/step/pallas_call | solution.py:345
  107.0 9.4 %all_to_all.40 = f32[16,8,128]{2,1,0:T(8,128)S(1)} all-to-all(f32[16,8,128]{2,1,0:T(8,128)S(1)} %bitcast.40), channel_id=1, replica_groups=mesh['tm'=32,'bat'=16] {'bat'}, dimensions={0} | all-to-all | bytes 131072 | tf_op jit(solution)/shard_map/all_to_all | solution.py:303
  116.4 18.7 %all_to_all.41 = f32[32,4,128]{2,1,0:T(4,128)S(1)} all-to-all(f32[32,4,128]{2,1,0:T(4,128)S(1)} %bitcast.34), channel_id=1, replica_groups=mesh['tm'=32,'bat'=16] {'tm'}, dimensions={0} | all-to-all | bytes 131072 | tf_op jit(solution)/shard_map/all_to_all | solution.py:303
  135.1 2.8 %last.1 = (f32[16,384]{1,0:T(8,128)}, f32[16,384]{1,0:T(8,128)}, f32[16,384]{1,0:T(8,128)}, f32[24,128]{1,0:T(8,128)}) custom-call(f32[256,128]{1,0:T(8,128)S(1)} %bitcast.25, f32[128,128]{1,0:T(8,128)S(1)} %bitcast.31, f32[128,128]{1,0:T(8,128)S(1)} %bitcast.37, f32[1,128]{1,0:T(1,128)S(1)} %get-tuple-element.69.weight_in, ...), custom_call_target="tpu_custom_call" | custom-call | flops 4718592 | bytes 4718592 | tf_op jit(solution)/shard_map/last/pallas_call | solution.py:345
  (10 shorter events, 0.1 us)
Async XLA Ops:
  1.6 16.7 %collective-permute-start = (f32[1,384]{1,0:T(1,128)S(1)}, f32[1,384]{1,0:T(1,128)S(1)}, u32[]{:S(2)}, u32[]{:S(2)}) collective-permute-start(f32[1,384]{1,0:T(1,128)S(1)} %slice_bitcast_fusion), channel_id=1, source_target_pairs={{16,0},{32,16},{48,32},{64,48},{80,64},{96,80},{112,96},{128,112},... | collective-permute-start | bytes 4616 | tf_op jit(solution)/shard_map/ppermute | solution.py:299
  10.5 7.9 %collective-permute-start.1 = (f32[2,384]{1,0:T(2,128)S(1)}, f32[2,384]{1,0:T(2,128)S(1)}, u32[]{:S(2)}, u32[]{:S(2)}) collective-permute-start(f32[2,384]{1,0:T(2,128)S(1)} %bitcast.44), channel_id=1, source_target_pairs={{0,16},{16,32},{32,48},{48,64},{64,80},{80,96},{96,112},{112,128},... | collective-permute-start | bytes 9224 | tf_op jit(solution)/shard_map/ppermute | solution.py:299
  13.9 2.3 %copy-start = (f32[72,128,128]{2,1,0:T(8,128)S(1)}, f32[72,128,128]{2,1,0:T(8,128)}, u32[]{:S(2)}) copy-start(f32[72,128,128]{2,1,0:T(8,128)} %values.9) | copy-start | bytes 14155780
  16.3 11.6 %copy-start.1 = (f32[72,128,128]{2,1,0:T(8,128)S(1)}, f32[72,128,128]{2,1,0:T(8,128)}, u32[]{:S(2)}) copy-start(f32[72,128,128]{2,1,0:T(8,128)} %values.9) | copy-start | bytes 14155780

commit v4 on v3

--- a/solution.py
+++ b/solution.py
@@ -12,6 +12,11 @@
 EPS_NORM = 1e-06
 LANES = 128
 HALF = LANES // 2
+ADJOINT_UNROLL = 8
+ADJOINT_PARTS = 4
+APPLY_UNROLL = 8
+CHUNKS = 4
+STREAMING_LIMIT = 50 * 1024 * 1024
 F32 = jnp.float32
 
 VMEM = pl.BlockSpec(memory_space=pltpu.VMEM)
@@ -47,46 +52,67 @@
         ref[pl.ds(array * pieces + i, groups, stride=slot_rows), :] = value[i * groups : (i + 1) * groups]
 
 
-def row_of_block(block, pieces, groups):
-    return (block % pieces) * groups + block // pieces
-
-
-def feeder_adjoint(values, table, duals_t, spread, sums, pieces, groups):
+def unrolled(count, most):
+    return max(u for u in range(1, most + 1) if count % u == 0)
+
+
+def adjoint_loop(values, table, spread, sums, begin, end):
     blocks, blk = values.shape[:2]
-    for f in range(spread.shape[0]):
-        spread[f] = jnp.broadcast_to(duals_t[:, f : f + 1], spread.shape[1:])
-    sums[...] = jnp.zeros_like(sums)
-
-    def step(j, f):
-        f = jnp.where(j == table[blocks + f + 1], f + 1, f)
-        product = values[j] * spread[f]
-        c = row_of_block(table[j], pieces, groups)
-        sums[c] = sums[c] + jnp.sum(product.reshape(blk // 8, 8, LANES), axis=0)
-        return f
-
-    lax.fori_loop(0, blocks, step, 0, unroll=4)
-    return jnp.sum(sums[...], axis=1)
-
-
-def feeder_apply(values, table, field, sums, pieces, groups):
+    ways = unrolled(end - begin, ADJOINT_UNROLL)
+
+    def step(k, carry):
+        for u in range(ways):
+            j = begin + k * ways + u
+            product = values[j] * spread[table[j]]
+            c = table[blocks + j]
+            part = sums[u % len(sums)]
+            part[c] = part[c] + jnp.sum(product.reshape(blk // 8, 8, LANES), axis=0)
+        return carry
+
+    lax.fori_loop(0, (end - begin) // ways, step, 0)
+
+
+def adjoint_start(sums):
+    for part in sums:
+        part[...] = jnp.zeros_like(part)
+
+
+def adjoint_total(sums):
+    return jnp.sum(sum(part[...] for part in sums), axis=1)
+
+
+def feeder_adjoint(values, table, spread, sums):
+    adjoint_start(sums)
+    adjoint_loop(values, table, spread, sums, 0, values.shape[0])
+    return adjoint_total(sums)
+
+
+def feeder_duals(values, table, field, weight, duals_t, limits_t, spread):
     blocks, blk = values.shape[:2]
-
-    def step(j, carry):
-        f, acc = carry
-        fresh = j == table[blocks + f + 1]
-        f = jnp.where(fresh, f + 1, f)
-        keep = jnp.where(fresh, 0.0, 1.0).astype(F32)
-        c = row_of_block(table[j], pieces, groups)
-        acc = acc * keep + values[j] * field[pl.ds(c, 1), :]
-        sums[f] = acc
-        return f, acc
-
-    lax.fori_loop(0, blocks, step, (0, jnp.zeros((blk, LANES), F32)), unroll=4)
+    feeds = spread.shape[0]
+    ways = unrolled(blocks, APPLY_UNROLL)
+
+    def step(k, acc):
+        for u in range(ways):
+            j = k * ways + u
+            f = table[j]
+            before = table[jnp.maximum(j - 1, 0)]
+            keep = jnp.where(f == before, 1.0, 0.0).astype(F32)
+            acc = acc * keep + values[j] * field[pl.ds(table[blocks + j], 1), :]
+            spread[f] = acc
+        return acc
+
+    lax.fori_loop(0, blocks // ways, step, jnp.zeros((blk, LANES), F32))
+    step_dual = ETA_STEP * weight[:, :1]
+    shifted = duals_t - step_dual * limits_t
     lane = lane_iota((blk, LANES))
-    out = jnp.zeros((blk, LANES), F32)
-    for f in range(sums.shape[0]):
-        out = jnp.where(lane == f, jnp.sum(sums[f], axis=1, keepdims=True), out)
-    return out
+    new = jnp.zeros((blk, LANES), F32)
+    for f in range(feeds):
+        moved = spread[f] + jnp.where(lane == f, shifted, 0.0)
+        dual = jnp.maximum(0.0, jnp.sum(moved, axis=1, keepdims=True))
+        spread[f] = jnp.broadcast_to(dual, (blk, LANES))
+        new = jnp.where(lane == f, dual, new)
+    return new
 
 
 def pack_sums(primal, dual):
@@ -109,18 +135,33 @@
     return jnp.sum(value, axis=0, keepdims=True)
 
 
-def first_kernel(dims, first_rows, duals, inputs, values, table, slots, duals_t, limits_t, pushed_out, spread, sums):
-    pieces, groups = dims
-    blk = values.shape[1]
+def first_kernel(dims, first_rows, chunks, duals, inputs, values_in, table, slots, duals_t, limits_t, pushed_out,
+                 values, spread, *rest):
+    pieces, groups = dims
+    sums, sems = rest[:-1], rest[-1]
+    blocks, blk = values.shape[:2]
     feeds = duals.shape[1]
+    size = blocks // chunks
+    copies = [
+        pltpu.make_async_copy(values_in.at[pl.ds(k * size, size)], values.at[pl.ds(k * size, size)], sems.at[k])
+        for k in range(chunks)
+    ]
+    for copy in copies:
+        copy.start()
     for i, target in enumerate((duals_t, limits_t)):
         padded = jnp.concatenate([duals[i], jnp.zeros((blk - feeds, LANES), F32)], axis=0)
         target[...] = jnp.transpose(padded)
+    for f in range(feeds):
+        spread[f] = jnp.broadcast_to(duals_t[:, f : f + 1], (blk, LANES))
     sent = ((SLOT_DYN, DYN), (SLOT_POWER, POWER), (SLOT_PRICE, PRICE), (SLOT_LIMIT, LIMIT))
     for i in range(pieces):
         for slot, array in sent:
             slots[pl.ds(slot * pieces + i, groups, stride=first_rows), :] = inputs[array, :, i * LANES : (i + 1) * LANES]
-    pushed = feeder_adjoint(values, table, duals_t[...], spread, sums, pieces, groups)
+    adjoint_start(sums)
+    for k, copy in enumerate(copies):
+        copy.wait()
+        adjoint_loop(values, table, spread, sums, k * size, (k + 1) * size)
+    pushed = adjoint_total(sums)
     pushed_out[...] = pushed
     put_row(slots, SLOT_PUSHED, pushed, pieces, groups, first_rows)
 
@@ -158,39 +199,33 @@
     return primal, dual
 
 
-def feeder_step(weight, coupled, duals_t, limits_t):
-    step_dual = ETA_STEP * weight[:, :1]
-    return jnp.maximum(0.0, duals_t + step_dual * (coupled - limits_t))
-
-
 def row_power(dims, first_rows, weight, first, power, dyn, pushed, bar):
     pieces, groups = dims
     step_primal = ETA_STEP / weight[:, :1]
     price = take_row(first, SLOT_PRICE, pieces, groups, first_rows)
     limit = take_row(first, SLOT_LIMIT, pieces, groups, first_rows)
     new = clip(power - step_primal * (price - dyn + pushed), -limit, limit)
-    bar[...] = 2.0 * new - power
+    bar[...] = (ETA_STEP * weight[:, :1]) * (2.0 * new - power)
     return new
 
 
 def feeder_part(dims, slot_rows, weight, primal, dual, bar, dyn, duals_t, limits_t, values, table,
                 duals_out, pushed_out, slots, spread, sums):
     pieces, groups = dims
-    coupled = feeder_apply(values, table, bar, spread, pieces, groups)
-    new = feeder_step(weight, coupled, duals_t[...], limits_t[...])
+    new = feeder_duals(values, table, bar, weight, duals_t[...], limits_t[...], spread)
     duals_out[...] = new
     parts = pack_sums(primal, dual + row_sum((new - duals_t[...]) ** 2))
     slots[pl.ds(2 * pieces, groups, stride=slot_rows), :] = jnp.broadcast_to(parts, (groups, LANES))
     for i in range(pieces):
         slots[pl.ds(SLOT_DYN * pieces + i, groups, stride=slot_rows), :] = dyn[:, i * LANES : (i + 1) * LANES]
-    pushed = feeder_adjoint(values, table, new, spread, sums, pieces, groups)
+    pushed = feeder_adjoint(values, table, spread, sums)
     pushed_out[...] = pushed
     put_row(slots, SLOT_PUSHED, pushed, pieces, groups, slot_rows)
 
 
 def step_one_kernel(dims, first_rows, slot_rows, first, after, before, pushed_row, inputs, duals_t, limits_t, values,
                     table, weight, power_row, power_out, charge_out, dyn_out, edge_out, duals_out, pushed_out, slots,
-                    bar, spread, sums):
+                    bar, spread, *sums):
     pieces, groups = dims
     weight[...] = jnp.ones_like(weight)
     state = [lambda cut, array=array: inputs[array, :, cut] for array in (POWER, CHARGE, DYN)]
@@ -223,7 +258,7 @@
 
 def step_kernel(dims, first_rows, slot_rows, first, received, parts, weight_in, row_in, power, charge, dyn, edge_in,
                 pushed_row, inputs, duals_t, limits_t, values, table, weight, power_row, power_out, charge_out,
-                dyn_out, edge_out, duals_out, pushed_out, slots, bar, spread, sums):
+                dyn_out, edge_out, duals_out, pushed_out, slots, bar, spread, *sums):
     weight[...] = later_weight(weight_in, parts)
     state = [lambda cut, ref=ref: ref[:, cut] for ref in (power, charge, dyn)]
     primal, dual = local_step(dims, slot_rows, weight[...], received, inputs, state, later_edges(parts, edge_in),
@@ -243,8 +278,7 @@
                (power_out, charge_out, dyn_out), None)
     row_power(dims, first_rows, weight, first, row_in[...], take_row(received, SLOT_DYN, *dims, slot_rows),
               pushed_row[...], bar)
-    coupled = feeder_apply(values, table, bar, spread, *dims)
-    new = feeder_step(weight, coupled, duals_t[...], limits_t[...])
+    new = feeder_duals(values, table, bar, weight, duals_t[...], limits_t[...], spread)
     duals_out[...] = jnp.transpose(new)[: duals_out.shape[0]]
 
 
@@ -272,15 +306,16 @@
     return [jax.ShapeDtypeStruct(dim, F32) for dim in dims]
 
 
-def call(kernel, name, in_specs, out_dims, scratch=(), flops=0, moved=0):
+def call(kernel, name, in_specs, out_dims, scratch=(), flops=0, moved=0, limit=16 * 1024 * 1024, copies=0):
+    semaphores = [pltpu.SemaphoreType.DMA((copies,))] if copies else []
     return pl.pallas_call(
         kernel,
         name=name,
         in_specs=in_specs,
         out_specs=[VMEM] * len(out_dims),
         out_shape=shapes(*out_dims),
-        scratch_shapes=[pltpu.VMEM(dim, F32) for dim in scratch],
-        compiler_params=pltpu.CompilerParams(vmem_limit_bytes=16 * 1024 * 1024),
+        scratch_shapes=[pltpu.VMEM(dim, F32) for dim in scratch] + semaphores,
+        compiler_params=pltpu.CompilerParams(vmem_limit_bytes=limit),
         cost_estimate=pl.CostEstimate(flops=flops, bytes_accessed=moved, transcendentals=0),
     )
 
@@ -315,23 +350,27 @@
     row, line, square, own = (pieces * groups, LANES), (1, LANES), (blk, LANES), (groups, local)
     spread, sums = (feeds, blk, LANES), (pieces * groups, 8, LANES)
     matrix_specs = [VMEM, SMEM]
+    chunks = unrolled(blocks, CHUNKS)
     work, moved = 2 * blocks * blk * LANES, 4 * blocks * blk * LANES
 
     inputs = stacked(power0, charge0, dyn_dual0, price, inflow, power_limit, capacity)
     duals = stacked(feeder_dual0.reshape(feeds, blk), feeder_limit.reshape(feeds, blk))
-    matrix = (block_values, jnp.concatenate([block_cols, block_offsets]))
+    index_all = lax.broadcasted_iota(jnp.int32, (blocks, feeds - 1), 0)
+    row_of = jnp.sum((index_all >= block_offsets[None, 1:-1]).astype(jnp.int32), axis=1)
+    matrix = (block_values, jnp.concatenate([row_of, (block_cols % pieces) * groups + block_cols // pieces]))
 
     after = moved_to(inputs[DYN, :1], "tm", -1)
     before = moved_to(inputs[CHARGE : DYN + 1, -1], "tm", 1)
     first, duals_t, limits_t, pushed = call(
-        functools.partial(first_kernel, dims, first_rows), "first",
-        [VMEM] * 2 + matrix_specs, [(groups * first_rows, LANES), square, square, row], [spread, sums], work, moved,
+        functools.partial(first_kernel, dims, first_rows, chunks), "first",
+        [VMEM, VMEM, pl.BlockSpec(memory_space=pl.ANY), SMEM], [(groups * first_rows, LANES), square, square, row],
+        [block_values.shape, spread] + [sums] * ADJOINT_PARTS, work, moved, STREAMING_LIMIT, chunks,
     )(duals, inputs, *matrix)
     first, after, before = lax.optimization_barrier((first, after, before))
     first = exchange(first.reshape(groups, first_rows, LANES), "bat").reshape(groups * first_rows, LANES)
 
     step_outs = [line, row] + [own] * 3 + [(1, local), square, row, (groups * slot_rows, LANES)]
-    scratch = [row, spread, sums]
+    scratch = [row, spread] + [sums] * ADJOINT_PARTS
     for iteration in range(ITERS):
         last = iteration + 1 == ITERS
         outs = [own] * 3 + [(feeds, blk)] if last else step_outs

time: 138 us -> 136 us (0.986)
  local copies, waits for them, and re-layouts: 2.35 us -> 0.75 us
    unnamed x5 -> x3, local copies, waits for them, and re-layouts: 2.34 us -> 0.01 us
    pallas_call x3, Pallas kernels: 10.3 us -> 8.72 us  [shards(): call(functools.partial(last_kernel if last else step_kernel, *sizes), 'la...]
    pallas_call x1, Pallas kernels: 2.05 us -> 3.53 us  [shards(): call(functools.partial(first_kernel, dims, first_rows, chunks), 'first',...]
  transfers between devices with their start and end apart: 2 -> 2, of which waited for: 0 -> 0; matrix products, arithmetic and copies ran while one was open for 1% -> 2% of each run, Pallas kernels for 1% -> 3%
where the time goes in v4:
time: 136 us
  blocking collectives  106 us (78%)
  Pallas kernels  15.1 us (11%)
  starting transfers between devices  10.8 us (8%)
  other arithmetic  2.75 us (2%)
    all_to_all x7, blocking collectives, exchange(): return lax.all_to_all(value, axis, 0, 0, tiled=True)  106 us
    ppermute x2, starting transfers between devices, moved_to(): lax.ppermute(value, axis, [(i, i + distance) for i in range(count) if 0 <...  10.8 us
    pallas_call x3, Pallas kernels, shards(): call(functools.partial(last_kernel if last else step_kernel, *sizes), 'la...  8.72 us
    pallas_call x1, Pallas kernels, shards(): call(functools.partial(first_kernel, dims, first_rows, chunks), 'first',...  3.53 us
    pallas_call x1, Pallas kernels, shards(): call(functools.partial(step_one_kernel, *sizes), 'step_one', [VMEM] * 7 +...  2.84 us
  transfers between devices with their start and end apart: 2, of which 0 were waited for; matrix products, arithmetic and copies ran while one was open for 2% of the time, Pallas kernels for 3%

profile of v4, /device:TPU:1, one launch (start us, length us, event | category | flops | bytes accessed | tf_op | source)
XLA Modules:
  0.0 135.8 jit_solution(1212906662366698571)
XLA Ops:
  0.6 0.0 copy-start
  0.7 1.1 select_select_fusion.inputs
  1.8 8.9 %collective-permute-start = (f32[1,384]{1,0:T(1,128)S(1)}, f32[1,384]{1,0:T(1,128)S(1)}, u32[]{:S(2)}, u32[]{:S(2)}) collective-permute-start(f32[1,384]{1,0:T(1,128)S(1)} %slice_bitcast_fusion), channel_id=1, source_target_pairs={{16,0},{32,16},{48,32},{64,48},{80,64},{96,80},{112,96},{128,112},... | collective-permute-start | bytes 4616 | tf_op jit(solution)/shard_map/ppermute | solution.py:334
  10.7 1.9 %collective-permute-start.1 = (f32[2,384]{1,0:T(2,128)S(1)}, f32[2,384]{1,0:T(2,128)S(1)}, u32[]{:S(2)}, u32[]{:S(2)}) collective-permute-start(f32[2,384]{1,0:T(2,128)S(1)} %bitcast.44), channel_id=1, source_target_pairs={{0,16},{16,32},{32,48},{48,64},{64,80},{80,96},{96,112},{112,128},... | collective-permute-start | bytes 9224 | tf_op jit(solution)/shard_map/ppermute | solution.py:334
  12.7 0.7 fusion.1
  13.4 0.7 slice.9
  14.1 0.1 convert_reduce_fusion
  14.2 0.8 broadcast_select_fusion.duals
  15.0 0.1 pad_add_fusion.table
  15.0 3.5 %first.1 = (f32[256,128]{1,0:T(8,128)S(1)}, f32[128,128]{1,0:T(8,128)S(1)}, f32[128,128]{1,0:T(8,128)S(1)}, f32[48,128]{1,0:T(8,128)S(1)}) custom-call(f32[2,24,128]{2,1,0:T(8,128)S(1)} %broadcast_select_fusion.duals, f32[7,16,384]{2,1,0:T(8,128)S(1)} %select_select_fusion.inputs, f32[72,128,128]{2,1,0:T(8,128)} %values.7, s32[144]{0:T(256)S(1)} %pad_add_fusion.table), custom_call_target="tpu_custom_call" | custom-call | flops 2359296 | bytes 4718592 | tf_op jit(solution)/shard_map/first/pallas_call | solution.py:364
  18.6 0.0 collective-permute-done.after
  18.6 0.0 collective-permute-done.1.before
  18.6 9.5 %all_to_all.35 = f32[16,16,128]{2,1,0:T(8,128)S(1)} all-to-all(f32[16,16,128]{2,1,0:T(8,128)S(1)} %bitcast.38), channel_id=1, replica_groups=mesh['tm'=32,'bat'=16] {'bat'}, dimensions={0} | all-to-all | bytes 262144 | tf_op jit(solution)/shard_map/all_to_all | solution.py:338
  28.2 0.0 copy-done
  28.2 2.8 %step_one.1 = (f32[1,128]{1,0:T(1,128)S(1)}, f32[48,128]{1,0:T(8,128)S(1)}, f32[16,384]{1,0:T(8,128)S(1)}, f32[16,384]{1,0:T(8,128)S(1)}, f32[16,384]{1,0:T(8,12...) custom-call(f32[256,128]{1,0:T(8,128)S(1)} %bitcast.22, ...), custom_call_target="tpu_custom_call" | custom-call | flops 4718592 | bytes 4718592 | tf_op jit(solution)/shard_map/step_one/pallas_call | solution.py:379
  31.0 9.6 %all_to_all.36 = f32[16,8,128]{2,1,0:T(8,128)S(1)} all-to-all(f32[16,8,128]{2,1,0:T(8,128)S(1)} %bitcast.41), channel_id=1, replica_groups=mesh['tm'=32,'bat'=16] {'bat'}, dimensions={0} | all-to-all | bytes 131072 | tf_op jit(solution)/shard_map/all_to_all | solution.py:338
  40.6 30.2 %all_to_all.37 = f32[32,4,128]{2,1,0:T(4,128)S(1)} all-to-all(f32[32,4,128]{2,1,0:T(4,128)S(1)} %bitcast.35), channel_id=1, replica_groups=mesh['tm'=32,'bat'=16] {'tm'}, dimensions={0} | all-to-all | bytes 131072 | tf_op jit(solution)/shard_map/all_to_all | solution.py:338
  70.8 3.0 %step.2 = (f32[1,128]{1,0:T(1,128)S(1)}, f32[48,128]{1,0:T(8,128)S(1)}, f32[16,384]{1,0:T(8,128)S(1)}, f32[16,384]{1,0:T(8,128)S(1)}, f32[16,384]{1,0:T(8,128)S(...) custom-call(f32[256,128]{1,0:T(8,128)S(1)} %bitcast.23, ...), custom_call_target="tpu_custom_call" | custom-call | flops 4718592 | bytes 4718592 | tf_op jit(solution)/shard_map/step/pallas_call | solution.py:384
  73.8 9.4 %all_to_all.38 = f32[16,8,128]{2,1,0:T(8,128)S(1)} all-to-all(f32[16,8,128]{2,1,0:T(8,128)S(1)} %bitcast.39), channel_id=1, replica_groups=mesh['tm'=32,'bat'=16] {'bat'}, dimensions={0} | all-to-all | bytes 131072 | tf_op jit(solution)/shard_map/all_to_all | solution.py:338
  83.2 18.7 %all_to_all.39 = f32[32,4,128]{2,1,0:T(4,128)S(1)} all-to-all(f32[32,4,128]{2,1,0:T(4,128)S(1)} %bitcast.36), channel_id=1, replica_groups=mesh['tm'=32,'bat'=16] {'tm'}, dimensions={0} | all-to-all | bytes 131072 | tf_op jit(solution)/shard_map/all_to_all | solution.py:338
  101.9 3.0 %step.3 = (f32[1,128]{1,0:T(1,128)S(1)}, f32[48,128]{1,0:T(8,128)S(1)}, f32[16,384]{1,0:T(8,128)S(1)}, f32[16,384]{1,0:T(8,128)S(1)}, f32[16,384]{1,0:T(8,128)S(...) custom-call(f32[256,128]{1,0:T(8,128)S(1)} %bitcast.24, ...), custom_call_target="tpu_custom_call" | custom-call | flops 4718592 | bytes 4718592 | tf_op jit(solution)/shard_map/step/pallas_call | solution.py:384
  104.9 9.4 %all_to_all.40 = f32[16,8,128]{2,1,0:T(8,128)S(1)} all-to-all(f32[16,8,128]{2,1,0:T(8,128)S(1)} %bitcast.40), channel_id=1, replica_groups=mesh['tm'=32,'bat'=16] {'bat'}, dimensions={0} | all-to-all | bytes 131072 | tf_op jit(solution)/shard_map/all_to_all | solution.py:338
  114.4 18.7 %all_to_all.41 = f32[32,4,128]{2,1,0:T(4,128)S(1)} all-to-all(f32[32,4,128]{2,1,0:T(4,128)S(1)} %bitcast.37), channel_id=1, replica_groups=mesh['tm'=32,'bat'=16] {'tm'}, dimensions={0} | all-to-all | bytes 131072 | tf_op jit(solution)/shard_map/all_to_all | solution.py:338
  133.1 2.7 %last.1 = (f32[16,384]{1,0:T(8,128)}, f32[16,384]{1,0:T(8,128)}, f32[16,384]{1,0:T(8,128)}, f32[24,128]{1,0:T(8,128)}) custom-call(f32[256,128]{1,0:T(8,128)S(1)} %bitcast.25, f32[128,128]{1,0:T(8,128)S(1)} %bitcast.31, f32[128,128]{1,0:T(8,128)S(1)} %bitcast.34, f32[1,128]{1,0:T(1,128)S(1)} %get-tuple-element.69.weight_in, ...), custom_call_target="tpu_custom_call" | custom-call | flops 4718592 | bytes 4718592 | tf_op jit(solution)/shard_map/last/pallas_call | solution.py:384
  (10 shorter events, 0.1 us)
Async XLA Ops:
  0.6 27.5 %copy-start = (f32[72,128,128]{2,1,0:T(8,128)S(1)}, f32[72,128,128]{2,1,0:T(8,128)}, u32[]{:S(2)}) copy-start(f32[72,128,128]{2,1,0:T(8,128)} %values.7) | copy-start | bytes 14155780
  1.8 16.8 %collective-permute-start = (f32[1,384]{1,0:T(1,128)S(1)}, f32[1,384]{1,0:T(1,128)S(1)}, u32[]{:S(2)}, u32[]{:S(2)}) collective-permute-start(f32[1,384]{1,0:T(1,128)S(1)} %slice_bitcast_fusion), channel_id=1, source_target_pairs={{16,0},{32,16},{48,32},{64,48},{80,64},{96,80},{112,96},{128,112},... | collective-permute-start | bytes 4616 | tf_op jit(solution)/shard_map/ppermute | solution.py:334
  10.7 7.9 %collective-permute-start.1 = (f32[2,384]{1,0:T(2,128)S(1)}, f32[2,384]{1,0:T(2,128)S(1)}, u32[]{:S(2)}, u32[]{:S(2)}) collective-permute-start(f32[2,384]{1,0:T(2,128)S(1)} %bitcast.44), channel_id=1, source_target_pairs={{0,16},{16,32},{32,48},{48,64},{64,80},{80,96},{96,112},{112,128},... | collective-permute-start | bytes 9224 | tf_op jit(solution)/shard_map/ppermute | solution.py:334

commit v5 on v4

--- a/solution.py
+++ b/solution.py
@@ -20,10 +20,13 @@
 F32 = jnp.float32
 
 VMEM = pl.BlockSpec(memory_space=pltpu.VMEM)
-SMEM = pl.BlockSpec(memory_space=pltpu.SMEM)
 
 POWER, CHARGE, DYN, PRICE, INFLOW, LIMIT, CAPACITY = range(7)
 SLOT_DYN, SLOT_PUSHED, SLOT_POWER, SLOT_PRICE, SLOT_LIMIT = range(5)
+
+
+def places():
+    return lax.axis_index("z"), lax.axis_index("core"), lax.axis_index("bat")
 
 
 def rows_up(count):
@@ -135,10 +138,17 @@
     return jnp.sum(value, axis=0, keepdims=True)
 
 
-def first_kernel(dims, first_rows, chunks, duals, inputs, values_in, table, slots, duals_t, limits_t, pushed_out,
+def table_load(table_in, table, sem):
+    copy = pltpu.make_async_copy(table_in, table, sem)
+    copy.start()
+    return copy
+
+
+def first_kernel(dims, first_rows, chunks, duals, inputs, values_in, table_in, slots, duals_t, limits_t, pushed_out,
                  values, spread, *rest):
     pieces, groups = dims
-    sums, sems = rest[:-1], rest[-1]
+    *sums, sems, table, sem = rest
+    load = table_load(table_in, table, sem)
     blocks, blk = values.shape[:2]
     feeds = duals.shape[1]
     size = blocks // chunks
@@ -158,6 +168,7 @@
         for slot, array in sent:
             slots[pl.ds(slot * pieces + i, groups, stride=first_rows), :] = inputs[array, :, i * LANES : (i + 1) * LANES]
     adjoint_start(sums)
+    load.wait()
     for k, copy in enumerate(copies):
         copy.wait()
         adjoint_loop(values, table, spread, sums, k * size, (k + 1) * size)
@@ -171,7 +182,8 @@
     step_primal = ETA_STEP / weight[:, :1]
     step_dual = ETA_STEP * weight[:, :1]
     after, before_dyn, before_charge = edges
-    begin = lax.axis_index("tm") == 0
+    z, core, _ = places()
+    begin = (z == 0) & (core == 0)
     line = lax.broadcasted_iota(jnp.int32, (groups, LANES), 0)
     primal = jnp.zeros((1, LANES), F32)
     dual = jnp.zeros((1, LANES), F32)
@@ -212,21 +224,30 @@
 def feeder_part(dims, slot_rows, weight, primal, dual, bar, dyn, duals_t, limits_t, values, table,
                 duals_out, pushed_out, slots, spread, sums):
     pieces, groups = dims
+    _, core, bat = places()
     new = feeder_duals(values, table, bar, weight, duals_t[...], limits_t[...], spread)
     duals_out[...] = new
     parts = pack_sums(primal, dual + row_sum((new - duals_t[...]) ** 2))
-    slots[pl.ds(2 * pieces, groups, stride=slot_rows), :] = jnp.broadcast_to(parts, (groups, LANES))
+    slots[...] = jnp.zeros_like(slots)
+    own, other = slots.at[core], slots.at[1 - core]
+    for side in (own, other):
+        side[pl.ds(2 * pieces, groups, stride=slot_rows), :] = jnp.broadcast_to(parts, (groups, LANES))
     for i in range(pieces):
-        slots[pl.ds(SLOT_DYN * pieces + i, groups, stride=slot_rows), :] = dyn[:, i * LANES : (i + 1) * LANES]
+        cut = slice(i * LANES, (i + 1) * LANES)
+        own[pl.ds(SLOT_DYN * pieces + i, groups, stride=slot_rows), :] = dyn[:, cut]
+        other[pl.ds(bat * slot_rows + i, 1), :] = dyn[:1, cut]
+        other[pl.ds(bat * slot_rows + pieces + i, 1), :] = dyn[groups - 1 :, cut]
     pushed = feeder_adjoint(values, table, spread, sums)
     pushed_out[...] = pushed
-    put_row(slots, SLOT_PUSHED, pushed, pieces, groups, slot_rows)
+    put_row(own, SLOT_PUSHED, pushed, pieces, groups, slot_rows)
 
 
 def step_one_kernel(dims, first_rows, slot_rows, first, after, before, pushed_row, inputs, duals_t, limits_t, values,
-                    table, weight, power_row, power_out, charge_out, dyn_out, edge_out, duals_out, pushed_out, slots,
-                    bar, spread, *sums):
-    pieces, groups = dims
+                    table_in, weight, power_row, power_out, charge_out, dyn_out, edge_out, duals_out, pushed_out, slots,
+                    bar, spread, *rest):
+    *sums, table, sem = rest
+    pieces, groups = dims
+    load = table_load(table_in, table, sem)
     weight[...] = jnp.ones_like(weight)
     state = [lambda cut, array=array: inputs[array, :, cut] for array in (POWER, CHARGE, DYN)]
     edges = [lambda i, ref=ref, k=k: ref[k : k + 1, i * LANES : (i + 1) * LANES]
@@ -236,85 +257,102 @@
     power_row[...] = row_power(dims, first_rows, weight[...], first,
                                take_row(first, SLOT_POWER, pieces, groups, first_rows),
                                take_row(first, SLOT_DYN, pieces, groups, first_rows), pushed_row[...], bar)
+    load.wait()
     feeder_part(dims, slot_rows, weight[...], primal, dual, bar, dyn_out, duals_t, limits_t, values, table,
                 duals_out, pushed_out, slots, spread, sums)
 
 
-def later_edges(parts, edge_in):
-    steps = lax.axis_size("tm")
-    here = lax.axis_index("tm")
-    lines = parts.shape[0] // steps
-    above, below = jnp.minimum(here + 1, steps - 1), jnp.maximum(here - 1, 0)
-    after = lambda i: jnp.where(here == steps - 1, 0.0, parts[pl.ds(above * lines + 1 + i, 1), :])
-    before_dyn = lambda i: parts[pl.ds(below * lines + 1 + i, 1), :]
+def later_edges(dims, slot_rows, received, parts, edge_in):
+    pieces, _ = dims
+    z, core, bat = places()
+    chips = lax.axis_size("z")
+    lines = parts.shape[0] // chips
+    above, below = jnp.minimum(z + 1, chips - 1), jnp.maximum(z - 1, 0)
+    end = jnp.where(z == chips - 1, 0.0, 1.0).astype(F32)
+    after = lambda i: jnp.where(
+        core == 0, received[1, pl.ds(bat * slot_rows + i, 1), :], end * parts[pl.ds(above * lines + 1 + i, 1), :]
+    )
+    before_dyn = lambda i: jnp.where(
+        core == 0, parts[pl.ds(below * lines + 1 + i, 1), :], received[0, pl.ds(bat * slot_rows + pieces + i, 1), :]
+    )
     before_charge = lambda i: edge_in[:, i * LANES : (i + 1) * LANES]
     return after, before_dyn, before_charge
 
 
 def later_weight(weight_in, parts):
-    steps = lax.axis_size("tm")
-    return next_weight(weight_in[...], parts[pl.ds(0, steps, stride=parts.shape[0] // steps), :])
+    chips = lax.axis_size("z")
+    return next_weight(weight_in[...], parts[pl.ds(0, chips, stride=parts.shape[0] // chips), :])
 
 
 def step_kernel(dims, first_rows, slot_rows, first, received, parts, weight_in, row_in, power, charge, dyn, edge_in,
-                pushed_row, inputs, duals_t, limits_t, values, table, weight, power_row, power_out, charge_out,
-                dyn_out, edge_out, duals_out, pushed_out, slots, bar, spread, *sums):
+                pushed_row, inputs, duals_t, limits_t, values, table_in, weight, power_row, power_out, charge_out,
+                dyn_out, edge_out, duals_out, pushed_out, slots, bar, spread, *rest):
+    *sums, table, sem = rest
+    load = table_load(table_in, table, sem)
     weight[...] = later_weight(weight_in, parts)
+    own = received.at[lax.axis_index("core")]
     state = [lambda cut, ref=ref: ref[:, cut] for ref in (power, charge, dyn)]
-    primal, dual = local_step(dims, slot_rows, weight[...], received, inputs, state, later_edges(parts, edge_in),
+    primal, dual = local_step(dims, slot_rows, weight[...], own, inputs, state,
+                              later_edges(dims, slot_rows, received, parts, edge_in),
                               (power_out, charge_out, dyn_out), edge_out)
     power_row[...] = row_power(dims, first_rows, weight[...], first, row_in[...],
-                               take_row(received, SLOT_DYN, *dims, slot_rows), pushed_row[...], bar)
+                               take_row(own, SLOT_DYN, *dims, slot_rows), pushed_row[...], bar)
+    load.wait()
     feeder_part(dims, slot_rows, weight[...], primal, dual, bar, dyn_out, duals_t, limits_t, values, table,
                 duals_out, pushed_out, slots, spread, sums)
 
 
 def last_kernel(dims, first_rows, slot_rows, first, received, parts, weight_in, row_in, power, charge, dyn, edge_in,
-                pushed_row, inputs, duals_t, limits_t, values, table, power_out, charge_out, dyn_out, duals_out,
-                bar, spread):
+                pushed_row, inputs, duals_t, limits_t, values, table_in, power_out, charge_out, dyn_out, duals_out,
+                bar, spread, table, sem):
+    load = table_load(table_in, table, sem)
     weight = later_weight(weight_in, parts)
+    own = received.at[lax.axis_index("core")]
     state = [lambda cut, ref=ref: ref[:, cut] for ref in (power, charge, dyn)]
-    local_step(dims, slot_rows, weight, received, inputs, state, later_edges(parts, edge_in),
+    local_step(dims, slot_rows, weight, own, inputs, state, later_edges(dims, slot_rows, received, parts, edge_in),
                (power_out, charge_out, dyn_out), None)
-    row_power(dims, first_rows, weight, first, row_in[...], take_row(received, SLOT_DYN, *dims, slot_rows),
+    row_power(dims, first_rows, weight, first, row_in[...], take_row(own, SLOT_DYN, *dims, slot_rows),
               pushed_row[...], bar)
+    load.wait()
     new = feeder_duals(values, table, bar, weight, duals_t[...], limits_t[...], spread)
     duals_out[...] = jnp.transpose(new)[: duals_out.shape[0]]
 
 
-def relay_kernel(dims, slot_rows, received, dyn, parts):
-    pieces, groups = dims
-    steps = lax.axis_size("tm")
-    here = lax.axis_index("tm")
-    lines = parts.shape[0] // steps
+def relay_kernel(dims, slot_rows, received, parts):
+    pieces, groups = dims
+    z, core, bat = places()
+    chips = lax.axis_size("z")
+    lines = parts.shape[0] // chips
     parts[...] = jnp.zeros_like(parts)
-    summed = row_sum(received[pl.ds(2 * pieces, groups, stride=slot_rows), :])
-    parts[pl.ds(0, steps, stride=lines), :] = jnp.broadcast_to(summed, (steps, LANES))
-
-    @pl.when(here > 0)
+    summed = sum(row_sum(received[k, pl.ds(2 * pieces, groups, stride=slot_rows), :]) for k in range(2))
+    parts[pl.ds(0, chips, stride=lines), :] = jnp.broadcast_to(summed, (chips, LANES))
+
+    @pl.when((core == 1) & (z > 0))
     def _():
         for i in range(pieces):
-            parts[pl.ds((here - 1) * lines + 1 + i, 1), :] = dyn[:1, i * LANES : (i + 1) * LANES]
-
-    @pl.when(here < steps - 1)
+            parts[pl.ds((z - 1) * lines + 1 + i, 1), :] = received[0, pl.ds(bat * slot_rows + i, 1), :]
+
+    @pl.when((core == 0) & (z < chips - 1))
     def _():
         for i in range(pieces):
-            parts[pl.ds((here + 1) * lines + 1 + i, 1), :] = dyn[groups - 1 :, i * LANES : (i + 1) * LANES]
+            parts[pl.ds((z + 1) * lines + 1 + i, 1), :] = received[1, pl.ds(bat * slot_rows + pieces + i, 1), :]
 
 
 def shapes(*dims):
     return [jax.ShapeDtypeStruct(dim, F32) for dim in dims]
 
 
-def call(kernel, name, in_specs, out_dims, scratch=(), flops=0, moved=0, limit=16 * 1024 * 1024, copies=0):
-    semaphores = [pltpu.SemaphoreType.DMA((copies,))] if copies else []
+def call(kernel, name, in_specs, out_dims, scratch=(), flops=0, moved=0, limit=16 * 1024 * 1024, copies=0, table=0):
+    more = [pltpu.SemaphoreType.DMA((copies,))] if copies else []
+    if table:
+        more += [pltpu.SMEM((table,), jnp.int32), pltpu.SemaphoreType.DMA]
     return pl.pallas_call(
         kernel,
         name=name,
         in_specs=in_specs,
         out_specs=[VMEM] * len(out_dims),
         out_shape=shapes(*out_dims),
-        scratch_shapes=[pltpu.VMEM(dim, F32) for dim in scratch] + semaphores,
+        scratch_shapes=[pltpu.VMEM(dim, F32) for dim in scratch] + more,
         compiler_params=pltpu.CompilerParams(vmem_limit_bytes=limit),
         cost_estimate=pl.CostEstimate(flops=flops, bytes_accessed=moved, transcendentals=0),
     )
@@ -344,32 +382,35 @@
     pieces = local // LANES
     blocks, blk = block_values.shape[:2]
     feeds = block_offsets.shape[0] - 1
-    steps = lax.axis_size("tm")
+    chips = lax.axis_size("z")
     first_rows, slot_rows, lines = rows_up(5 * pieces), rows_up(2 * pieces + 1), 1 + pieces
     dims = (pieces, groups)
     row, line, square, own = (pieces * groups, LANES), (1, LANES), (blk, LANES), (groups, local)
     spread, sums = (feeds, blk, LANES), (pieces * groups, 8, LANES)
-    matrix_specs = [VMEM, SMEM]
+    matrix_specs = [VMEM, VMEM]
     chunks = unrolled(blocks, CHUNKS)
     work, moved = 2 * blocks * blk * LANES, 4 * blocks * blk * LANES
 
     inputs = stacked(power0, charge0, dyn_dual0, price, inflow, power_limit, capacity)
     duals = stacked(feeder_dual0.reshape(feeds, blk), feeder_limit.reshape(feeds, blk))
+    tables = lax.optimization_barrier(jnp.concatenate([block_cols, block_offsets]))
+    block_cols, block_offsets = tables[:blocks], tables[blocks:]
     index_all = lax.broadcasted_iota(jnp.int32, (blocks, feeds - 1), 0)
     row_of = jnp.sum((index_all >= block_offsets[None, 1:-1]).astype(jnp.int32), axis=1)
     matrix = (block_values, jnp.concatenate([row_of, (block_cols % pieces) * groups + block_cols // pieces]))
 
-    after = moved_to(inputs[DYN, :1], "tm", -1)
-    before = moved_to(inputs[CHARGE : DYN + 1, -1], "tm", 1)
+    after = moved_to(inputs[DYN, :1], ("z", "core"), -1)
+    before = moved_to(inputs[CHARGE : DYN + 1, -1], ("z", "core"), 1)
     first, duals_t, limits_t, pushed = call(
         functools.partial(first_kernel, dims, first_rows, chunks), "first",
-        [VMEM, VMEM, pl.BlockSpec(memory_space=pl.ANY), SMEM], [(groups * first_rows, LANES), square, square, row],
-        [block_values.shape, spread] + [sums] * ADJOINT_PARTS, work, moved, STREAMING_LIMIT, chunks,
+        [VMEM, VMEM, pl.BlockSpec(memory_space=pl.ANY), VMEM], [(groups * first_rows, LANES), square, square, row],
+        [block_values.shape, spread] + [sums] * ADJOINT_PARTS, work, moved, STREAMING_LIMIT, chunks, 2 * blocks,
     )(duals, inputs, *matrix)
     first, after, before = lax.optimization_barrier((first, after, before))
     first = exchange(first.reshape(groups, first_rows, LANES), "bat").reshape(groups * first_rows, LANES)
 
-    step_outs = [line, row] + [own] * 3 + [(1, local), square, row, (groups * slot_rows, LANES)]
+    both = (2, groups * slot_rows, LANES)
+    step_outs = [line, row] + [own] * 3 + [(1, local), square, row, both]
     scratch = [row, spread] + [sums] * ADJOINT_PARTS
     for iteration in range(ITERS):
         last = iteration + 1 == ITERS
@@ -378,31 +419,35 @@
         if iteration == 0:
             results = call(
                 functools.partial(step_one_kernel, *sizes), "step_one", [VMEM] * 7 + matrix_specs, outs, scratch,
-                2 * work, moved,
+                2 * work, moved, table=2 * blocks,
             )(first, after, before, pushed, inputs, duals_t, limits_t, *matrix)
         else:
             results = call(
                 functools.partial(last_kernel if last else step_kernel, *sizes), "last" if last else "step",
                 [VMEM] * 13 + matrix_specs, outs, scratch[:2] if last else scratch, 2 * work, moved,
+                table=2 * blocks,
             )(first, received, parts, weight, power_row, power, charge, dyn, edge, pushed, inputs, duals_t, limits_t,
               *matrix)
         if not last:
             weight, power_row, power, charge, dyn, edge, duals_t, pushed, slots = results
-            received = exchange(slots.reshape(groups, slot_rows, LANES), "bat").reshape(groups * slot_rows, LANES)
+            received = exchange(slots.reshape(2 * groups, slot_rows, LANES), ("core", "bat")).reshape(both)
             parts = call(
-                functools.partial(relay_kernel, dims, slot_rows), "relay", [VMEM] * 2, [(steps * lines, LANES)]
-            )(received, dyn)[0]
-            parts = exchange(parts.reshape(steps, lines, LANES), "tm").reshape(steps * lines, LANES)
+                functools.partial(relay_kernel, dims, slot_rows), "relay", [VMEM], [(chips * lines, LANES)]
+            )(received)[0]
+            parts = exchange(parts.reshape(chips, lines, LANES), "z").reshape(chips * lines, LANES)
     power, charge, dyn_dual, feeder_dual = results
     return power, charge, dyn_dual, feeder_dual.reshape(1, feeds * blk)
 
 
 def solution(mesh):
-    split = P("tm", "bat")
-    steps = P(("tm", "bat"), None)
+    fine = jax.sharding.Mesh(
+        mesh.devices.reshape(mesh.shape["tm"] // 2, 2, mesh.shape["bat"]), ("z", "core", "bat")
+    )
+    split = P(("z", "core"), "bat")
+    steps = P(("z", "core", "bat"), None)
     return jax.shard_map(
         shards,
-        mesh=mesh,
+        mesh=fine,
         in_specs=(split, split, split, steps, split, split, P("bat"), P("bat"), P(), P(), P(), P()),
         out_specs=(split, split, split, steps),
         check_vma=False,

time: 136 us -> 129 us (0.949)
  blocking collectives: 106 us -> 100 us
    all_to_all x7, blocking collectives: 106 us -> 100 us  [exchange(): return lax.all_to_all(value, axis, 0, 0, tiled=True)]
  transfers between devices with their start and end apart: 2 -> 2, of which waited for: 0 -> 0; matrix products, arithmetic and copies ran while one was open for 2% -> 1% of each run, Pallas kernels for 3% -> 2%
where the time goes in v5:
time: 129 us
  blocking collectives  100 us (78%)
  Pallas kernels  13.9 us (11%)
  starting transfers between devices  10.8 us (8%)
  other arithmetic  2.84 us (2%)
    all_to_all x7, blocking collectives, exchange(): return lax.all_to_all(value, axis, 0, 0, tiled=True)  100 us
    ppermute x2, starting transfers between devices, moved_to(): lax.ppermute(value, axis, [(i, i + distance) for i in range(count) if 0 <...  10.8 us
    pallas_call x3, Pallas kernels, shards(): call(functools.partial(last_kernel if last else step_kernel, *sizes), 'la...  8.07 us
    pallas_call x1, Pallas kernels, shards(): call(functools.partial(first_kernel, dims, first_rows, chunks), 'first',...  2.99 us
    pallas_call x1, Pallas kernels, shards(): call(functools.partial(step_one_kernel, *sizes), 'step_one', [VMEM] * 7 +...  2.76 us
  transfers between devices with their start and end apart: 2, of which 0 were waited for; matrix products, arithmetic and copies ran while one was open for 1% of the time, Pallas kernels for 2%

profile of v5, /device:TPU:1, one launch (start us, length us, event | category | flops | bytes accessed | tf_op | source)
XLA Modules:
  0.0 128.6 jit_solution(6480070651418790939)
XLA Ops:
  0.6 0.0 copy-start
  0.7 1.1 select_select_fusion.inputs
  1.8 8.9 %collective-permute-start = (f32[1,384]{1,0:T(1,128)S(1)}, f32[1,384]{1,0:T(1,128)S(1)}, u32[]{:S(2)}, u32[]{:S(2)}) collective-permute-start(f32[1,384]{1,0:T(1,128)S(1)} %slice_bitcast_fusion), channel_id=1, source_target_pairs={{16,0},{32,16},{48,32},{64,48},{80,64},{96,80},{112,96},{128,112},... | collective-permute-start | bytes 4616 | tf_op jit(solution)/shard_map/ppermute | solution.py:372
  10.7 1.9 %collective-permute-start.1 = (f32[2,384]{1,0:T(2,128)S(1)}, f32[2,384]{1,0:T(2,128)S(1)}, u32[]{:S(2)}, u32[]{:S(2)}) collective-permute-start(f32[2,384]{1,0:T(2,128)S(1)} %bitcast.44), channel_id=1, source_target_pairs={{0,16},{16,32},{32,48},{48,64},{64,80},{80,96},{96,112},{112,128},... | collective-permute-start | bytes 9224 | tf_op jit(solution)/shard_map/ppermute | solution.py:372
  12.7 0.7 pad_add_fusion.1
  13.4 0.1 slice.14
  13.5 0.1 convert_reduce_fusion
  13.6 0.8 broadcast_select_fusion.duals
  14.4 0.1 pad_add_fusion.table_in
  14.5 3.0 %first.1 = (f32[256,128]{1,0:T(8,128)S(1)}, f32[128,128]{1,0:T(8,128)S(1)}, f32[128,128]{1,0:T(8,128)S(1)}, f32[48,128]{1,0:T(8,128)S(1)}) custom-call(f32[2,24,128]{2,1,0:T(8,128)S(1)} %broadcast_select_fusion.duals, f32[7,16,384]{2,1,0:T(8,128)S(1)} %select_select_fusion.inputs, f32[72,128,128]{2,1,0:T(8,128)} %values.7, s32[144]{0:T(256)S(1)} %pad_add_fusion.table_in), custom_call_target="tpu_custom_call" | custom-call | flops 2359296 | bytes 4718592 | tf_op jit(solution)/shard_map/first/pallas_call | solution.py:404
  17.5 0.0 collective-permute-done.after
  17.5 0.0 collective-permute-done.1.before
  17.5 9.5 %all_to_all.35 = f32[16,16,128]{2,1,0:T(8,128)S(1)} all-to-all(f32[16,16,128]{2,1,0:T(8,128)S(1)} %bitcast.40), channel_id=1, replica_groups=mesh['z'=16,'core'=2,'bat'=16] {'bat'}, dimensions={0} | all-to-all | bytes 262144 | tf_op jit(solution)/shard_map/all_to_all | solution.py:376
  27.0 0.0 copy-done
  27.0 2.8 %step_one.1 = (f32[1,128]{1,0:T(1,128)S(1)}, f32[48,128]{1,0:T(8,128)S(1)}, f32[16,384]{1,0:T(8,128)S(1)}, f32[16,384]{1,0:T(8,128)S(1)}, f32[16,384]{1,0:T(8,12...) custom-call(f32[256,128]{1,0:T(8,128)S(1)} %bitcast.22, ...), custom_call_target="tpu_custom_call" | custom-call | flops 4718592 | bytes 4718592 | tf_op jit(solution)/shard_map/step_one/pallas_call | solution.py:420
  29.8 12.2 %all_to_all.36 = f32[32,8,128]{2,1,0:T(8,128)S(1)} all-to-all(f32[32,8,128]{2,1,0:T(8,128)S(1)} %bitcast.41), channel_id=1, replica_groups=mesh['z'=16,'core'=2,'bat'=16] {'core','bat'}, dimensions={0} | all-to-all | bytes 262144 | tf_op jit(solution)/shard_map/all_to_all | solution.py:376
  42.0 25.6 %all_to_all.37 = f32[16,4,128]{2,1,0:T(4,128)S(1)} all-to-all(f32[16,4,128]{2,1,0:T(4,128)S(1)} %bitcast.35), channel_id=1, replica_groups=mesh['z'=16,'core'=2,'bat'=16] {'z'}, dimensions={0} | all-to-all | bytes 65536 | tf_op jit(solution)/shard_map/all_to_all | solution.py:376
  67.6 2.8 %step.2 = (f32[1,128]{1,0:T(1,128)S(1)}, f32[48,128]{1,0:T(8,128)S(1)}, f32[16,384]{1,0:T(8,128)S(1)}, f32[16,384]{1,0:T(8,128)S(1)}, f32[16,384]{1,0:T(8,128)S(...) custom-call(f32[256,128]{1,0:T(8,128)S(1)} %bitcast.23, ...), custom_call_target="tpu_custom_call" | custom-call | flops 4718592 | bytes 4718592 | tf_op jit(solution)/shard_map/step/pallas_call | solution.py:425
  70.4 12.6 %all_to_all.38 = f32[32,8,128]{2,1,0:T(8,128)S(1)} all-to-all(f32[32,8,128]{2,1,0:T(8,128)S(1)} %bitcast.38), channel_id=1, replica_groups=mesh['z'=16,'core'=2,'bat'=16] {'core','bat'}, dimensions={0} | all-to-all | bytes 262144 | tf_op jit(solution)/shard_map/all_to_all | solution.py:376
  83.0 14.0 %all_to_all.39 = f32[16,4,128]{2,1,0:T(4,128)S(1)} all-to-all(f32[16,4,128]{2,1,0:T(4,128)S(1)} %bitcast.36), channel_id=1, replica_groups=mesh['z'=16,'core'=2,'bat'=16] {'z'}, dimensions={0} | all-to-all | bytes 65536 | tf_op jit(solution)/shard_map/all_to_all | solution.py:376
  97.0 2.8 %step.3 = (f32[1,128]{1,0:T(1,128)S(1)}, f32[48,128]{1,0:T(8,128)S(1)}, f32[16,384]{1,0:T(8,128)S(1)}, f32[16,384]{1,0:T(8,128)S(1)}, f32[16,384]{1,0:T(8,128)S(...) custom-call(f32[256,128]{1,0:T(8,128)S(1)} %bitcast.24, ...), custom_call_target="tpu_custom_call" | custom-call | flops 4718592 | bytes 4718592 | tf_op jit(solution)/shard_map/step/pallas_call | solution.py:425
  99.8 12.3 %all_to_all.40 = f32[32,8,128]{2,1,0:T(8,128)S(1)} all-to-all(f32[32,8,128]{2,1,0:T(8,128)S(1)} %bitcast.39), channel_id=1, replica_groups=mesh['z'=16,'core'=2,'bat'=16] {'core','bat'}, dimensions={0} | all-to-all | bytes 262144 | tf_op jit(solution)/shard_map/all_to_all | solution.py:376
  112.1 14.0 %all_to_all.41 = f32[16,4,128]{2,1,0:T(4,128)S(1)} all-to-all(f32[16,4,128]{2,1,0:T(4,128)S(1)} %bitcast.37), channel_id=1, replica_groups=mesh['z'=16,'core'=2,'bat'=16] {'z'}, dimensions={0} | all-to-all | bytes 65536 | tf_op jit(solution)/shard_map/all_to_all | solution.py:376
  126.1 2.5 %last.1 = (f32[16,384]{1,0:T(8,128)}, f32[16,384]{1,0:T(8,128)}, f32[16,384]{1,0:T(8,128)}, f32[24,128]{1,0:T(8,128)}) custom-call(f32[256,128]{1,0:T(8,128)S(1)} %bitcast.25, f32[2,128,128]{2,1,0:T(8,128)S(1)} %bitcast.31, f32[64,128]{1,0:T(8,128)S(1)} %bitcast.34, f32[1,128]{1,0:T(1,128)S(1)} %get-tuple-element.68.weight_in, ...), custom_call_target="tpu_custom_call" | custom-call | flops 4718592 | bytes 4718592 | tf_op jit(solution)/shard_map/last/pallas_call | solution.py:425
  (11 shorter events, 0.1 us)
Async XLA Ops:
  0.6 26.4 %copy-start = (f32[72,128,128]{2,1,0:T(8,128)S(1)}, f32[72,128,128]{2,1,0:T(8,128)}, u32[]{:S(2)}) copy-start(f32[72,128,128]{2,1,0:T(8,128)} %values.7) | copy-start | bytes 14155780
  1.8 15.7 %collective-permute-start = (f32[1,384]{1,0:T(1,128)S(1)}, f32[1,384]{1,0:T(1,128)S(1)}, u32[]{:S(2)}, u32[]{:S(2)}) collective-permute-start(f32[1,384]{1,0:T(1,128)S(1)} %slice_bitcast_fusion), channel_id=1, source_target_pairs={{16,0},{32,16},{48,32},{64,48},{80,64},{96,80},{112,96},{128,112},... | collective-permute-start | bytes 4616 | tf_op jit(solution)/shard_map/ppermute | solution.py:372
  10.7 6.7 %collective-permute-start.1 = (f32[2,384]{1,0:T(2,128)S(1)}, f32[2,384]{1,0:T(2,128)S(1)}, u32[]{:S(2)}, u32[]{:S(2)}) collective-permute-start(f32[2,384]{1,0:T(2,128)S(1)} %bitcast.44), channel_id=1, source_target_pairs={{0,16},{16,32},{32,48},{48,64},{64,80},{80,96},{96,112},{112,128},... | collective-permute-start | bytes 9224 | tf_op jit(solution)/shard_map/ppermute | solution.py:372

commit v6 on v5

--- a/solution.py
+++ b/solution.py
@@ -15,9 +15,9 @@
 ADJOINT_UNROLL = 8
 ADJOINT_PARTS = 4
 APPLY_UNROLL = 8
-CHUNKS = 4
-STREAMING_LIMIT = 50 * 1024 * 1024
+EARLY_COPY_FLOPS = 2 * 10**10
 F32 = jnp.float32
+
 
 VMEM = pl.BlockSpec(memory_space=pltpu.VMEM)
 
@@ -85,7 +85,6 @@
 
 
 def feeder_adjoint(values, table, spread, sums):
-    adjoint_start(sums)
     adjoint_loop(values, table, spread, sums, 0, values.shape[0])
     return adjoint_total(sums)
 
@@ -144,20 +143,20 @@
     return copy
 
 
-def first_kernel(dims, first_rows, chunks, duals, inputs, values_in, table_in, slots, duals_t, limits_t, pushed_out,
-                 values, spread, *rest):
-    pieces, groups = dims
-    *sums, sems, table, sem = rest
+def edges_kernel(inputs, top, bottom):
+    last = inputs.shape[1] - 1
+    top[...] = inputs[DYN, :1, :]
+    bottom[:1, :] = inputs[CHARGE, last:, :]
+    bottom[1:, :] = inputs[DYN, last:, :]
+
+
+def first_kernel(dims, first_rows, duals, inputs, values, table_in, slots, duals_t, limits_t, pushed_out,
+                 spread, *rest):
+    pieces, groups = dims
+    *sums, table, sem = rest
     load = table_load(table_in, table, sem)
     blocks, blk = values.shape[:2]
     feeds = duals.shape[1]
-    size = blocks // chunks
-    copies = [
-        pltpu.make_async_copy(values_in.at[pl.ds(k * size, size)], values.at[pl.ds(k * size, size)], sems.at[k])
-        for k in range(chunks)
-    ]
-    for copy in copies:
-        copy.start()
     for i, target in enumerate((duals_t, limits_t)):
         padded = jnp.concatenate([duals[i], jnp.zeros((blk - feeds, LANES), F32)], axis=0)
         target[...] = jnp.transpose(padded)
@@ -169,9 +168,7 @@
             slots[pl.ds(slot * pieces + i, groups, stride=first_rows), :] = inputs[array, :, i * LANES : (i + 1) * LANES]
     adjoint_start(sums)
     load.wait()
-    for k, copy in enumerate(copies):
-        copy.wait()
-        adjoint_loop(values, table, spread, sums, k * size, (k + 1) * size)
+    adjoint_loop(values, table, spread, sums, 0, blocks)
     pushed = adjoint_total(sums)
     pushed_out[...] = pushed
     put_row(slots, SLOT_PUSHED, pushed, pieces, groups, first_rows)
@@ -221,13 +218,15 @@
     return new
 
 
-def feeder_part(dims, slot_rows, weight, primal, dual, bar, dyn, duals_t, limits_t, values, table,
+def feeder_part(dims, slot_rows, load, weight, primal, dual, bar, dyn, duals_t, limits_t, values, table,
                 duals_out, pushed_out, slots, spread, sums):
     pieces, groups = dims
     _, core, bat = places()
+    load.wait()
     new = feeder_duals(values, table, bar, weight, duals_t[...], limits_t[...], spread)
     duals_out[...] = new
     parts = pack_sums(primal, dual + row_sum((new - duals_t[...]) ** 2))
+    adjoint_start(sums)
     slots[...] = jnp.zeros_like(slots)
     own, other = slots.at[core], slots.at[1 - core]
     for side in (own, other):
@@ -257,8 +256,7 @@
     power_row[...] = row_power(dims, first_rows, weight[...], first,
                                take_row(first, SLOT_POWER, pieces, groups, first_rows),
                                take_row(first, SLOT_DYN, pieces, groups, first_rows), pushed_row[...], bar)
-    load.wait()
-    feeder_part(dims, slot_rows, weight[...], primal, dual, bar, dyn_out, duals_t, limits_t, values, table,
+    feeder_part(dims, slot_rows, load, weight[...], primal, dual, bar, dyn_out, duals_t, limits_t, values, table,
                 duals_out, pushed_out, slots, spread, sums)
 
 
@@ -297,8 +295,7 @@
                               (power_out, charge_out, dyn_out), edge_out)
     power_row[...] = row_power(dims, first_rows, weight[...], first, row_in[...],
                                take_row(own, SLOT_DYN, *dims, slot_rows), pushed_row[...], bar)
-    load.wait()
-    feeder_part(dims, slot_rows, weight[...], primal, dual, bar, dyn_out, duals_t, limits_t, values, table,
+    feeder_part(dims, slot_rows, load, weight[...], primal, dual, bar, dyn_out, duals_t, limits_t, values, table,
                 duals_out, pushed_out, slots, spread, sums)
 
 
@@ -388,7 +385,6 @@
     row, line, square, own = (pieces * groups, LANES), (1, LANES), (blk, LANES), (groups, local)
     spread, sums = (feeds, blk, LANES), (pieces * groups, 8, LANES)
     matrix_specs = [VMEM, VMEM]
-    chunks = unrolled(blocks, CHUNKS)
     work, moved = 2 * blocks * blk * LANES, 4 * blocks * blk * LANES
 
     inputs = stacked(power0, charge0, dyn_dual0, price, inflow, power_limit, capacity)
@@ -399,12 +395,13 @@
     row_of = jnp.sum((index_all >= block_offsets[None, 1:-1]).astype(jnp.int32), axis=1)
     matrix = (block_values, jnp.concatenate([row_of, (block_cols % pieces) * groups + block_cols // pieces]))
 
-    after = moved_to(inputs[DYN, :1], ("z", "core"), -1)
-    before = moved_to(inputs[CHARGE : DYN + 1, -1], ("z", "core"), 1)
+    top, bottom = call(edges_kernel, "edges", [VMEM], [(1, local), (2, local)], flops=EARLY_COPY_FLOPS)(inputs)
+    after = moved_to(top, ("z", "core"), -1)
+    before = moved_to(bottom, ("z", "core"), 1)
     first, duals_t, limits_t, pushed = call(
-        functools.partial(first_kernel, dims, first_rows, chunks), "first",
-        [VMEM, VMEM, pl.BlockSpec(memory_space=pl.ANY), VMEM], [(groups * first_rows, LANES), square, square, row],
-        [block_values.shape, spread] + [sums] * ADJOINT_PARTS, work, moved, STREAMING_LIMIT, chunks, 2 * blocks,
+        functools.partial(first_kernel, dims, first_rows), "first",
+        [VMEM] * 4, [(groups * first_rows, LANES), square, square, row],
+        [spread] + [sums] * ADJOINT_PARTS, work, moved, table=2 * blocks,
     )(duals, inputs, *matrix)
     first, after, before = lax.optimization_barrier((first, after, before))
     first = exchange(first.reshape(groups, first_rows, LANES), "bat").reshape(groups * first_rows, LANES)

time: 129 us -> 128 us (level)
  blocking collectives: 100 us -> 102 us
  other arithmetic: 2.84 us -> 1.3 us
  Pallas kernels: 13.9 us -> 12.5 us
    pallas_call x1 -> x2, Pallas kernels: 2.99 us -> 1.33 us  [the longest x1 1.33 us: shards(): call(functools.partial(first_kernel, dims, first_rows), 'first', [VMEM] *...]
    all_to_all x7, blocking collectives: 100 us -> 102 us  [exchange(): return lax.all_to_all(value, axis, 0, 0, tiled=True)]
  transfers between devices with their start and end apart: 2 -> 2, of which waited for: 0 -> 0; matrix products, arithmetic and copies ran while one was open for 1% -> 0% of each run, Pallas kernels for 2% -> 1%
where the time goes in v6:
time: 128 us; the launch traced here: 127 us
  blocking collectives  102 us (80%)
  Pallas kernels  12.5 us (10%)
  starting transfers between devices  11 us (9%)
  other arithmetic  1.3 us (1%)
    all_to_all x7, blocking collectives, exchange(): return lax.all_to_all(value, axis, 0, 0, tiled=True)  102 us
    ppermute x2, starting transfers between devices, moved_to(): lax.ppermute(value, axis, [(i, i + distance) for i in range(count) if 0 <...  11 us
    pallas_call x3, Pallas kernels, shards(): call(functools.partial(last_kernel if last else step_kernel, *sizes), 'la...  8.4 us
    pallas_call x1, Pallas kernels, shards(): call(functools.partial(step_one_kernel, *sizes), 'step_one', [VMEM] * 7 +...  2.75 us
  transfers between devices with their start and end apart: 2, of which 0 were waited for; matrix products, arithmetic and copies ran while one was open for 0% of the time, Pallas kernels for 1%

profile of v6, /device:TPU:1, one launch (start us, length us, event | category | flops | bytes accessed | tf_op | source)
XLA Modules:
  0.0 127.2 jit_solution(15464258467642203615)
XLA Ops:
  0.7 0.9 select_select_fusion.inputs
  1.6 0.0 copy-start.3
  1.6 0.0 copy-start.4
  1.6 0.0 copy-start.1
  1.7 0.0 copy-start.2
  1.7 0.0 copy-start
  1.7 9.1 %collective-permute-start = (f32[1,384]{1,0:T(1,128)S(1)}, f32[1,384]{1,0:T(1,128)S(1)}, u32[]{:S(2)}, u32[]{:S(2)}) collective-permute-start(f32[1,384]{1,0:T(1,128)S(1)} %get-tuple-element.45), channel_id=1, source_target_pairs={{16,0},{32,16},{48,32},{64,48},{80,64},{96,80},{112,96},{128,112},... | collective-permute-start | bytes 4616 | tf_op jit(solution)/shard_map/ppermute | solution.py:369
  10.8 1.9 %collective-permute-start.1 = (f32[2,384]{1,0:T(2,128)S(1)}, f32[2,384]{1,0:T(2,128)S(1)}, u32[]{:S(2)}, u32[]{:S(2)}) collective-permute-start(f32[2,384]{1,0:T(2,128)S(1)} %get-tuple-element.46), channel_id=1, source_target_pairs={{0,16},{16,32},{32,48},{48,64},{64,80},{80,96},{96,112},{112,128},... | collective-permute-start | bytes 9224 | tf_op jit(solution)/shard_map/ppermute | solution.py:369
  12.7 0.0 copy-done.3
  12.7 0.0 copy-done.4
  12.7 0.1 pad_add_fusion.1
  12.8 0.1 slice.8
  12.9 0.1 convert_reduce_fusion
  13.0 0.0 copy-done.1
  13.0 0.0 copy-done.2
  13.0 0.1 broadcast_select_fusion.duals
  13.1 0.1 pad_add_fusion.table_in
  13.1 0.0 copy-done
  13.1 1.3 %first.1 = (f32[256,128]{1,0:T(8,128)S(1)}, f32[128,128]{1,0:T(8,128)S(1)}, f32[128,128]{1,0:T(8,128)S(1)}, f32[48,128]{1,0:T(8,128)S(1)}) custom-call(f32[2,24,128]{2,1,0:T(8,128)S(1)} %broadcast_select_fusion.duals, f32[7,16,384]{2,1,0:T(8,128)S(1)} %select_select_fusion.inputs, f32[72,128,128]{2,1,0:T(8,128)S(1)} %copy-done, s32[144]{0:T(256)S(1)} %pad_add_fusion.table_in), custom_call_target="tpu_custom_call" | custom-call | flops 2359296 | bytes 4718592 | tf_op jit(solution)/shard_map/first/pallas_call | solution.py:401
  14.5 0.0 collective-permute-done.after
  14.5 0.0 collective-permute-done.1.before
  14.5 9.5 %all_to_all.35 = f32[16,16,128]{2,1,0:T(8,128)S(1)} all-to-all(f32[16,16,128]{2,1,0:T(8,128)S(1)} %bitcast.35), channel_id=1, replica_groups=mesh['z'=16,'core'=2,'bat'=16] {'bat'}, dimensions={0} | all-to-all | bytes 262144 | tf_op jit(solution)/shard_map/all_to_all | solution.py:373
  24.0 2.8 %step_one.1 = (f32[1,128]{1,0:T(1,128)S(1)}, f32[48,128]{1,0:T(8,128)S(1)}, f32[16,384]{1,0:T(8,128)S(1)}, f32[16,384]{1,0:T(8,128)S(1)}, f32[16,384]{1,0:T(8,12...) custom-call(f32[256,128]{1,0:T(8,128)S(1)} %bitcast.17, ...), custom_call_target="tpu_custom_call" | custom-call | flops 4718592 | bytes 4718592 | tf_op jit(solution)/shard_map/step_one/pallas_call | solution.py:417
  26.8 12.2 %all_to_all.36 = f32[32,8,128]{2,1,0:T(8,128)S(1)} all-to-all(f32[32,8,128]{2,1,0:T(8,128)S(1)} %bitcast.36), channel_id=1, replica_groups=mesh['z'=16,'core'=2,'bat'=16] {'core','bat'}, dimensions={0} | all-to-all | bytes 262144 | tf_op jit(solution)/shard_map/all_to_all | solution.py:373
  39.0 27.0 %all_to_all.37 = f32[16,4,128]{2,1,0:T(4,128)S(1)} all-to-all(f32[16,4,128]{2,1,0:T(4,128)S(1)} %bitcast.30), channel_id=1, replica_groups=mesh['z'=16,'core'=2,'bat'=16] {'z'}, dimensions={0} | all-to-all | bytes 65536 | tf_op jit(solution)/shard_map/all_to_all | solution.py:373
  66.0 3.0 %step.2 = (f32[1,128]{1,0:T(1,128)S(1)}, f32[48,128]{1,0:T(8,128)S(1)}, f32[16,384]{1,0:T(8,128)S(1)}, f32[16,384]{1,0:T(8,128)S(1)}, f32[16,384]{1,0:T(8,128)S(...) custom-call(f32[256,128]{1,0:T(8,128)S(1)} %bitcast.18, ...), custom_call_target="tpu_custom_call" | custom-call | flops 4718592 | bytes 4718592 | tf_op jit(solution)/shard_map/step/pallas_call | solution.py:422
  68.9 12.6 %all_to_all.38 = f32[32,8,128]{2,1,0:T(8,128)S(1)} all-to-all(f32[32,8,128]{2,1,0:T(8,128)S(1)} %bitcast.33), channel_id=1, replica_groups=mesh['z'=16,'core'=2,'bat'=16] {'core','bat'}, dimensions={0} | all-to-all | bytes 262144 | tf_op jit(solution)/shard_map/all_to_all | solution.py:373
  81.5 14.0 %all_to_all.39 = f32[16,4,128]{2,1,0:T(4,128)S(1)} all-to-all(f32[16,4,128]{2,1,0:T(4,128)S(1)} %bitcast.31), channel_id=1, replica_groups=mesh['z'=16,'core'=2,'bat'=16] {'z'}, dimensions={0} | all-to-all | bytes 65536 | tf_op jit(solution)/shard_map/all_to_all | solution.py:373
  95.5 3.0 %step.3 = (f32[1,128]{1,0:T(1,128)S(1)}, f32[48,128]{1,0:T(8,128)S(1)}, f32[16,384]{1,0:T(8,128)S(1)}, f32[16,384]{1,0:T(8,128)S(1)}, f32[16,384]{1,0:T(8,128)S(...) custom-call(f32[256,128]{1,0:T(8,128)S(1)} %bitcast.19, ...), custom_call_target="tpu_custom_call" | custom-call | flops 4718592 | bytes 4718592 | tf_op jit(solution)/shard_map/step/pallas_call | solution.py:422
  98.5 12.3 %all_to_all.40 = f32[32,8,128]{2,1,0:T(8,128)S(1)} all-to-all(f32[32,8,128]{2,1,0:T(8,128)S(1)} %bitcast.34), channel_id=1, replica_groups=mesh['z'=16,'core'=2,'bat'=16] {'core','bat'}, dimensions={0} | all-to-all | bytes 262144 | tf_op jit(solution)/shard_map/all_to_all | solution.py:373
  110.8 14.0 %all_to_all.41 = f32[16,4,128]{2,1,0:T(4,128)S(1)} all-to-all(f32[16,4,128]{2,1,0:T(4,128)S(1)} %bitcast.32), channel_id=1, replica_groups=mesh['z'=16,'core'=2,'bat'=16] {'z'}, dimensions={0} | all-to-all | bytes 65536 | tf_op jit(solution)/shard_map/all_to_all | solution.py:373
  124.8 2.5 %last.1 = (f32[16,384]{1,0:T(8,128)}, f32[16,384]{1,0:T(8,128)}, f32[16,384]{1,0:T(8,128)}, f32[24,128]{1,0:T(8,128)}) custom-call(f32[256,128]{1,0:T(8,128)S(1)} %bitcast.20, f32[2,128,128]{2,1,0:T(8,128)S(1)} %bitcast.26, f32[64,128]{1,0:T(8,128)S(1)} %bitcast.29, f32[1,128]{1,0:T(1,128)S(1)} %get-tuple-element.72.weight_in, ...), custom_call_target="tpu_custom_call" | custom-call | flops 4718592 | bytes 4718592 | tf_op jit(solution)/shard_map/last/pallas_call | solution.py:422
  (9 shorter events, 0.1 us)
Async XLA Ops:
  1.6 11.1 %copy-start.3 = (s32[25]{0:T(128)S(1)}, s32[25]{0:T(128)}, u32[]{:S(2)}) copy-start(s32[25]{0:T(128)} %param.23) | copy-start | bytes 304
  1.6 11.1 %copy-start.4 = (s32[72]{0:T(128)S(1)}, s32[72]{0:T(128)}, u32[]{:S(2)}) copy-start(s32[72]{0:T(128)} %param.22) | copy-start | bytes 868
  1.6 11.3 %copy-start.1 = (f32[3072]{0:T(1024)S(1)}, f32[3072]{0:T(1024)}, u32[]{:S(2)}) copy-start(f32[3072]{0:T(1024)} %param.20) | copy-start | bytes 36868
  1.7 11.3 %copy-start.2 = (f32[1,3072]{1,0:T(1,128)S(1)}, f32[1,3072]{1,0:T(1,128)}, u32[]{:S(2)}) copy-start(f32[1,3072]{1,0:T(1,128)} %param.15) | copy-start | bytes 36868
  1.7 11.5 %copy-start = (f32[72,128,128]{2,1,0:T(8,128)S(1)}, f32[72,128,128]{2,1,0:T(8,128)}, u32[]{:S(2)}) copy-start(f32[72,128,128]{2,1,0:T(8,128)} %values.9) | copy-start | bytes 14155780
  1.7 12.8 %collective-permute-start = (f32[1,384]{1,0:T(1,128)S(1)}, f32[1,384]{1,0:T(1,128)S(1)}, u32[]{:S(2)}, u32[]{:S(2)}) collective-permute-start(f32[1,384]{1,0:T(1,128)S(1)} %get-tuple-element.45), channel_id=1, source_target_pairs={{16,0},{32,16},{48,32},{64,48},{80,64},{96,80},{112,96},{128,112},... | collective-permute-start | bytes 4616 | tf_op jit(solution)/shard_map/ppermute | solution.py:369
  10.8 3.7 %collective-permute-start.1 = (f32[2,384]{1,0:T(2,128)S(1)}, f32[2,384]{1,0:T(2,128)S(1)}, u32[]{:S(2)}, u32[]{:S(2)}) collective-permute-start(f32[2,384]{1,0:T(2,128)S(1)} %get-tuple-element.46), channel_id=1, source_target_pairs={{0,16},{16,32},{32,48},{48,64},{64,80},{80,96},{96,112},{112,128},... | collective-permute-start | bytes 9224 | tf_op jit(solution)/shard_map/ppermute | solution.py:369

commit v7 on v6

--- a/solution.py
+++ b/solution.py
@@ -12,7 +12,7 @@
 EPS_NORM = 1e-06
 LANES = 128
 HALF = LANES // 2
-ADJOINT_UNROLL = 8
+ADJOINT_UNROLL = 24
 ADJOINT_PARTS = 4
 APPLY_UNROLL = 8
 EARLY_COPY_FLOPS = 2 * 10**10
@@ -89,29 +89,28 @@
     return adjoint_total(sums)
 
 
-def feeder_duals(values, table, field, weight, duals_t, limits_t, spread):
+def feeder_duals(values, table, load, field, weight, duals_t, limits_t, spread):
     blocks, blk = values.shape[:2]
     feeds = spread.shape[0]
     ways = unrolled(blocks, APPLY_UNROLL)
-
-    def step(k, acc):
+    step_dual = ETA_STEP * weight[:, :1]
+    shifted = duals_t - step_dual * limits_t
+    lane = lane_iota((blk, LANES))
+    for f in range(feeds):
+        spread[f] = jnp.where(lane == f, shifted, 0.0)
+    load.wait()
+
+    def step(k, carry):
         for u in range(ways):
             j = k * ways + u
             f = table[j]
-            before = table[jnp.maximum(j - 1, 0)]
-            keep = jnp.where(f == before, 1.0, 0.0).astype(F32)
-            acc = acc * keep + values[j] * field[pl.ds(table[blocks + j], 1), :]
-            spread[f] = acc
-        return acc
-
-    lax.fori_loop(0, blocks // ways, step, jnp.zeros((blk, LANES), F32))
-    step_dual = ETA_STEP * weight[:, :1]
-    shifted = duals_t - step_dual * limits_t
-    lane = lane_iota((blk, LANES))
+            spread[f] = spread[f] + values[j] * field[pl.ds(table[blocks + j], 1), :]
+        return carry
+
+    lax.fori_loop(0, blocks // ways, step, 0)
     new = jnp.zeros((blk, LANES), F32)
     for f in range(feeds):
-        moved = spread[f] + jnp.where(lane == f, shifted, 0.0)
-        dual = jnp.maximum(0.0, jnp.sum(moved, axis=1, keepdims=True))
+        dual = jnp.maximum(0.0, jnp.sum(spread[f], axis=1, keepdims=True))
         spread[f] = jnp.broadcast_to(dual, (blk, LANES))
         new = jnp.where(lane == f, dual, new)
     return new
@@ -143,11 +142,10 @@
     return copy
 
 
-def edges_kernel(inputs, top, bottom):
+def edges_kernel(inputs, edges):
     last = inputs.shape[1] - 1
-    top[...] = inputs[DYN, :1, :]
-    bottom[:1, :] = inputs[CHARGE, last:, :]
-    bottom[1:, :] = inputs[DYN, last:, :]
+    edges[:1, :] = jnp.where(lax.axis_index("core") == 0, inputs[DYN, :1, :], inputs[DYN, last:, :])
+    edges[1:, :] = inputs[CHARGE, last:, :]
 
 
 def first_kernel(dims, first_rows, duals, inputs, values, table_in, slots, duals_t, limits_t, pushed_out,
@@ -163,15 +161,21 @@
     for f in range(feeds):
         spread[f] = jnp.broadcast_to(duals_t[:, f : f + 1], (blk, LANES))
     sent = ((SLOT_DYN, DYN), (SLOT_POWER, POWER), (SLOT_PRICE, PRICE), (SLOT_LIMIT, LIMIT))
+    _, core, bat = places()
+    slots[...] = jnp.zeros_like(slots)
+    own, other = slots.at[core], slots.at[1 - core]
     for i in range(pieces):
+        cut = slice(i * LANES, (i + 1) * LANES)
         for slot, array in sent:
-            slots[pl.ds(slot * pieces + i, groups, stride=first_rows), :] = inputs[array, :, i * LANES : (i + 1) * LANES]
+            own[pl.ds(slot * pieces + i, groups, stride=first_rows), :] = inputs[array, :, cut]
+        for k, (array, line) in enumerate(((DYN, 0), (DYN, groups - 1), (CHARGE, groups - 1))):
+            other[pl.ds(bat * first_rows + k * pieces + i, 1), :] = inputs[array, line : line + 1, cut]
     adjoint_start(sums)
     load.wait()
     adjoint_loop(values, table, spread, sums, 0, blocks)
     pushed = adjoint_total(sums)
     pushed_out[...] = pushed
-    put_row(slots, SLOT_PUSHED, pushed, pieces, groups, first_rows)
+    put_row(own, SLOT_PUSHED, pushed, pieces, groups, first_rows)
 
 
 def local_step(dims, slot_rows, weight, received, inputs, state, edges, state_out, edge_out):
@@ -222,8 +226,7 @@
                 duals_out, pushed_out, slots, spread, sums):
     pieces, groups = dims
     _, core, bat = places()
-    load.wait()
-    new = feeder_duals(values, table, bar, weight, duals_t[...], limits_t[...], spread)
+    new = feeder_duals(values, table, load, bar, weight, duals_t[...], limits_t[...], spread)
     duals_out[...] = new
     parts = pack_sums(primal, dual + row_sum((new - duals_t[...]) ** 2))
     adjoint_start(sums)
@@ -241,7 +244,7 @@
     put_row(own, SLOT_PUSHED, pushed, pieces, groups, slot_rows)
 
 
-def step_one_kernel(dims, first_rows, slot_rows, first, after, before, pushed_row, inputs, duals_t, limits_t, values,
+def step_one_kernel(dims, first_rows, slot_rows, first, across, pushed_row, inputs, duals_t, limits_t, values,
                     table_in, weight, power_row, power_out, charge_out, dyn_out, edge_out, duals_out, pushed_out, slots,
                     bar, spread, *rest):
     *sums, table, sem = rest
@@ -249,13 +252,20 @@
     load = table_load(table_in, table, sem)
     weight[...] = jnp.ones_like(weight)
     state = [lambda cut, array=array: inputs[array, :, cut] for array in (POWER, CHARGE, DYN)]
-    edges = [lambda i, ref=ref, k=k: ref[k : k + 1, i * LANES : (i + 1) * LANES]
-             for ref, k in ((after, 0), (before, 1), (before, 0))]
-    primal, dual = local_step(dims, first_rows, weight[...], first, inputs, state, edges,
+    _, core, bat = places()
+    own, other = first.at[core], first.at[1 - core]
+    linked = lambda k, i: across[k : k + 1, i * LANES : (i + 1) * LANES]
+    partner = lambda k, i: other[pl.ds(bat * first_rows + k * pieces + i, 1), :]
+    edges = (
+        lambda i: jnp.where(core == 0, partner(0, i), linked(0, i)),
+        lambda i: jnp.where(core == 0, linked(0, i), partner(1, i)),
+        lambda i: jnp.where(core == 0, linked(1, i), partner(2, i)),
+    )
+    primal, dual = local_step(dims, first_rows, weight[...], own, inputs, state, edges,
                               (power_out, charge_out, dyn_out), edge_out)
-    power_row[...] = row_power(dims, first_rows, weight[...], first,
-                               take_row(first, SLOT_POWER, pieces, groups, first_rows),
-                               take_row(first, SLOT_DYN, pieces, groups, first_rows), pushed_row[...], bar)
+    power_row[...] = row_power(dims, first_rows, weight[...], own,
+                               take_row(own, SLOT_POWER, pieces, groups, first_rows),
+                               take_row(own, SLOT_DYN, pieces, groups, first_rows), pushed_row[...], bar)
     feeder_part(dims, slot_rows, load, weight[...], primal, dual, bar, dyn_out, duals_t, limits_t, values, table,
                 duals_out, pushed_out, slots, spread, sums)
 
@@ -293,7 +303,7 @@
     primal, dual = local_step(dims, slot_rows, weight[...], own, inputs, state,
                               later_edges(dims, slot_rows, received, parts, edge_in),
                               (power_out, charge_out, dyn_out), edge_out)
-    power_row[...] = row_power(dims, first_rows, weight[...], first, row_in[...],
+    power_row[...] = row_power(dims, first_rows, weight[...], first.at[lax.axis_index("core")], row_in[...],
                                take_row(own, SLOT_DYN, *dims, slot_rows), pushed_row[...], bar)
     feeder_part(dims, slot_rows, load, weight[...], primal, dual, bar, dyn_out, duals_t, limits_t, values, table,
                 duals_out, pushed_out, slots, spread, sums)
@@ -308,10 +318,9 @@
     state = [lambda cut, ref=ref: ref[:, cut] for ref in (power, charge, dyn)]
     local_step(dims, slot_rows, weight, own, inputs, state, later_edges(dims, slot_rows, received, parts, edge_in),
                (power_out, charge_out, dyn_out), None)
-    row_power(dims, first_rows, weight, first, row_in[...], take_row(own, SLOT_DYN, *dims, slot_rows),
+    row_power(dims, first_rows, weight, first.at[lax.axis_index("core")], row_in[...], take_row(own, SLOT_DYN, *dims, slot_rows),
               pushed_row[...], bar)
-    load.wait()
-    new = feeder_duals(values, table, bar, weight, duals_t[...], limits_t[...], spread)
+    new = feeder_duals(values, table, load, bar, weight, duals_t[...], limits_t[...], spread)
     duals_out[...] = jnp.transpose(new)[: duals_out.shape[0]]
 
 
@@ -364,11 +373,6 @@
     return out
 
 
-def moved_to(value, axis, distance):
-    count = lax.axis_size(axis)
-    return lax.ppermute(value, axis, [(i, i + distance) for i in range(count) if 0 <= i + distance < count])
-
-
 def exchange(value, axis):
     return lax.all_to_all(value, axis, 0, 0, tiled=True)
 
@@ -395,16 +399,17 @@
     row_of = jnp.sum((index_all >= block_offsets[None, 1:-1]).astype(jnp.int32), axis=1)
     matrix = (block_values, jnp.concatenate([row_of, (block_cols % pieces) * groups + block_cols // pieces]))
 
-    top, bottom = call(edges_kernel, "edges", [VMEM], [(1, local), (2, local)], flops=EARLY_COPY_FLOPS)(inputs)
-    after = moved_to(top, ("z", "core"), -1)
-    before = moved_to(bottom, ("z", "core"), 1)
+    edges = call(edges_kernel, "edges", [VMEM], [(2, local)], flops=EARLY_COPY_FLOPS)(inputs)[0]
+    links = [(i, i + 1 if i % 2 else i - 1) for i in range(1, 2 * chips - 1)]
+    across = lax.ppermute(edges, ("z", "core"), links)
     first, duals_t, limits_t, pushed = call(
         functools.partial(first_kernel, dims, first_rows), "first",
-        [VMEM] * 4, [(groups * first_rows, LANES), square, square, row],
+        [VMEM] * 4, [(2, groups * first_rows, LANES), square, square, row],
         [spread] + [sums] * ADJOINT_PARTS, work, moved, table=2 * blocks,
     )(duals, inputs, *matrix)
-    first, after, before = lax.optimization_barrier((first, after, before))
-    first = exchange(first.reshape(groups, first_rows, LANES), "bat").reshape(groups * first_rows, LANES)
+    first, across = lax.optimization_barrier((first, across))
+    first = exchange(first.reshape(2 * groups, first_rows, LANES), ("core", "bat"))
+    first = first.reshape(2, groups * first_rows, LANES)
 
     both = (2, groups * slot_rows, LANES)
     step_outs = [line, row] + [own] * 3 + [(1, local), square, row, both]
@@ -415,9 +420,9 @@
         sizes = (dims, first_rows, slot_rows)
         if iteration == 0:
             results = call(
-                functools.partial(step_one_kernel, *sizes), "step_one", [VMEM] * 7 + matrix_specs, outs, scratch,
+                functools.partial(step_one_kernel, *sizes), "step_one", [VMEM] * 6 + matrix_specs, outs, scratch,
                 2 * work, moved, table=2 * blocks,
-            )(first, after, before, pushed, inputs, duals_t, limits_t, *matrix)
+            )(first, across, pushed, inputs, duals_t, limits_t, *matrix)
         else:
             results = call(
                 functools.partial(last_kernel if last else step_kernel, *sizes), "last" if last else "step",

time: 128 us -> 126 us (0.984)
  starting transfers between devices: 11 us -> 5.2 us
  blocking collectives: 102 us -> 107 us
  Pallas kernels: 12.5 us -> 10.9 us
    ppermute x2 -> x1, starting transfers between devices: 11 us -> 5.2 us  [shards(): across = lax.ppermute(edges, ('z', 'core'), links)]
    all_to_all x7, blocking collectives: 102 us -> 107 us  [exchange(): return lax.all_to_all(value, axis, 0, 0, tiled=True)]
  transfers between devices with their start and end apart: 2 -> 1, of which waited for: 0 -> 0; matrix products, arithmetic and copies ran while one was open for 0% -> 0% of each run, Pallas kernels for 1% -> 1%
where the time goes in v7:
time: 126 us; the launch traced here: 125 us
  blocking collectives  107 us (85%)
  Pallas kernels  10.9 us (9%)
  starting transfers between devices  5.2 us (4%)
  other arithmetic  1.3 us (1%)
    all_to_all x7, blocking collectives, exchange(): return lax.all_to_all(value, axis, 0, 0, tiled=True)  107 us
    pallas_call x3, Pallas kernels, shards(): call(functools.partial(last_kernel if last else step_kernel, *sizes), 'la...  7.17 us
    ppermute x1, starting transfers between devices, shards(): across = lax.ppermute(edges, ('z', 'core'), links)  5.2 us
  transfers between devices with their start and end apart: 1, of which 0 were waited for; matrix products, arithmetic and copies ran while one was open for 0% of the time, Pallas kernels for 1%

profile of v7, /device:TPU:1, one launch (start us, length us, event | category | flops | bytes accessed | tf_op | source)
XLA Modules:
  0.0 125.1 jit_solution(10682957615560764551)
XLA Ops:
  0.7 0.9 select_select_fusion.inputs
  1.6 0.0 copy-start.3
  1.6 0.0 copy-start.4
  1.6 0.0 copy-start.1
  1.7 0.0 copy-start.2
  1.7 0.0 copy-start
  1.7 5.2 %collective-permute-start = (f32[2,384]{1,0:T(2,128)S(1)}, f32[2,384]{1,0:T(2,128)S(1)}, u32[]{:S(2)}, u32[]{:S(2)}) collective-permute-start(f32[2,384]{1,0:T(2,128)S(1)} %edges.1), channel_id=1, source_target_pairs={{16,32},{32,16},{48,64},{64,48},{80,96},{96,80},{112,128},{128,112... | collective-permute-start | bytes 9224 | tf_op jit(solution)/shard_map/ppermute | solution.py:404
  6.9 0.0 copy-done.3
  6.9 0.0 copy-done.4
  6.9 0.1 pad_add_fusion.1
  7.0 0.1 slice.8
  7.1 0.1 convert_reduce_fusion
  7.2 0.0 copy-done.1
  7.2 0.0 copy-done.2
  7.2 0.1 broadcast_select_fusion.duals
  7.3 0.1 pad_add_fusion.table_in
  7.4 0.0 copy-done
  7.4 1.3 %first.1 = (f32[2,256,128]{2,1,0:T(8,128)S(1)}, f32[128,128]{1,0:T(8,128)S(1)}, f32[128,128]{1,0:T(8,128)S(1)}, f32[48,128]{1,0:T(8,128)S(1)}) custom-call(f32[2,24,128]{2,1,0:T(8,128)S(1)} %broadcast_select_fusion.duals, f32[7,16,384]{2,1,0:T(8,128)S(1)} %select_select_fusion.inputs, f32[72,128,128]{2,1,0:T(8,128)S(1)} %copy-done, s32[144]{0:T(256)S(1)} %pad_add_fusion.table_in), custom_call_target="tpu_custom_call" | custom-call | flops 2359296 | bytes 4718592 | tf_op jit(solution)/shard_map/first/pallas_call | solution.py:405
  8.7 0.0 collective-permute-done.across
  8.7 15.3 %all_to_all.35 = f32[32,16,128]{2,1,0:T(8,128)S(1)} all-to-all(f32[32,16,128]{2,1,0:T(8,128)S(1)} %bitcast.27), channel_id=1, replica_groups=mesh['z'=16,'core'=2,'bat'=16] {'core','bat'}, dimensions={0} | all-to-all | bytes 524288 | tf_op jit(solution)/shard_map/all_to_all | solution.py:377
  24.0 2.4 %step_one.1 = (f32[1,128]{1,0:T(1,128)S(1)}, f32[48,128]{1,0:T(8,128)S(1)}, f32[16,384]{1,0:T(8,128)S(1)}, f32[16,384]{1,0:T(8,128)S(1)}, f32[16,384]{1,0:T(8,12...) custom-call(f32[2,256,128]{2,1,0:T(8,128)S(1)} %bitcast.17, ...), custom_call_target="tpu_custom_call" | custom-call | flops 4718592 | bytes 4718592 | tf_op jit(solution)/shard_map/step_one/pallas_call | solution.py:422
  26.4 11.6 %all_to_all.36 = f32[32,8,128]{2,1,0:T(8,128)S(1)} all-to-all(f32[32,8,128]{2,1,0:T(8,128)S(1)} %bitcast.36), channel_id=1, replica_groups=mesh['z'=16,'core'=2,'bat'=16] {'core','bat'}, dimensions={0} | all-to-all | bytes 262144 | tf_op jit(solution)/shard_map/all_to_all | solution.py:377
  38.0 27.0 %all_to_all.37 = f32[16,4,128]{2,1,0:T(4,128)S(1)} all-to-all(f32[16,4,128]{2,1,0:T(4,128)S(1)} %bitcast.31), channel_id=1, replica_groups=mesh['z'=16,'core'=2,'bat'=16] {'z'}, dimensions={0} | all-to-all | bytes 65536 | tf_op jit(solution)/shard_map/all_to_all | solution.py:377
  65.0 2.4 %step.2 = (f32[1,128]{1,0:T(1,128)S(1)}, f32[48,128]{1,0:T(8,128)S(1)}, f32[16,384]{1,0:T(8,128)S(1)}, f32[16,384]{1,0:T(8,128)S(1)}, f32[16,384]{1,0:T(8,128)S(...) custom-call(f32[2,256,128]{2,1,0:T(8,128)S(1)} %bitcast.18, ...), custom_call_target="tpu_custom_call" | custom-call | flops 4718592 | bytes 4718592 | tf_op jit(solution)/shard_map/step/pallas_call | solution.py:427
  67.5 12.6 %all_to_all.38 = f32[32,8,128]{2,1,0:T(8,128)S(1)} all-to-all(f32[32,8,128]{2,1,0:T(8,128)S(1)} %bitcast.34), channel_id=1, replica_groups=mesh['z'=16,'core'=2,'bat'=16] {'core','bat'}, dimensions={0} | all-to-all | bytes 262144 | tf_op jit(solution)/shard_map/all_to_all | solution.py:377
  80.1 14.0 %all_to_all.39 = f32[16,4,128]{2,1,0:T(4,128)S(1)} all-to-all(f32[16,4,128]{2,1,0:T(4,128)S(1)} %bitcast.32), channel_id=1, replica_groups=mesh['z'=16,'core'=2,'bat'=16] {'z'}, dimensions={0} | all-to-all | bytes 65536 | tf_op jit(solution)/shard_map/all_to_all | solution.py:377
  94.0 2.4 %step.3 = (f32[1,128]{1,0:T(1,128)S(1)}, f32[48,128]{1,0:T(8,128)S(1)}, f32[16,384]{1,0:T(8,128)S(1)}, f32[16,384]{1,0:T(8,128)S(1)}, f32[16,384]{1,0:T(8,128)S(...) custom-call(f32[2,256,128]{2,1,0:T(8,128)S(1)} %bitcast.19, ...), custom_call_target="tpu_custom_call" | custom-call | flops 4718592 | bytes 4718592 | tf_op jit(solution)/shard_map/step/pallas_call | solution.py:427
  96.5 12.3 %all_to_all.40 = f32[32,8,128]{2,1,0:T(8,128)S(1)} all-to-all(f32[32,8,128]{2,1,0:T(8,128)S(1)} %bitcast.35), channel_id=1, replica_groups=mesh['z'=16,'core'=2,'bat'=16] {'core','bat'}, dimensions={0} | all-to-all | bytes 262144 | tf_op jit(solution)/shard_map/all_to_all | solution.py:377
  108.8 14.0 %all_to_all.41 = f32[16,4,128]{2,1,0:T(4,128)S(1)} all-to-all(f32[16,4,128]{2,1,0:T(4,128)S(1)} %bitcast.33), channel_id=1, replica_groups=mesh['z'=16,'core'=2,'bat'=16] {'z'}, dimensions={0} | all-to-all | bytes 65536 | tf_op jit(solution)/shard_map/all_to_all | solution.py:377
  122.8 2.3 %last.1 = (f32[16,384]{1,0:T(8,128)}, f32[16,384]{1,0:T(8,128)}, f32[16,384]{1,0:T(8,128)}, f32[24,128]{1,0:T(8,128)}) custom-call(f32[2,256,128]{2,1,0:T(8,128)S(1)} %bitcast.20, f32[2,128,128]{2,1,0:T(8,128)S(1)} %bitcast.26, f32[64,128]{1,0:T(8,128)S(1)} %bitcast.30, f32[1,128]{1,0:T(1,128)S(1)} %get-tuple-element.66.weight_in, ...), custom_call_target="tpu_custom_call" | custom-call | flops 4718592 | bytes 4718592 | tf_op jit(solution)/shard_map/last/pallas_call | solution.py:427
  (9 shorter events, 0.1 us)
Async XLA Ops:
  1.6 5.3 %copy-start.3 = (s32[25]{0:T(128)S(1)}, s32[25]{0:T(128)}, u32[]{:S(2)}) copy-start(s32[25]{0:T(128)} %param.23) | copy-start | bytes 304
  1.6 5.3 %copy-start.4 = (s32[72]{0:T(128)S(1)}, s32[72]{0:T(128)}, u32[]{:S(2)}) copy-start(s32[72]{0:T(128)} %param.22) | copy-start | bytes 868
  1.6 5.5 %copy-start.1 = (f32[3072]{0:T(1024)S(1)}, f32[3072]{0:T(1024)}, u32[]{:S(2)}) copy-start(f32[3072]{0:T(1024)} %param.20) | copy-start | bytes 36868
  1.7 5.5 %copy-start.2 = (f32[1,3072]{1,0:T(1,128)S(1)}, f32[1,3072]{1,0:T(1,128)}, u32[]{:S(2)}) copy-start(f32[1,3072]{1,0:T(1,128)} %param.15) | copy-start | bytes 36868
  1.7 5.7 %copy-start = (f32[72,128,128]{2,1,0:T(8,128)S(1)}, f32[72,128,128]{2,1,0:T(8,128)}, u32[]{:S(2)}) copy-start(f32[72,128,128]{2,1,0:T(8,128)} %values.9) | copy-start | bytes 14155780
  1.7 7.0 %collective-permute-start = (f32[2,384]{1,0:T(2,128)S(1)}, f32[2,384]{1,0:T(2,128)S(1)}, u32[]{:S(2)}, u32[]{:S(2)}) collective-permute-start(f32[2,384]{1,0:T(2,128)S(1)} %edges.1), channel_id=1, source_target_pairs={{16,32},{32,16},{48,64},{64,48},{80,96},{96,80},{112,128},{128,112... | collective-permute-start | bytes 9224 | tf_op jit(solution)/shard_map/ppermute | solution.py:404

commit v8 on v7

--- a/solution.py
+++ b/solution.py
@@ -142,10 +142,12 @@
     return copy
 
 
-def edges_kernel(inputs, edges):
+def edges_kernel(inputs, edges, swapped):
     last = inputs.shape[1] - 1
     edges[:1, :] = jnp.where(lax.axis_index("core") == 0, inputs[DYN, :1, :], inputs[DYN, last:, :])
     edges[1:, :] = inputs[CHARGE, last:, :]
+    for k, (array, line) in enumerate(((DYN, 0), (DYN, last), (CHARGE, last))):
+        swapped[k : k + 1, :] = inputs[array, line : line + 1, :]
 
 
 def first_kernel(dims, first_rows, duals, inputs, values, table_in, slots, duals_t, limits_t, pushed_out,
@@ -161,21 +163,15 @@
     for f in range(feeds):
         spread[f] = jnp.broadcast_to(duals_t[:, f : f + 1], (blk, LANES))
     sent = ((SLOT_DYN, DYN), (SLOT_POWER, POWER), (SLOT_PRICE, PRICE), (SLOT_LIMIT, LIMIT))
-    _, core, bat = places()
-    slots[...] = jnp.zeros_like(slots)
-    own, other = slots.at[core], slots.at[1 - core]
     for i in range(pieces):
-        cut = slice(i * LANES, (i + 1) * LANES)
         for slot, array in sent:
-            own[pl.ds(slot * pieces + i, groups, stride=first_rows), :] = inputs[array, :, cut]
-        for k, (array, line) in enumerate(((DYN, 0), (DYN, groups - 1), (CHARGE, groups - 1))):
-            other[pl.ds(bat * first_rows + k * pieces + i, 1), :] = inputs[array, line : line + 1, cut]
+            slots[pl.ds(slot * pieces + i, groups, stride=first_rows), :] = inputs[array, :, i * LANES : (i + 1) * LANES]
     adjoint_start(sums)
     load.wait()
     adjoint_loop(values, table, spread, sums, 0, blocks)
     pushed = adjoint_total(sums)
     pushed_out[...] = pushed
-    put_row(own, SLOT_PUSHED, pushed, pieces, groups, first_rows)
+    put_row(slots, SLOT_PUSHED, pushed, pieces, groups, first_rows)
 
 
 def local_step(dims, slot_rows, weight, received, inputs, state, edges, state_out, edge_out):
@@ -244,7 +240,7 @@
     put_row(own, SLOT_PUSHED, pushed, pieces, groups, slot_rows)
 
 
-def step_one_kernel(dims, first_rows, slot_rows, first, across, pushed_row, inputs, duals_t, limits_t, values,
+def step_one_kernel(dims, first_rows, slot_rows, first, across, swapped, pushed_row, inputs, duals_t, limits_t, values,
                     table_in, weight, power_row, power_out, charge_out, dyn_out, edge_out, duals_out, pushed_out, slots,
                     bar, spread, *rest):
     *sums, table, sem = rest
@@ -252,20 +248,19 @@
     load = table_load(table_in, table, sem)
     weight[...] = jnp.ones_like(weight)
     state = [lambda cut, array=array: inputs[array, :, cut] for array in (POWER, CHARGE, DYN)]
-    _, core, bat = places()
-    own, other = first.at[core], first.at[1 - core]
+    core = lax.axis_index("core")
     linked = lambda k, i: across[k : k + 1, i * LANES : (i + 1) * LANES]
-    partner = lambda k, i: other[pl.ds(bat * first_rows + k * pieces + i, 1), :]
+    partner = lambda k, i: swapped[k : k + 1, i * LANES : (i + 1) * LANES]
     edges = (
         lambda i: jnp.where(core == 0, partner(0, i), linked(0, i)),
         lambda i: jnp.where(core == 0, linked(0, i), partner(1, i)),
         lambda i: jnp.where(core == 0, linked(1, i), partner(2, i)),
     )
-    primal, dual = local_step(dims, first_rows, weight[...], own, inputs, state, edges,
+    primal, dual = local_step(dims, first_rows, weight[...], first, inputs, state, edges,
                               (power_out, charge_out, dyn_out), edge_out)
-    power_row[...] = row_power(dims, first_rows, weight[...], own,
-                               take_row(own, SLOT_POWER, pieces, groups, first_rows),
-                               take_row(own, SLOT_DYN, pieces, groups, first_rows), pushed_row[...], bar)
+    power_row[...] = row_power(dims, first_rows, weight[...], first,
+                               take_row(first, SLOT_POWER, pieces, groups, first_rows),
+                               take_row(first, SLOT_DYN, pieces, groups, first_rows), pushed_row[...], bar)
     feeder_part(dims, slot_rows, load, weight[...], primal, dual, bar, dyn_out, duals_t, limits_t, values, table,
                 duals_out, pushed_out, slots, spread, sums)
 
@@ -303,7 +298,7 @@
     primal, dual = local_step(dims, slot_rows, weight[...], own, inputs, state,
                               later_edges(dims, slot_rows, received, parts, edge_in),
                               (power_out, charge_out, dyn_out), edge_out)
-    power_row[...] = row_power(dims, first_rows, weight[...], first.at[lax.axis_index("core")], row_in[...],
+    power_row[...] = row_power(dims, first_rows, weight[...], first, row_in[...],
                                take_row(own, SLOT_DYN, *dims, slot_rows), pushed_row[...], bar)
     feeder_part(dims, slot_rows, load, weight[...], primal, dual, bar, dyn_out, duals_t, limits_t, values, table,
                 duals_out, pushed_out, slots, spread, sums)
@@ -318,7 +313,7 @@
     state = [lambda cut, ref=ref: ref[:, cut] for ref in (power, charge, dyn)]
     local_step(dims, slot_rows, weight, own, inputs, state, later_edges(dims, slot_rows, received, parts, edge_in),
                (power_out, charge_out, dyn_out), None)
-    row_power(dims, first_rows, weight, first.at[lax.axis_index("core")], row_in[...], take_row(own, SLOT_DYN, *dims, slot_rows),
+    row_power(dims, first_rows, weight, first, row_in[...], take_row(own, SLOT_DYN, *dims, slot_rows),
               pushed_row[...], bar)
     new = feeder_duals(values, table, load, bar, weight, duals_t[...], limits_t[...], spread)
     duals_out[...] = jnp.transpose(new)[: duals_out.shape[0]]
@@ -399,17 +394,17 @@
     row_of = jnp.sum((index_all >= block_offsets[None, 1:-1]).astype(jnp.int32), axis=1)
     matrix = (block_values, jnp.concatenate([row_of, (block_cols % pieces) * groups + block_cols // pieces]))
 
-    edges = call(edges_kernel, "edges", [VMEM], [(2, local)], flops=EARLY_COPY_FLOPS)(inputs)[0]
+    edges, swapped = call(edges_kernel, "edges", [VMEM], [(2, local), (3, local)], flops=EARLY_COPY_FLOPS)(inputs)
+    swapped = lax.ppermute(swapped, "core", [(0, 1), (1, 0)])
     links = [(i, i + 1 if i % 2 else i - 1) for i in range(1, 2 * chips - 1)]
     across = lax.ppermute(edges, ("z", "core"), links)
     first, duals_t, limits_t, pushed = call(
         functools.partial(first_kernel, dims, first_rows), "first",
-        [VMEM] * 4, [(2, groups * first_rows, LANES), square, square, row],
+        [VMEM] * 4, [(groups * first_rows, LANES), square, square, row],
         [spread] + [sums] * ADJOINT_PARTS, work, moved, table=2 * blocks,
     )(duals, inputs, *matrix)
-    first, across = lax.optimization_barrier((first, across))
-    first = exchange(first.reshape(2 * groups, first_rows, LANES), ("core", "bat"))
-    first = first.reshape(2, groups * first_rows, LANES)
+    first, across, swapped = lax.optimization_barrier((first, across, swapped))
+    first = exchange(first.reshape(groups, first_rows, LANES), "bat").reshape(groups * first_rows, LANES)
 
     both = (2, groups * slot_rows, LANES)
     step_outs = [line, row] + [own] * 3 + [(1, local), square, row, both]
@@ -420,9 +415,9 @@
         sizes = (dims, first_rows, slot_rows)
         if iteration == 0:
             results = call(
-                functools.partial(step_one_kernel, *sizes), "step_one", [VMEM] * 6 + matrix_specs, outs, scratch,
+                functools.partial(step_one_kernel, *sizes), "step_one", [VMEM] * 7 + matrix_specs, outs, scratch,
                 2 * work, moved, table=2 * blocks,
-            )(first, across, pushed, inputs, duals_t, limits_t, *matrix)
+            )(first, across, swapped, pushed, inputs, duals_t, limits_t, *matrix)
         else:
             results = call(
                 functools.partial(last_kernel if last else step_kernel, *sizes), "last" if last else "step",

time: 126 us -> 125 us (level)
  blocking collectives: 107 us -> 101 us
  starting transfers between devices: 5.2 us -> 9.71 us
    all_to_all x7, blocking collectives: 107 us -> 101 us  [exchange(): return lax.all_to_all(value, axis, 0, 0, tiled=True)]
    ppermute x0 -> x1, starting transfers between devices: none -> 4.51 us  [shards(): swapped = lax.ppermute(swapped, 'core', [(0, 1), (1, 0)])]
  transfers between devices with their start and end apart: 1 -> 2, of which waited for: 0 -> 0; matrix products, arithmetic and copies ran while one was open for 0% -> 0% of each run, Pallas kernels for 1% -> 1%
where the time goes in v8:
time: 125 us; the launch traced here: 124 us
  blocking collectives  101 us (81%)
  Pallas kernels  10.9 us (9%)
  starting transfers between devices  9.71 us (8%)
  other arithmetic  1.3 us (1%)
    all_to_all x7, blocking collectives, exchange(): return lax.all_to_all(value, axis, 0, 0, tiled=True)  101 us
    pallas_call x3, Pallas kernels, shards(): call(functools.partial(last_kernel if last else step_kernel, *sizes), 'la...  7.18 us
    ppermute x1, starting transfers between devices, shards(): across = lax.ppermute(edges, ('z', 'core'), links)  5.2 us
    ppermute x1, starting transfers between devices, shards(): swapped = lax.ppermute(swapped, 'core', [(0, 1), (1, 0)])  4.51 us
  transfers between devices with their start and end apart: 2, of which 0 were waited for; matrix products, arithmetic and copies ran while one was open for 0% of the time, Pallas kernels for 1%

profile of v8, /device:TPU:1, one launch (start us, length us, event | category | flops | bytes accessed | tf_op | source)
XLA Modules:
  0.0 124.4 jit_solution(17521995693779562971)
XLA Ops:
  0.7 0.9 select_select_fusion.inputs
  1.6 0.0 copy-start.3
  1.6 0.0 copy-start.4
  1.6 0.0 copy-start.1
  1.7 0.0 copy-start.2
  1.7 0.0 copy-start
  1.7 5.2 %collective-permute-start = (f32[2,384]{1,0:T(2,128)S(1)}, f32[2,384]{1,0:T(2,128)S(1)}, u32[]{:S(2)}, u32[]{:S(2)}) collective-permute-start(f32[2,384]{1,0:T(2,128)S(1)} %get-tuple-element.45), channel_id=1, source_target_pairs={{16,32},{32,16},{48,64},{64,48},{80,96},{96,80},{112,128},{128,112... | collective-permute-start | bytes 9224 | tf_op jit(solution)/shard_map/ppermute | solution.py:400
  6.9 4.5 %collective-permute-start.1 = (f32[3,384]{1,0:T(4,128)S(1)}, f32[3,384]{1,0:T(4,128)S(1)}, u32[]{:S(2)}, u32[]{:S(2)}) collective-permute-start(f32[3,384]{1,0:T(4,128)S(1)} %get-tuple-element.46), channel_id=1, source_target_pairs={{0,16},{16,0},{1,17},{17,1},{2,18},{18,2},{3,19},{19,3},{4,20},{20... | collective-permute-start | bytes 13832 | tf_op jit(solution)/shard_map/ppermute | solution.py:398
  11.4 0.0 copy-done.3
  11.4 0.0 copy-done.4
  11.5 0.1 pad_add_fusion.1
  11.5 0.1 slice.8
  11.6 0.1 convert_reduce_fusion
  11.7 0.0 copy-done.1
  11.7 0.0 copy-done.2
  11.7 0.1 broadcast_select_fusion.duals
  11.8 0.1 pad_add_fusion.table_in
  11.9 0.0 copy-done
  11.9 1.3 %first.1 = (f32[256,128]{1,0:T(8,128)S(1)}, f32[128,128]{1,0:T(8,128)S(1)}, f32[128,128]{1,0:T(8,128)S(1)}, f32[48,128]{1,0:T(8,128)S(1)}) custom-call(f32[2,24,128]{2,1,0:T(8,128)S(1)} %broadcast_select_fusion.duals, f32[7,16,384]{2,1,0:T(8,128)S(1)} %select_select_fusion.inputs, f32[72,128,128]{2,1,0:T(8,128)S(1)} %copy-done, s32[144]{0:T(256)S(1)} %pad_add_fusion.table_in), custom_call_target="tpu_custom_call" | custom-call | flops 2359296 | bytes 4718592 | tf_op jit(solution)/shard_map/first/pallas_call | solution.py:401
  13.2 0.0 collective-permute-done.across
  13.2 0.0 collective-permute-done.1.swapped
  13.2 10.8 %all_to_all.35 = f32[16,16,128]{2,1,0:T(8,128)S(1)} all-to-all(f32[16,16,128]{2,1,0:T(8,128)S(1)} %bitcast.35), channel_id=1, replica_groups=mesh['z'=16,'core'=2,'bat'=16] {'bat'}, dimensions={0} | all-to-all | bytes 262144 | tf_op jit(solution)/shard_map/all_to_all | solution.py:372
  24.0 2.4 %step_one.1 = (f32[1,128]{1,0:T(1,128)S(1)}, f32[48,128]{1,0:T(8,128)S(1)}, f32[16,384]{1,0:T(8,128)S(1)}, f32[16,384]{1,0:T(8,128)S(1)}, f32[16,384]{1,0:T(8,12...) custom-call(f32[256,128]{1,0:T(8,128)S(1)} %bitcast.17, ...), custom_call_target="tpu_custom_call" | custom-call | flops 4718592 | bytes 4718592 | tf_op jit(solution)/shard_map/step_one/pallas_call | solution.py:417
  26.4 12.6 %all_to_all.36 = f32[32,8,128]{2,1,0:T(8,128)S(1)} all-to-all(f32[32,8,128]{2,1,0:T(8,128)S(1)} %bitcast.36), channel_id=1, replica_groups=mesh['z'=16,'core'=2,'bat'=16] {'core','bat'}, dimensions={0} | all-to-all | bytes 262144 | tf_op jit(solution)/shard_map/all_to_all | solution.py:372
  39.0 25.3 %all_to_all.37 = f32[16,4,128]{2,1,0:T(4,128)S(1)} all-to-all(f32[16,4,128]{2,1,0:T(4,128)S(1)} %bitcast.30), channel_id=1, replica_groups=mesh['z'=16,'core'=2,'bat'=16] {'z'}, dimensions={0} | all-to-all | bytes 65536 | tf_op jit(solution)/shard_map/all_to_all | solution.py:372
  64.3 2.4 %step.2 = (f32[1,128]{1,0:T(1,128)S(1)}, f32[48,128]{1,0:T(8,128)S(1)}, f32[16,384]{1,0:T(8,128)S(1)}, f32[16,384]{1,0:T(8,128)S(1)}, f32[16,384]{1,0:T(8,128)S(...) custom-call(f32[256,128]{1,0:T(8,128)S(1)} %bitcast.18, ...), custom_call_target="tpu_custom_call" | custom-call | flops 4718592 | bytes 4718592 | tf_op jit(solution)/shard_map/step/pallas_call | solution.py:422
  66.7 12.6 %all_to_all.38 = f32[32,8,128]{2,1,0:T(8,128)S(1)} all-to-all(f32[32,8,128]{2,1,0:T(8,128)S(1)} %bitcast.33), channel_id=1, replica_groups=mesh['z'=16,'core'=2,'bat'=16] {'core','bat'}, dimensions={0} | all-to-all | bytes 262144 | tf_op jit(solution)/shard_map/all_to_all | solution.py:372
  79.4 14.0 %all_to_all.39 = f32[16,4,128]{2,1,0:T(4,128)S(1)} all-to-all(f32[16,4,128]{2,1,0:T(4,128)S(1)} %bitcast.31), channel_id=1, replica_groups=mesh['z'=16,'core'=2,'bat'=16] {'z'}, dimensions={0} | all-to-all | bytes 65536 | tf_op jit(solution)/shard_map/all_to_all | solution.py:372
  93.3 2.4 %step.3 = (f32[1,128]{1,0:T(1,128)S(1)}, f32[48,128]{1,0:T(8,128)S(1)}, f32[16,384]{1,0:T(8,128)S(1)}, f32[16,384]{1,0:T(8,128)S(1)}, f32[16,384]{1,0:T(8,128)S(...) custom-call(f32[256,128]{1,0:T(8,128)S(1)} %bitcast.19, ...), custom_call_target="tpu_custom_call" | custom-call | flops 4718592 | bytes 4718592 | tf_op jit(solution)/shard_map/step/pallas_call | solution.py:422
  95.8 12.3 %all_to_all.40 = f32[32,8,128]{2,1,0:T(8,128)S(1)} all-to-all(f32[32,8,128]{2,1,0:T(8,128)S(1)} %bitcast.34), channel_id=1, replica_groups=mesh['z'=16,'core'=2,'bat'=16] {'core','bat'}, dimensions={0} | all-to-all | bytes 262144 | tf_op jit(solution)/shard_map/all_to_all | solution.py:372
  108.1 14.0 %all_to_all.41 = f32[16,4,128]{2,1,0:T(4,128)S(1)} all-to-all(f32[16,4,128]{2,1,0:T(4,128)S(1)} %bitcast.32), channel_id=1, replica_groups=mesh['z'=16,'core'=2,'bat'=16] {'z'}, dimensions={0} | all-to-all | bytes 65536 | tf_op jit(solution)/shard_map/all_to_all | solution.py:372
  122.0 2.3 %last.1 = (f32[16,384]{1,0:T(8,128)}, f32[16,384]{1,0:T(8,128)}, f32[16,384]{1,0:T(8,128)}, f32[24,128]{1,0:T(8,128)}) custom-call(f32[256,128]{1,0:T(8,128)S(1)} %bitcast.20, f32[2,128,128]{2,1,0:T(8,128)S(1)} %bitcast.26, f32[64,128]{1,0:T(8,128)S(1)} %bitcast.29, f32[1,128]{1,0:T(1,128)S(1)} %get-tuple-element.72.weight_in, ...), custom_call_target="tpu_custom_call" | custom-call | flops 4718592 | bytes 4718592 | tf_op jit(solution)/shard_map/last/pallas_call | solution.py:422
  (9 shorter events, 0.1 us)
Async XLA Ops:
  1.6 9.8 %copy-start.3 = (s32[25]{0:T(128)S(1)}, s32[25]{0:T(128)}, u32[]{:S(2)}) copy-start(s32[25]{0:T(128)} %param.23) | copy-start | bytes 304
  1.6 9.8 %copy-start.4 = (s32[72]{0:T(128)S(1)}, s32[72]{0:T(128)}, u32[]{:S(2)}) copy-start(s32[72]{0:T(128)} %param.22) | copy-start | bytes 868
  1.6 10.1 %copy-start.1 = (f32[3072]{0:T(1024)S(1)}, f32[3072]{0:T(1024)}, u32[]{:S(2)}) copy-start(f32[3072]{0:T(1024)} %param.20) | copy-start | bytes 36868
  1.7 10.1 %copy-start.2 = (f32[1,3072]{1,0:T(1,128)S(1)}, f32[1,3072]{1,0:T(1,128)}, u32[]{:S(2)}) copy-start(f32[1,3072]{1,0:T(1,128)} %param.15) | copy-start | bytes 36868
  1.7 10.2 %copy-start = (f32[72,128,128]{2,1,0:T(8,128)S(1)}, f32[72,128,128]{2,1,0:T(8,128)}, u32[]{:S(2)}) copy-start(f32[72,128,128]{2,1,0:T(8,128)} %values.9) | copy-start | bytes 14155780
  1.7 11.4 %collective-permute-start = (f32[2,384]{1,0:T(2,128)S(1)}, f32[2,384]{1,0:T(2,128)S(1)}, u32[]{:S(2)}, u32[]{:S(2)}) collective-permute-start(f32[2,384]{1,0:T(2,128)S(1)} %get-tuple-element.45), channel_id=1, source_target_pairs={{16,32},{32,16},{48,64},{64,48},{80,96},{96,80},{112,128},{128,112... | collective-permute-start | bytes 9224 | tf_op jit(solution)/shard_map/ppermute | solution.py:400
  6.9 6.3 %collective-permute-start.1 = (f32[3,384]{1,0:T(4,128)S(1)}, f32[3,384]{1,0:T(4,128)S(1)}, u32[]{:S(2)}, u32[]{:S(2)}) collective-permute-start(f32[3,384]{1,0:T(4,128)S(1)} %get-tuple-element.46), channel_id=1, source_target_pairs={{0,16},{16,0},{1,17},{17,1},{2,18},{18,2},{3,19},{19,3},{4,20},{20... | collective-permute-start | bytes 13832 | tf_op jit(solution)/shard_map/ppermute | solution.py:398

commit v9 on v8

--- a/solution.py
+++ b/solution.py
@@ -89,7 +89,7 @@
     return adjoint_total(sums)
 
 
-def feeder_duals(values, table, load, field, weight, duals_t, limits_t, spread):
+def feeder_duals(values, table, load, field, weight, duals_t, limits_t, spread, local):
     blocks, blk = values.shape[:2]
     feeds = spread.shape[0]
     ways = unrolled(blocks, APPLY_UNROLL)
@@ -108,12 +108,13 @@
         return carry
 
     lax.fori_loop(0, blocks // ways, step, 0)
+    squares = local()
     new = jnp.zeros((blk, LANES), F32)
     for f in range(feeds):
         dual = jnp.maximum(0.0, jnp.sum(spread[f], axis=1, keepdims=True))
         spread[f] = jnp.broadcast_to(dual, (blk, LANES))
         new = jnp.where(lane == f, dual, new)
-    return new
+    return new, squares
 
 
 def pack_sums(primal, dual):
@@ -218,11 +219,11 @@
     return new
 
 
-def feeder_part(dims, slot_rows, load, weight, primal, dual, bar, dyn, duals_t, limits_t, values, table,
+def feeder_part(dims, slot_rows, load, weight, local, bar, dyn, duals_t, limits_t, values, table,
                 duals_out, pushed_out, slots, spread, sums):
     pieces, groups = dims
     _, core, bat = places()
-    new = feeder_duals(values, table, load, bar, weight, duals_t[...], limits_t[...], spread)
+    new, (primal, dual) = feeder_duals(values, table, load, bar, weight, duals_t[...], limits_t[...], spread, local)
     duals_out[...] = new
     parts = pack_sums(primal, dual + row_sum((new - duals_t[...]) ** 2))
     adjoint_start(sums)
@@ -256,12 +257,12 @@
         lambda i: jnp.where(core == 0, linked(0, i), partner(1, i)),
         lambda i: jnp.where(core == 0, linked(1, i), partner(2, i)),
     )
-    primal, dual = local_step(dims, first_rows, weight[...], first, inputs, state, edges,
+    local = lambda: local_step(dims, first_rows, weight[...], first, inputs, state, edges,
                               (power_out, charge_out, dyn_out), edge_out)
     power_row[...] = row_power(dims, first_rows, weight[...], first,
                                take_row(first, SLOT_POWER, pieces, groups, first_rows),
                                take_row(first, SLOT_DYN, pieces, groups, first_rows), pushed_row[...], bar)
-    feeder_part(dims, slot_rows, load, weight[...], primal, dual, bar, dyn_out, duals_t, limits_t, values, table,
+    feeder_part(dims, slot_rows, load, weight[...], local, bar, dyn_out, duals_t, limits_t, values, table,
                 duals_out, pushed_out, slots, spread, sums)
 
 
@@ -295,12 +296,12 @@
     weight[...] = later_weight(weight_in, parts)
     own = received.at[lax.axis_index("core")]
     state = [lambda cut, ref=ref: ref[:, cut] for ref in (power, charge, dyn)]
-    primal, dual = local_step(dims, slot_rows, weight[...], own, inputs, state,
+    local = lambda: local_step(dims, slot_rows, weight[...], own, inputs, state,
                               later_edges(dims, slot_rows, received, parts, edge_in),
                               (power_out, charge_out, dyn_out), edge_out)
     power_row[...] = row_power(dims, first_rows, weight[...], first, row_in[...],
                                take_row(own, SLOT_DYN, *dims, slot_rows), pushed_row[...], bar)
-    feeder_part(dims, slot_rows, load, weight[...], primal, dual, bar, dyn_out, duals_t, limits_t, values, table,
+    feeder_part(dims, slot_rows, load, weight[...], local, bar, dyn_out, duals_t, limits_t, values, table,
                 duals_out, pushed_out, slots, spread, sums)
 
 
@@ -311,11 +312,11 @@
     weight = later_weight(weight_in, parts)
     own = received.at[lax.axis_index("core")]
     state = [lambda cut, ref=ref: ref[:, cut] for ref in (power, charge, dyn)]
-    local_step(dims, slot_rows, weight, own, inputs, state, later_edges(dims, slot_rows, received, parts, edge_in),
+    local = lambda: local_step(dims, slot_rows, weight, own, inputs, state, later_edges(dims, slot_rows, received, parts, edge_in),
                (power_out, charge_out, dyn_out), None)
     row_power(dims, first_rows, weight, first, row_in[...], take_row(own, SLOT_DYN, *dims, slot_rows),
               pushed_row[...], bar)
-    new = feeder_duals(values, table, load, bar, weight, duals_t[...], limits_t[...], spread)
+    new, _ = feeder_duals(values, table, load, bar, weight, duals_t[...], limits_t[...], spread, local)
     duals_out[...] = jnp.transpose(new)[: duals_out.shape[0]]
 
 

time: 125 us -> 125 us (level)
  no operation moved by 1% of the time
where the time goes in v9:
time: 125 us; the launch traced here: 124 us
  blocking collectives  101 us (81%)
  Pallas kernels  10.9 us (9%)
  starting transfers between devices  9.71 us (8%)
  other arithmetic  1.3 us (1%)
    all_to_all x7, blocking collectives, exchange(): return lax.all_to_all(value, axis, 0, 0, tiled=True)  101 us
    pallas_call x3, Pallas kernels, shards(): call(functools.partial(last_kernel if last else step_kernel, *sizes), 'la...  7.17 us
    ppermute x1, starting transfers between devices, shards(): across = lax.ppermute(edges, ('z', 'core'), links)  5.2 us
    ppermute x1, starting transfers between devices, shards(): swapped = lax.ppermute(swapped, 'core', [(0, 1), (1, 0)])  4.51 us
  transfers between devices with their start and end apart: 2, of which 0 were waited for; matrix products, arithmetic and copies ran while one was open for 0% of the time, Pallas kernels for 1%

profile of v9, /device:TPU:1, one launch (start us, length us, event | category | flops | bytes accessed | tf_op | source)
XLA Modules:
  0.0 124.3 jit_solution(1890226590231645032)
XLA Ops:
  0.7 0.9 select_select_fusion.inputs
  1.6 0.0 copy-start.3
  1.6 0.0 copy-start.4
  1.6 0.0 copy-start.1
  1.7 0.0 copy-start.2
  1.7 0.0 copy-start
  1.7 5.2 %collective-permute-start = (f32[2,384]{1,0:T(2,128)S(1)}, f32[2,384]{1,0:T(2,128)S(1)}, u32[]{:S(2)}, u32[]{:S(2)}) collective-permute-start(f32[2,384]{1,0:T(2,128)S(1)} %get-tuple-element.45), channel_id=1, source_target_pairs={{16,32},{32,16},{48,64},{64,48},{80,96},{96,80},{112,128},{128,112... | collective-permute-start | bytes 9224 | tf_op jit(solution)/shard_map/ppermute | solution.py:401
  6.9 4.5 %collective-permute-start.1 = (f32[3,384]{1,0:T(4,128)S(1)}, f32[3,384]{1,0:T(4,128)S(1)}, u32[]{:S(2)}, u32[]{:S(2)}) collective-permute-start(f32[3,384]{1,0:T(4,128)S(1)} %get-tuple-element.46), channel_id=1, source_target_pairs={{0,16},{16,0},{1,17},{17,1},{2,18},{18,2},{3,19},{19,3},{4,20},{20... | collective-permute-start | bytes 13832 | tf_op jit(solution)/shard_map/ppermute | solution.py:399
  11.4 0.0 copy-done.3
  11.4 0.0 copy-done.4
  11.5 0.1 pad_add_fusion.1
  11.5 0.1 slice.8
  11.6 0.1 convert_reduce_fusion
  11.7 0.0 copy-done.1
  11.7 0.0 copy-done.2
  11.7 0.1 broadcast_select_fusion.duals
  11.8 0.1 pad_add_fusion.table_in
  11.9 0.0 copy-done
  11.9 1.3 %first.1 = (f32[256,128]{1,0:T(8,128)S(1)}, f32[128,128]{1,0:T(8,128)S(1)}, f32[128,128]{1,0:T(8,128)S(1)}, f32[48,128]{1,0:T(8,128)S(1)}) custom-call(f32[2,24,128]{2,1,0:T(8,128)S(1)} %broadcast_select_fusion.duals, f32[7,16,384]{2,1,0:T(8,128)S(1)} %select_select_fusion.inputs, f32[72,128,128]{2,1,0:T(8,128)S(1)} %copy-done, s32[144]{0:T(256)S(1)} %pad_add_fusion.table_in), custom_call_target="tpu_custom_call" | custom-call | flops 2359296 | bytes 4718592 | tf_op jit(solution)/shard_map/first/pallas_call | solution.py:402
  13.1 0.0 collective-permute-done.across
  13.2 0.0 collective-permute-done.1.swapped
  13.2 10.8 %all_to_all.35 = f32[16,16,128]{2,1,0:T(8,128)S(1)} all-to-all(f32[16,16,128]{2,1,0:T(8,128)S(1)} %bitcast.35), channel_id=1, replica_groups=mesh['z'=16,'core'=2,'bat'=16] {'bat'}, dimensions={0} | all-to-all | bytes 262144 | tf_op jit(solution)/shard_map/all_to_all | solution.py:373
  24.0 2.4 %step_one.1 = (f32[1,128]{1,0:T(1,128)S(1)}, f32[48,128]{1,0:T(8,128)S(1)}, f32[16,384]{1,0:T(8,128)S(1)}, f32[16,384]{1,0:T(8,128)S(1)}, f32[16,384]{1,0:T(8,12...) custom-call(f32[256,128]{1,0:T(8,128)S(1)} %bitcast.17, ...), custom_call_target="tpu_custom_call" | custom-call | flops 4718592 | bytes 4718592 | tf_op jit(solution)/shard_map/step_one/pallas_call | solution.py:418
  26.4 12.6 %all_to_all.36 = f32[32,8,128]{2,1,0:T(8,128)S(1)} all-to-all(f32[32,8,128]{2,1,0:T(8,128)S(1)} %bitcast.36), channel_id=1, replica_groups=mesh['z'=16,'core'=2,'bat'=16] {'core','bat'}, dimensions={0} | all-to-all | bytes 262144 | tf_op jit(solution)/shard_map/all_to_all | solution.py:373
  39.0 25.3 %all_to_all.37 = f32[16,4,128]{2,1,0:T(4,128)S(1)} all-to-all(f32[16,4,128]{2,1,0:T(4,128)S(1)} %bitcast.30), channel_id=1, replica_groups=mesh['z'=16,'core'=2,'bat'=16] {'z'}, dimensions={0} | all-to-all | bytes 65536 | tf_op jit(solution)/shard_map/all_to_all | solution.py:373
  64.3 2.4 %step.2 = (f32[1,128]{1,0:T(1,128)S(1)}, f32[48,128]{1,0:T(8,128)S(1)}, f32[16,384]{1,0:T(8,128)S(1)}, f32[16,384]{1,0:T(8,128)S(1)}, f32[16,384]{1,0:T(8,128)S(...) custom-call(f32[256,128]{1,0:T(8,128)S(1)} %bitcast.18, ...), custom_call_target="tpu_custom_call" | custom-call | flops 4718592 | bytes 4718592 | tf_op jit(solution)/shard_map/step/pallas_call | solution.py:423
  66.7 12.6 %all_to_all.38 = f32[32,8,128]{2,1,0:T(8,128)S(1)} all-to-all(f32[32,8,128]{2,1,0:T(8,128)S(1)} %bitcast.33), channel_id=1, replica_groups=mesh['z'=16,'core'=2,'bat'=16] {'core','bat'}, dimensions={0} | all-to-all | bytes 262144 | tf_op jit(solution)/shard_map/all_to_all | solution.py:373
  79.3 14.0 %all_to_all.39 = f32[16,4,128]{2,1,0:T(4,128)S(1)} all-to-all(f32[16,4,128]{2,1,0:T(4,128)S(1)} %bitcast.31), channel_id=1, replica_groups=mesh['z'=16,'core'=2,'bat'=16] {'z'}, dimensions={0} | all-to-all | bytes 65536 | tf_op jit(solution)/shard_map/all_to_all | solution.py:373
  93.3 2.4 %step.3 = (f32[1,128]{1,0:T(1,128)S(1)}, f32[48,128]{1,0:T(8,128)S(1)}, f32[16,384]{1,0:T(8,128)S(1)}, f32[16,384]{1,0:T(8,128)S(1)}, f32[16,384]{1,0:T(8,128)S(...) custom-call(f32[256,128]{1,0:T(8,128)S(1)} %bitcast.19, ...), custom_call_target="tpu_custom_call" | custom-call | flops 4718592 | bytes 4718592 | tf_op jit(solution)/shard_map/step/pallas_call | solution.py:423
  95.7 12.3 %all_to_all.40 = f32[32,8,128]{2,1,0:T(8,128)S(1)} all-to-all(f32[32,8,128]{2,1,0:T(8,128)S(1)} %bitcast.34), channel_id=1, replica_groups=mesh['z'=16,'core'=2,'bat'=16] {'core','bat'}, dimensions={0} | all-to-all | bytes 262144 | tf_op jit(solution)/shard_map/all_to_all | solution.py:373
  108.0 14.0 %all_to_all.41 = f32[16,4,128]{2,1,0:T(4,128)S(1)} all-to-all(f32[16,4,128]{2,1,0:T(4,128)S(1)} %bitcast.32), channel_id=1, replica_groups=mesh['z'=16,'core'=2,'bat'=16] {'z'}, dimensions={0} | all-to-all | bytes 65536 | tf_op jit(solution)/shard_map/all_to_all | solution.py:373
  122.0 2.3 %last.1 = (f32[16,384]{1,0:T(8,128)}, f32[16,384]{1,0:T(8,128)}, f32[16,384]{1,0:T(8,128)}, f32[24,128]{1,0:T(8,128)}) custom-call(f32[256,128]{1,0:T(8,128)S(1)} %bitcast.20, f32[2,128,128]{2,1,0:T(8,128)S(1)} %bitcast.26, f32[64,128]{1,0:T(8,128)S(1)} %bitcast.29, f32[1,128]{1,0:T(1,128)S(1)} %get-tuple-element.72.weight_in, ...), custom_call_target="tpu_custom_call" | custom-call | flops 4718592 | bytes 4718592 | tf_op jit(solution)/shard_map/last/pallas_call | solution.py:423
  (9 shorter events, 0.1 us)
Async XLA Ops:
  1.6 9.8 %copy-start.3 = (s32[25]{0:T(128)S(1)}, s32[25]{0:T(128)}, u32[]{:S(2)}) copy-start(s32[25]{0:T(128)} %param.23) | copy-start | bytes 304
  1.6 9.8 %copy-start.4 = (s32[72]{0:T(128)S(1)}, s32[72]{0:T(128)}, u32[]{:S(2)}) copy-start(s32[72]{0:T(128)} %param.22) | copy-start | bytes 868
  1.6 10.1 %copy-start.1 = (f32[3072]{0:T(1024)S(1)}, f32[3072]{0:T(1024)}, u32[]{:S(2)}) copy-start(f32[3072]{0:T(1024)} %param.20) | copy-start | bytes 36868
  1.7 10.1 %copy-start.2 = (f32[1,3072]{1,0:T(1,128)S(1)}, f32[1,3072]{1,0:T(1,128)}, u32[]{:S(2)}) copy-start(f32[1,3072]{1,0:T(1,128)} %param.15) | copy-start | bytes 36868
  1.7 10.2 %copy-start = (f32[72,128,128]{2,1,0:T(8,128)S(1)}, f32[72,128,128]{2,1,0:T(8,128)}, u32[]{:S(2)}) copy-start(f32[72,128,128]{2,1,0:T(8,128)} %values.9) | copy-start | bytes 14155780
  1.7 11.4 %collective-permute-start = (f32[2,384]{1,0:T(2,128)S(1)}, f32[2,384]{1,0:T(2,128)S(1)}, u32[]{:S(2)}, u32[]{:S(2)}) collective-permute-start(f32[2,384]{1,0:T(2,128)S(1)} %get-tuple-element.45), channel_id=1, source_target_pairs={{16,32},{32,16},{48,64},{64,48},{80,96},{96,80},{112,128},{128,112... | collective-permute-start | bytes 9224 | tf_op jit(solution)/shard_map/ppermute | solution.py:401
  6.9 6.2 %collective-permute-start.1 = (f32[3,384]{1,0:T(4,128)S(1)}, f32[3,384]{1,0:T(4,128)S(1)}, u32[]{:S(2)}, u32[]{:S(2)}) collective-permute-start(f32[3,384]{1,0:T(4,128)S(1)} %get-tuple-element.46), channel_id=1, source_target_pairs={{0,16},{16,0},{1,17},{17,1},{2,18},{18,2},{3,19},{19,3},{4,20},{20... | collective-permute-start | bytes 13832 | tf_op jit(solution)/shard_map/ppermute | solution.py:399

commit v10 on v9

--- a/solution.py
+++ b/solution.py
@@ -13,7 +13,7 @@
 LANES = 128
 HALF = LANES // 2
 ADJOINT_UNROLL = 24
-ADJOINT_PARTS = 4
+ADJOINT_PARTS = 2
 APPLY_UNROLL = 8
 EARLY_COPY_FLOPS = 2 * 10**10
 F32 = jnp.float32

time: 125 us -> 125 us (level)
  no operation moved by 1% of the time
where the time goes in v10:
time: 125 us
  blocking collectives  101 us (81%)
  Pallas kernels  11.5 us (9%)
  starting transfers between devices  9.71 us (8%)
  other arithmetic  1.3 us (1%)
    all_to_all x7, blocking collectives, exchange(): return lax.all_to_all(value, axis, 0, 0, tiled=True)  101 us
    pallas_call x3, Pallas kernels, shards(): call(functools.partial(last_kernel if last else step_kernel, *sizes), 'la...  7.53 us
    ppermute x1, starting transfers between devices, shards(): across = lax.ppermute(edges, ('z', 'core'), links)  5.2 us
    ppermute x1, starting transfers between devices, shards(): swapped = lax.ppermute(swapped, 'core', [(0, 1), (1, 0)])  4.51 us
    pallas_call x1, Pallas kernels, shards(): call(functools.partial(step_one_kernel, *sizes), 'step_one', [VMEM] * 7 +...  2.59 us
  transfers between devices with their start and end apart: 2, of which 0 were waited for; matrix products, arithmetic and copies ran while one was open for 0% of the time, Pallas kernels for 1%

profile of v10, /device:TPU:1, one launch (start us, length us, event | category | flops | bytes accessed | tf_op | source)
XLA Modules:
  0.0 124.9 jit_solution(3397719282136921646)
XLA Ops:
  0.7 0.9 select_select_fusion.inputs
  1.6 0.0 copy-start.3
  1.6 0.0 copy-start.4
  1.6 0.0 copy-start.1
  1.7 0.0 copy-start.2
  1.7 0.0 copy-start
  1.7 5.2 %collective-permute-start = (f32[2,384]{1,0:T(2,128)S(1)}, f32[2,384]{1,0:T(2,128)S(1)}, u32[]{:S(2)}, u32[]{:S(2)}) collective-permute-start(f32[2,384]{1,0:T(2,128)S(1)} %get-tuple-element.45), channel_id=1, source_target_pairs={{16,32},{32,16},{48,64},{64,48},{80,96},{96,80},{112,128},{128,112... | collective-permute-start | bytes 9224 | tf_op jit(solution)/shard_map/ppermute | solution.py:401
  6.9 4.5 %collective-permute-start.1 = (f32[3,384]{1,0:T(4,128)S(1)}, f32[3,384]{1,0:T(4,128)S(1)}, u32[]{:S(2)}, u32[]{:S(2)}) collective-permute-start(f32[3,384]{1,0:T(4,128)S(1)} %get-tuple-element.46), channel_id=1, source_target_pairs={{0,16},{16,0},{1,17},{17,1},{2,18},{18,2},{3,19},{19,3},{4,20},{20... | collective-permute-start | bytes 13832 | tf_op jit(solution)/shard_map/ppermute | solution.py:399
  11.4 0.0 copy-done.3
  11.4 0.0 copy-done.4
  11.5 0.1 pad_add_fusion.1
  11.5 0.1 slice.8
  11.6 0.1 convert_reduce_fusion
  11.7 0.0 copy-done.1
  11.7 0.0 copy-done.2
  11.7 0.1 broadcast_select_fusion.duals
  11.8 0.1 pad_add_fusion.table_in
  11.9 0.0 copy-done
  11.9 1.3 %first.1 = (f32[256,128]{1,0:T(8,128)S(1)}, f32[128,128]{1,0:T(8,128)S(1)}, f32[128,128]{1,0:T(8,128)S(1)}, f32[48,128]{1,0:T(8,128)S(1)}) custom-call(f32[2,24,128]{2,1,0:T(8,128)S(1)} %broadcast_select_fusion.duals, f32[7,16,384]{2,1,0:T(8,128)S(1)} %select_select_fusion.inputs, f32[72,128,128]{2,1,0:T(8,128)S(1)} %copy-done, s32[144]{0:T(256)S(1)} %pad_add_fusion.table_in), custom_call_target="tpu_custom_call" | custom-call | flops 2359296 | bytes 4718592 | tf_op jit(solution)/shard_map/first/pallas_call | solution.py:402
  13.2 0.0 collective-permute-done.across
  13.2 0.0 collective-permute-done.1.swapped
  13.2 10.8 %all_to_all.35 = f32[16,16,128]{2,1,0:T(8,128)S(1)} all-to-all(f32[16,16,128]{2,1,0:T(8,128)S(1)} %bitcast.35), channel_id=1, replica_groups=mesh['z'=16,'core'=2,'bat'=16] {'bat'}, dimensions={0} | all-to-all | bytes 262144 | tf_op jit(solution)/shard_map/all_to_all | solution.py:373
  24.0 2.6 %step_one.1 = (f32[1,128]{1,0:T(1,128)S(1)}, f32[48,128]{1,0:T(8,128)S(1)}, f32[16,384]{1,0:T(8,128)S(1)}, f32[16,384]{1,0:T(8,128)S(1)}, f32[16,384]{1,0:T(8,12...) custom-call(f32[256,128]{1,0:T(8,128)S(1)} %bitcast.17, ...), custom_call_target="tpu_custom_call" | custom-call | flops 4718592 | bytes 4718592 | tf_op jit(solution)/shard_map/step_one/pallas_call | solution.py:418
  26.6 12.6 %all_to_all.36 = f32[32,8,128]{2,1,0:T(8,128)S(1)} all-to-all(f32[32,8,128]{2,1,0:T(8,128)S(1)} %bitcast.36), channel_id=1, replica_groups=mesh['z'=16,'core'=2,'bat'=16] {'core','bat'}, dimensions={0} | all-to-all | bytes 262144 | tf_op jit(solution)/shard_map/all_to_all | solution.py:373
  39.2 25.3 %all_to_all.37 = f32[16,4,128]{2,1,0:T(4,128)S(1)} all-to-all(f32[16,4,128]{2,1,0:T(4,128)S(1)} %bitcast.30), channel_id=1, replica_groups=mesh['z'=16,'core'=2,'bat'=16] {'z'}, dimensions={0} | all-to-all | bytes 65536 | tf_op jit(solution)/shard_map/all_to_all | solution.py:373
  64.5 2.6 %step.2 = (f32[1,128]{1,0:T(1,128)S(1)}, f32[48,128]{1,0:T(8,128)S(1)}, f32[16,384]{1,0:T(8,128)S(1)}, f32[16,384]{1,0:T(8,128)S(1)}, f32[16,384]{1,0:T(8,128)S(...) custom-call(f32[256,128]{1,0:T(8,128)S(1)} %bitcast.18, ...), custom_call_target="tpu_custom_call" | custom-call | flops 4718592 | bytes 4718592 | tf_op jit(solution)/shard_map/step/pallas_call | solution.py:423
  67.1 12.6 %all_to_all.38 = f32[32,8,128]{2,1,0:T(8,128)S(1)} all-to-all(f32[32,8,128]{2,1,0:T(8,128)S(1)} %bitcast.33), channel_id=1, replica_groups=mesh['z'=16,'core'=2,'bat'=16] {'core','bat'}, dimensions={0} | all-to-all | bytes 262144 | tf_op jit(solution)/shard_map/all_to_all | solution.py:373
  79.7 14.0 %all_to_all.39 = f32[16,4,128]{2,1,0:T(4,128)S(1)} all-to-all(f32[16,4,128]{2,1,0:T(4,128)S(1)} %bitcast.31), channel_id=1, replica_groups=mesh['z'=16,'core'=2,'bat'=16] {'z'}, dimensions={0} | all-to-all | bytes 65536 | tf_op jit(solution)/shard_map/all_to_all | solution.py:373
  93.7 2.6 %step.3 = (f32[1,128]{1,0:T(1,128)S(1)}, f32[48,128]{1,0:T(8,128)S(1)}, f32[16,384]{1,0:T(8,128)S(1)}, f32[16,384]{1,0:T(8,128)S(1)}, f32[16,384]{1,0:T(8,128)S(...) custom-call(f32[256,128]{1,0:T(8,128)S(1)} %bitcast.19, ...), custom_call_target="tpu_custom_call" | custom-call | flops 4718592 | bytes 4718592 | tf_op jit(solution)/shard_map/step/pallas_call | solution.py:423
  96.3 12.3 %all_to_all.40 = f32[32,8,128]{2,1,0:T(8,128)S(1)} all-to-all(f32[32,8,128]{2,1,0:T(8,128)S(1)} %bitcast.34), channel_id=1, replica_groups=mesh['z'=16,'core'=2,'bat'=16] {'core','bat'}, dimensions={0} | all-to-all | bytes 262144 | tf_op jit(solution)/shard_map/all_to_all | solution.py:373
  108.6 14.0 %all_to_all.41 = f32[16,4,128]{2,1,0:T(4,128)S(1)} all-to-all(f32[16,4,128]{2,1,0:T(4,128)S(1)} %bitcast.32), channel_id=1, replica_groups=mesh['z'=16,'core'=2,'bat'=16] {'z'}, dimensions={0} | all-to-all | bytes 65536 | tf_op jit(solution)/shard_map/all_to_all | solution.py:373
  122.6 2.3 %last.1 = (f32[16,384]{1,0:T(8,128)}, f32[16,384]{1,0:T(8,128)}, f32[16,384]{1,0:T(8,128)}, f32[24,128]{1,0:T(8,128)}) custom-call(f32[256,128]{1,0:T(8,128)S(1)} %bitcast.20, f32[2,128,128]{2,1,0:T(8,128)S(1)} %bitcast.26, f32[64,128]{1,0:T(8,128)S(1)} %bitcast.29, f32[1,128]{1,0:T(1,128)S(1)} %get-tuple-element.72.weight_in, ...), custom_call_target="tpu_custom_call" | custom-call | flops 4718592 | bytes 4718592 | tf_op jit(solution)/shard_map/last/pallas_call | solution.py:423
  (9 shorter events, 0.1 us)
Async XLA Ops:
  1.6 9.8 %copy-start.3 = (s32[25]{0:T(128)S(1)}, s32[25]{0:T(128)}, u32[]{:S(2)}) copy-start(s32[25]{0:T(128)} %param.23) | copy-start | bytes 304
  1.6 9.8 %copy-start.4 = (s32[72]{0:T(128)S(1)}, s32[72]{0:T(128)}, u32[]{:S(2)}) copy-start(s32[72]{0:T(128)} %param.22) | copy-start | bytes 868
  1.6 10.1 %copy-start.1 = (f32[3072]{0:T(1024)S(1)}, f32[3072]{0:T(1024)}, u32[]{:S(2)}) copy-start(f32[3072]{0:T(1024)} %param.20) | copy-start | bytes 36868
  1.7 10.1 %copy-start.2 = (f32[1,3072]{1,0:T(1,128)S(1)}, f32[1,3072]{1,0:T(1,128)}, u32[]{:S(2)}) copy-start(f32[1,3072]{1,0:T(1,128)} %param.15) | copy-start | bytes 36868
  1.7 10.2 %copy-start = (f32[72,128,128]{2,1,0:T(8,128)S(1)}, f32[72,128,128]{2,1,0:T(8,128)}, u32[]{:S(2)}) copy-start(f32[72,128,128]{2,1,0:T(8,128)} %values.9) | copy-start | bytes 14155780
  1.7 11.5 %collective-permute-start = (f32[2,384]{1,0:T(2,128)S(1)}, f32[2,384]{1,0:T(2,128)S(1)}, u32[]{:S(2)}, u32[]{:S(2)}) collective-permute-start(f32[2,384]{1,0:T(2,128)S(1)} %get-tuple-element.45), channel_id=1, source_target_pairs={{16,32},{32,16},{48,64},{64,48},{80,96},{96,80},{112,128},{128,112... | collective-permute-start | bytes 9224 | tf_op jit(solution)/shard_map/ppermute | solution.py:401
  6.9 6.3 %collective-permute-start.1 = (f32[3,384]{1,0:T(4,128)S(1)}, f32[3,384]{1,0:T(4,128)S(1)}, u32[]{:S(2)}, u32[]{:S(2)}) collective-permute-start(f32[3,384]{1,0:T(4,128)S(1)} %get-tuple-element.46), channel_id=1, source_target_pairs={{0,16},{16,0},{1,17},{17,1},{2,18},{18,2},{3,19},{19,3},{4,20},{20... | collective-permute-start | bytes 13832 | tf_op jit(solution)/shard_map/ppermute | solution.py:399
